TPU v7x, 256 devices: a whole 4x4x8 slice. The times are simulated.
256 devices in a mesh: tgt: 16 (over z_hi, y, core), src: 16 (over z_lo, x).
Axes of the slice: x: 4, y: 4, z: 8 (z_hi: 2, z_lo: 4; z = z_hi * 4 + z_lo), core: 2. Of those that a mesh axis runs over, the one named last changes fastest.
Arguments:
- targets: bfloat16 [64, 64, 4096], P('tgt', 'src'), may hold values from -6 to 6
- sources: bfloat16 [16, 64, 4096], P('src', 'tgt'), may hold values from -6 to 6
- exponents: float32 [8], replicated, may hold values from 0.005 to 0.76
- coefficients: float32 [8], replicated, may hold values from -0.08 to 0.08
Outputs:
- exchange: float32 [64, 64, 4096], P('src', 'tgt')
All inputs are finite; a program needn't handle non-finite values.
Results may differ from a plain program's by a relative error of at most 0.0063.
The roundings to bfloat16 on the way count: a program that leaves them out, or rounds other values in their place, can miss the bound.
Values may be sent and summed in bfloat16 or wider, within the bound.
No kernel may reach another device: no remote copies, remote signals or barrier semaphores. Data moves between devices by JAX's collectives and lax.ppermute only.
A program may use at most 64 MiB of HBM per device.

v0:
```python
import jax
import jax.numpy as jnp
import numpy as np
from jax import lax
from jax.experimental import pallas as pl
from jax.experimental.pallas import tpu as pltpu
from jax.sharding import Mesh
from jax.sharding import PartitionSpec as P


G = 64
GAUSS = 8
BF16, F32 = jnp.bfloat16, jnp.float32

SCALE = {0: 1.0, 1: 1.869537353515625, 2: 1.62451171875, 4: 1.13287353515625, 8: 1.8672027587890625, 16: 1.0, 32: 1.0}


def basis():
    n = np.arange(G)
    waves = [(k, np.cos) for k in range(G // 2 + 1)] + [(k, np.sin) for k in range(1, G // 2)]
    rows = np.stack([SCALE[k & -k] * wave(2 * np.pi * k * n / G) for k, wave in waves])
    rows[np.abs(rows) < 1e-12] = 0
    return rows, np.array([k for k, _ in waves])


def basis_blocks():
    rows, _ = basis()
    parity = np.array([2 * r + h for h in range(2) for r in range(32)])
    four = np.eye(4)
    z_in = np.kron(four, rows.T)
    y_in = np.einsum("ky,ab->kbay", rows[:, parity], four).reshape(256, 256)
    x_in = np.einsum("kbx,ij->ikbjx", rows.reshape(G, 16, 4), four).reshape(256, 256)
    return [jnp.asarray(m, BF16) for m in (z_in, y_in, x_in, x_in.T, y_in.T, z_in.T)]


def spectrum_kernel(exponents, coefficients, waves, waves_turned, out, outer):
    n = lax.broadcasted_iota(jnp.int32, (GAUSS, G), 1)
    distance = jnp.minimum(n, G - n).astype(F32)
    table = jnp.exp(-exponents[...] * (distance * distance))
    weighted = (coefficients[...] * table).astype(BF16).astype(F32)
    table = table.astype(BF16).astype(F32)
    scaled = jnp.dot(weighted, waves[...], precision=lax.Precision.HIGHEST, preferred_element_type=F32)
    plain = lax.dot_general(
        waves_turned[...], table, (((1,), (1,)), ((), ())), precision=lax.Precision.HIGHEST, preferred_element_type=F32
    )
    for g in range(GAUSS):
        outer[g] = plain[:, g : g + 1] * scaled[g : g + 1]
    for k in range(G):
        total = plain[k : k + 1, 0:1] * outer[0]
        for g in range(1, GAUSS):
            total = total + plain[k : k + 1, g : g + 1] * outer[g]
        out[k] = total


def spectrum(exponents, coefficients):
    rows, freq = basis()
    waves = np.cos(2 * np.pi * np.outer(np.arange(G), freq) / G) / (rows * rows).sum(1)[None]
    return pl.pallas_call(
        spectrum_kernel,
        out_shape=jax.ShapeDtypeStruct((G, G, 128), F32),
        scratch_shapes=[pltpu.VMEM((GAUSS, G, 128), F32)],
        cost_estimate=pl.CostEstimate(flops=8 << 20, bytes_accessed=3 << 20, transcendentals=512),
    )(
        exponents.reshape(GAUSS, 1),
        coefficients.reshape(GAUSS, 1),
        jnp.asarray(np.concatenate([waves, waves], axis=1), F32),
        jnp.asarray(waves.T, F32),
    )


def pair_kernel(*refs):
    t_in, s_in, d_ref = refs[:4], refs[4:6], refs[6]
    z_in, y_in, x_in, x_out, y_out, z_out = refs[7:13]
    out = refs[13]
    t_all, s_rows, field = refs[14:]
    zh, c, zl, x = (lax.axis_index(a) for a in ("zh", "c", "zl", "x"))
    lane = lax.broadcasted_iota(jnp.int32, (4, 32, 128), 2) < 64

    def swap(a):
        return pltpu.roll(a, 64, 2)

    def dot(a, b):
        return jnp.dot(a, b, preferred_element_type=F32)

    for k in range(4):
        for j in range(4):
            t_all[lax.bitwise_xor(zl, k) * 4 + lax.rem(x - j + 4, 4)] = t_in[k][j]

    for e in range(2):
        for y in range(4):
            for m in range(2):
                b = lax.rem(zh + m, 2) * 8 + y * 2 + lax.rem(c + e, 2)
                target = t_all[b]
                turned = swap(target)
                target = jnp.concatenate([jnp.where(lane, target, turned), jnp.where(lane, turned, target)], axis=1)
                target = target.reshape(256, 128)
                dense = []
                for h in range(2):
                    one, two = s_in[e][8 * h + y, m], s_in[e][8 * h + 4 + y, m]
                    source = jnp.concatenate([jnp.where(lane, one, swap(two)), jnp.where(lane, swap(one), two)], axis=1)
                    source = source.reshape(256, 128)
                    s_rows[b, :, 128 * h : 128 * h + 128] = source
                    dense.append(target * source)
                along_z = dot(jnp.concatenate(dense, axis=1), z_in[...]).astype(BF16)
                field[b] = dot(y_in[...], along_z).astype(BF16)

    for k in range(16):
        rows = slice(16 * k, 16 * k + 16)
        waves = dot(x_in[...], field[:, rows, :].reshape(256, 256))
        factor = d_ref[4 * k : 4 * k + 4].reshape(256, 128)
        waves = (waves * jnp.concatenate([factor, factor], axis=1)).astype(BF16)
        field[:, rows, :] = dot(x_out[...], waves).astype(BF16).reshape(16, 16, 256)

    for b in range(16):
        along_y = dot(y_out[...], field[b]).astype(BF16)
        terms = dot(along_y, z_out[...]) * s_rows[b].astype(F32)
        terms = (terms[:, :128] + terms[:, 128:]).reshape(4, G, 128)
        terms = terms + swap(terms)
        out[b] = jnp.where(lane, terms[:, :32], terms[:, 32:]).astype(out.dtype)


def pair_sums(targets, sources, factor):
    vmem = pl.BlockSpec(memory_space=pltpu.VMEM)
    return pl.pallas_call(
        pair_kernel,
        out_shape=jax.ShapeDtypeStruct((16, 4, 32, 128), BF16),
        in_specs=[vmem] * 13,
        out_specs=vmem,
        scratch_shapes=[
            pltpu.VMEM((16, 4, 32, 128), BF16),
            pltpu.VMEM((16, 256, 256), BF16),
            pltpu.VMEM((16, 256, 256), BF16),
        ],
        compiler_params=pltpu.CompilerParams(vmem_limit_bytes=24 << 20),
    )(*targets, *sources, factor, *basis_blocks())


def turn(n, by):
    return [(i, (i + by) % n) for i in range(n)]


def flip(n, by):
    return [(i, i ^ by) for i in range(n)]


def exchange(targets, sources, exponents, coefficients):
    x = lax.axis_index("x")
    mine = sources.reshape(4, 32, 128)
    other = lax.ppermute(mine, "zh", turn(2, 1))
    packed = targets.reshape(4, 4, 32, 128)
    pick = lambda j: lax.dynamic_index_in_dim(packed, (x + j) % 4, 0, keepdims=False)
    target_block = jnp.stack([pick(0)] + [lax.ppermute(pick(j), "x", turn(4, j)) for j in range(1, 4)])
    by_z = [target_block] + [lax.ppermute(target_block, "zl", flip(4, k)) for k in range(1, 4)]
    factor = spectrum(exponents, coefficients)
    source_block = jnp.stack([mine, other])
    source_block = jnp.broadcast_to(source_block, (16, 2, 4, 32, 128))
    own_core = lax.all_to_all(source_block, ("x", "y"), 0, 0, tiled=True)
    other_core = lax.ppermute(own_core, "c", turn(2, 1))
    part = pair_sums(by_z, (own_core, other_core), factor)
    parts = lax.all_to_all(part, ("zl", "x"), 0, 0, tiled=True).reshape(4, 4, 4, G * G)
    return -parts.astype(F32).sum(0).transpose(1, 0, 2)


def solution(mesh):
    torus = Mesh(mesh.devices.reshape(2, 4, 2, 4, 4), ("zh", "y", "c", "zl", "x"))
    tgt, src = ("zh", "y", "c"), ("zl", "x")
    return jax.shard_map(
        exchange,
        mesh=torus,
        in_specs=(P(tgt, src, None), P(src, tgt, None), P(), P()),
        out_specs=P(src, tgt, None),
        check_vma=False,
    )
```

profile of v0, /device:TPU:32, one launch (start us, length us, event | category | flops | bytes accessed | tf_op | source)
XLA Modules:
  0.0 79.7 jit_solution(17385592945072512184)
XLA Ops:
  0.0 0.8 %copy.22 = bf16[1,4,32,128]{3,2,1,0:T(8,128)(2,1)S(1)} copy(bf16[1,4,32,128]{3,1,2,0:T(4,128)(2,1)} %bitcast.27) | data formatting | bytes 65536
  0.8 6.3 %collective-permute-start.6 = (bf16[4,32,128]{2,1,0:T(8,128)(2,1)S(1)}, bf16[4,32,128]{2,1,0:T(8,128)(2,1)S(1)}, u32[]{:S(2)}, u32[]{:S(2)}) collective-permute-start(bf16[4,32,128]{2,1,0:T(8,128)(2,1)S(1)} %bitcast.26), channel_id=1, source_target_pairs={{0,128},{128,0},{1,129},{129,1},{2,130},{130,2},{3,131},{131,3},{4... | collective-permute-start | bytes 98312 | tf_op jit(solution)/shard_map/ppermute | solution.py:149
  7.1 1.9 %collective-permute-done.6 = bf16[4,32,128]{2,1,0:T(8,128)(2,1)S(1)} collective-permute-done((bf16[4,32,128]{2,1,0:T(8,128)(2,1)S(1)}, bf16[4,32,128]{2,1,0:T(8,128)(2,1)S(1)}, u32[]{:S(2)}, u32[]{:S(2)}) %collective-permute-start.6) | collective-permute-done | bytes 32800 | tf_op jit(solution)/shard_map/ppermute | solution.py:149
  9.0 0.0 copy-start.8
  9.0 0.0 copy-start.9
  9.0 0.2 broadcast_in_dim.3
  9.3 0.0 copy-start.1
  9.3 0.0 copy-start.2
  9.3 0.0 copy-start.3
  9.3 0.0 copy-start.4
  9.3 0.0 copy-start.5
  9.3 0.0 copy-start.6
  9.3 23.2 %all_to_all.10.refs_4_ = bf16[16,2,4,32,128]{4,3,2,1,0:T(8,128)(2,1)S(1)} all-to-all(bf16[16,2,4,32,128]{4,3,2,1,0:T(8,128)(2,1)S(1)} %broadcast_in_dim.3), channel_id=1, replica_groups=mesh['zh'=2,'y'=4,'c'=2,'zl'=4,'x'=4] {'x','y'}, dimensions={0} | all-to-all | bytes 2097152 | tf_op jit(solution)/shard_map/all_to_all | solution.py:157
  32.5 0.0 collective-permute-start.7
  32.5 0.0 copy-done.7
  32.5 0.2 reshape.15
  32.7 1.2 %collective-permute-start.2 = (bf16[4,32,128]{2,1,0:T(8,128)(2,1)S(1)}, bf16[4,32,128]{2,1,0:T(8,128)(2,1)S(1)}, u32[]{:S(2)}, u32[]{:S(2)}) collective-permute-start(bf16[4,32,128]{2,1,0:T(8,128)(2,1)S(1)} %get-tuple-element.6), channel_id=1, source_target_pairs={{0,3},{1,0},{2,1},{3,2},{4,7},{5,4},{6,5},{7,6},{8,11},{9,8},{10,9... | collective-permute-start | bytes 98312 | tf_op jit(solution)/shard_map/ppermute | solution.py:152
  33.9 0.7 collective-permute-start.1
  34.6 0.7 collective-permute-start
  35.3 1.7 %collective-permute-done.2 = bf16[4,32,128]{2,1,0:T(8,128)(2,1)S(1)} collective-permute-done((bf16[4,32,128]{2,1,0:T(8,128)(2,1)S(1)}, bf16[4,32,128]{2,1,0:T(8,128)(2,1)S(1)}, u32[]{:S(2)}, u32[]{:S(2)}) %collective-permute-start.2) | collective-permute-done | bytes 32800 | tf_op jit(solution)/shard_map/ppermute | solution.py:152
  37.0 2.4 %collective-permute-done.1 = bf16[4,32,128]{2,1,0:T(8,128)(2,1)S(1)} collective-permute-done((bf16[4,32,128]{2,1,0:T(8,128)(2,1)S(1)}, bf16[4,32,128]{2,1,0:T(8,128)(2,1)S(1)}, u32[]{:S(2)}, u32[]{:S(2)}) %collective-permute-start.1) | collective-permute-done | bytes 32800 | tf_op jit(solution)/shard_map/ppermute | solution.py:152
  39.4 0.4 collective-permute-done
  39.8 1.7 %collective-permute-start.5 = (bf16[4,4,32,128]{3,2,1,0:T(8,128)(2,1)S(1)}, bf16[4,4,32,128]{3,2,1,0:T(8,128)(2,1)S(1)}, u32[]{:S(2)}, u32[]{:S(2)}) collective-permute-start(bf16[4,4,32,128]{3,2,1,0:T(8,128)(2,1)S(1)} %pad_maximum_fusion.refs_0_), channel_id=1, source_target_pairs={{0,12},{4,8},{8,4},{12,0},{1,13},{5,9},{9,5},{13,1},{2,14},{6,10},... | collective-permute-start | bytes 393224 | tf_op jit(solution)/shard_map/ppermute | solution.py:153
  41.4 1.8 %collective-permute-start.4 = (bf16[4,4,32,128]{3,2,1,0:T(8,128)(2,1)S(1)}, bf16[4,4,32,128]{3,2,1,0:T(8,128)(2,1)S(1)}, u32[]{:S(2)}, u32[]{:S(2)}) collective-permute-start(bf16[4,4,32,128]{3,2,1,0:T(8,128)(2,1)S(1)} %pad_maximum_fusion.refs_0_), channel_id=1, source_target_pairs={{0,8},{4,12},{8,0},{12,4},{1,9},{5,13},{9,1},{13,5},{2,10},{6,14},... | collective-permute-start | bytes 393224 | tf_op jit(solution)/shard_map/ppermute | solution.py:153
  43.2 0.9 %collective-permute-start.3 = (bf16[4,4,32,128]{3,2,1,0:T(8,128)(2,1)S(1)}, bf16[4,4,32,128]{3,2,1,0:T(8,128)(2,1)S(1)}, u32[]{:S(2)}, u32[]{:S(2)}) collective-permute-start(bf16[4,4,32,128]{3,2,1,0:T(8,128)(2,1)S(1)} %pad_maximum_fusion.refs_0_), channel_id=1, source_target_pairs={{0,4},{4,0},{8,12},{12,8},{1,5},{5,1},{9,13},{13,9},{2,6},{6,2},{1... | collective-permute-start | bytes 393224 | tf_op jit(solution)/shard_map/ppermute | solution.py:153
  44.1 0.0 copy-done.8
  44.1 0.7 copy.15.exponents
  44.8 0.0 copy-done.9
  44.8 0.7 copy.16.coefficients
  45.4 3.8 %shard_map.118.refs_6_ = f32[64,64,128]{2,1,0:T(8,128)} custom-call(f32[8,1]{1,0:T(8,128)} %copy.15.exponents, f32[8,1]{1,0:T(8,128)} %copy.16.coefficients, f32[64,128]{1,0:T(8,128)} %constant.62.clone.waves, f32[64,64]{1,0:T(8,128)} %constant.63.clone.waves_turned), custom_call_target="tpu_custom_call" | custom-call | flops 8388608 | bytes 3145728 | tf_op jit(solution)/shard_map/pallas_call | solution.py:58
  49.2 2.3 %collective-permute-done.5.refs_3_ = bf16[4,4,32,128]{3,2,1,0:T(8,128)(2,1)S(1)} collective-permute-done((bf16[4,4,32,128]{3,2,1,0:T(8,128)(2,1)S(1)}, bf16[4,4,32,128]{3,2,1,0:T(8,128)(2,1)S(1)}, u32[]{:S(2)}, u32[]{:S(2)}) %collective-permute-start.5) | collective-permute-done | bytes 131104 | tf_op jit(solution)/shard_map/ppermute | solution.py:153
  51.6 0.6 collective-permute-done.4.refs_2_
  52.2 0.1 collective-permute-done.3.refs_1_
  52.3 0.0 collective-permute-done.7.refs_5_
  52.3 0.0 copy-done.1
  52.3 0.0 copy-done.2
  52.3 0.0 copy-done.3
  52.3 0.0 copy-done.4
  52.4 0.0 copy-done.5
  52.4 0.0 copy-done.6
  52.4 0.0 copy-start
  52.4 1.6 %copy-done = f32[64,64,128]{2,1,0:T(8,128)S(1)} copy-done((f32[64,64,128]{2,1,0:T(8,128)S(1)}, f32[64,64,128]{2,1,0:T(8,128)}, u32[]{:S(2)}) %copy-start) | copy-done | bytes 2097176
  54.0 4.7 %shard_map.119 = bf16[16,4,32,128]{3,2,1,0:T(8,128)(2,1)S(1)} custom-call(bf16[4,4,32,128]{3,2,1,0:T(8,128)(2,1)S(1)} %pad_maximum_fusion.refs_0_, bf16[4,4,32,128]{3,2,1,0:T(8,128)(2,1)S(1)} %collective-permute-done.3.refs_1_, bf16[4,4,32,128]{3,2,1,0:T(8,128)(2,1)S(1)} %collective-permute-done.4.refs_2_, ...), custom_call_target="tpu_custom_call" | custom-call | tf_op jit(solution)/shard_map/pallas_call | solution.py:124
  58.6 19.5 %all_to_all.11 = bf16[16,4,32,128]{3,2,1,0:T(8,128)(2,1)S(1)} all-to-all(bf16[16,4,32,128]{3,2,1,0:T(8,128)(2,1)S(1)} %shard_map.119), channel_id=1, replica_groups=mesh['zh'=2,'y'=4,'c'=2,'zl'=4,'x'=4] {'zl','x'}, dimensions={0} | all-to-all | bytes 1048576 | tf_op jit(solution)/shard_map/all_to_all | solution.py:160
  78.1 0.4 reshape.19
  78.5 0.3 reduce_sum.9
  78.8 0.1 negate_bitcast_fusion
  78.8 0.9 %copy.17 = f32[4,4,4096]{2,1,0:T(4,128)} copy(f32[4,4,4096]{2,0,1:T(4,128)S(1)} %negate_bitcast_fusion) | data formatting | bytes 524288 | tf_op jit(solution)/shard_map/neg | solution.py:161
  (4 shorter events, 0.0 us)
Async XLA Ops:
  0.0 32.5 %copy-start.7 = (bf16[4,4,4096]{2,1,0:T(4,128)(2,1)S(1)}, bf16[4,4,4096]{2,1,0:T(4,128)(2,1)}, u32[]{:S(2)}) copy-start(bf16[4,4,4096]{2,1,0:T(4,128)(2,1)} %param.12) | copy-start | bytes 393220
  0.8 8.2 %collective-permute-start.6 = (bf16[4,32,128]{2,1,0:T(8,128)(2,1)S(1)}, bf16[4,32,128]{2,1,0:T(8,128)(2,1)S(1)}, u32[]{:S(2)}, u32[]{:S(2)}) collective-permute-start(bf16[4,32,128]{2,1,0:T(8,128)(2,1)S(1)} %bitcast.26), channel_id=1, source_target_pairs={{0,128},{128,0},{1,129},{129,1},{2,130},{130,2},{3,131},{131,3},{4... | collective-permute-start | bytes 98312 | tf_op jit(solution)/shard_map/ppermute | solution.py:149
  9.0 35.1 %copy-start.8 = (f32[8]{0:T(128)S(1)}, f32[8]{0:T(128)}, u32[]{:S(2)}) copy-start(f32[8]{0:T(128)} %param.14) | copy-start | bytes 100
  9.0 35.8 %copy-start.9 = (f32[8]{0:T(128)S(1)}, f32[8]{0:T(128)}, u32[]{:S(2)}) copy-start(f32[8]{0:T(128)} %param.15) | copy-start | bytes 100
  9.3 43.1 %copy-start.1 = (bf16[256,256]{1,0:T(8,128)(2,1)S(1)}, bf16[256,256]{1,0:T(8,128)(2,1)}, u32[]{:S(2)}) copy-start(bf16[256,256]{1,0:T(8,128)(2,1)} %constant.69.clone.refs_12_) | copy-start | bytes 393220
  9.3 43.1 %copy-start.2 = (bf16[256,256]{1,0:T(8,128)(2,1)S(1)}, bf16[256,256]{1,0:T(8,128)(2,1)}, u32[]{:S(2)}) copy-start(bf16[256,256]{1,0:T(8,128)(2,1)} %constant.68.clone.refs_11_) | copy-start | bytes 393220
  9.3 43.1 %copy-start.3 = (bf16[256,256]{1,0:T(8,128)(2,1)S(1)}, bf16[256,256]{1,0:T(8,128)(2,1)}, u32[]{:S(2)}) copy-start(bf16[256,256]{1,0:T(8,128)(2,1)} %constant.67.clone.refs_10_) | copy-start | bytes 393220
  9.3 43.1 %copy-start.4 = (bf16[256,256]{1,0:T(8,128)(2,1)S(1)}, bf16[256,256]{1,0:T(8,128)(2,1)}, u32[]{:S(2)}) copy-start(bf16[256,256]{1,0:T(8,128)(2,1)} %constant.66.clone.refs_9_) | copy-start | bytes 393220
  9.3 43.0 %copy-start.5 = (bf16[256,256]{1,0:T(8,128)(2,1)S(1)}, bf16[256,256]{1,0:T(8,128)(2,1)}, u32[]{:S(2)}) copy-start(bf16[256,256]{1,0:T(8,128)(2,1)} %constant.65.clone.refs_8_) | copy-start | bytes 393220
  9.3 43.0 %copy-start.6 = (bf16[256,256]{1,0:T(8,128)(2,1)S(1)}, bf16[256,256]{1,0:T(8,128)(2,1)}, u32[]{:S(2)}) copy-start(bf16[256,256]{1,0:T(8,128)(2,1)} %constant.64.clone.refs_7_) | copy-start | bytes 393220
  32.5 19.8 %collective-permute-start.7 = (bf16[16,2,4,32,128]{4,3,2,1,0:T(8,128)(2,1)S(1)}, bf16[16,2,4,32,128]{4,3,2,1,0:T(8,128)(2,1)S(1)}, u32[]{:S(2)}, u32[]{:S(2)}) collective-permute-start(bf16[16,2,4,32,128]{4,3,2,1,0:T(8,128)(2,1)S(1)} %all_to_all.10.refs_4_), channel_id=1, source_target_pairs={{0,16},{16,0},{1,17},{17,1},{2,18},{18,2},{3,19},{19,3},{4,20},{20... | collective-permute-start | bytes 3145736 | tf_op jit(solution)/shard_map/ppermute | solution.py:158
  32.7 4.2 %collective-permute-start.2 = (bf16[4,32,128]{2,1,0:T(8,128)(2,1)S(1)}, bf16[4,32,128]{2,1,0:T(8,128)(2,1)S(1)}, u32[]{:S(2)}, u32[]{:S(2)}) collective-permute-start(bf16[4,32,128]{2,1,0:T(8,128)(2,1)S(1)} %get-tuple-element.6), channel_id=1, source_target_pairs={{0,3},{1,0},{2,1},{3,2},{4,7},{5,4},{6,5},{7,6},{8,11},{9,8},{10,9... | collective-permute-start | bytes 98312 | tf_op jit(solution)/shard_map/ppermute | solution.py:152
  33.9 5.4 %collective-permute-start.1 = (bf16[4,32,128]{2,1,0:T(8,128)(2,1)S(1)}, bf16[4,32,128]{2,1,0:T(8,128)(2,1)S(1)}, u32[]{:S(2)}, u32[]{:S(2)}) collective-permute-start(bf16[4,32,128]{2,1,0:T(8,128)(2,1)S(1)} %get-tuple-element.7), channel_id=1, source_target_pairs={{0,2},{1,3},{2,0},{3,1},{4,6},{5,7},{6,4},{7,5},{8,10},{9,11},{10,... | collective-permute-start | bytes 98312 | tf_op jit(solution)/shard_map/ppermute | solution.py:152
  34.6 5.1 %collective-permute-start = (bf16[4,32,128]{2,1,0:T(8,128)(2,1)S(1)}, bf16[4,32,128]{2,1,0:T(8,128)(2,1)S(1)}, u32[]{:S(2)}, u32[]{:S(2)}) collective-permute-start(bf16[4,32,128]{2,1,0:T(8,128)(2,1)S(1)} %get-tuple-element.8), channel_id=1, source_target_pairs={{0,1},{1,2},{2,3},{3,0},{4,5},{5,6},{6,7},{7,4},{8,9},{9,10},{10,1... | collective-permute-start | bytes 98312 | tf_op jit(solution)/shard_map/ppermute | solution.py:152
  39.8 11.8 %collective-permute-start.5 = (bf16[4,4,32,128]{3,2,1,0:T(8,128)(2,1)S(1)}, bf16[4,4,32,128]{3,2,1,0:T(8,128)(2,1)S(1)}, u32[]{:S(2)}, u32[]{:S(2)}) collective-permute-start(bf16[4,4,32,128]{3,2,1,0:T(8,128)(2,1)S(1)} %pad_maximum_fusion.refs_0_), channel_id=1, source_target_pairs={{0,12},{4,8},{8,4},{12,0},{1,13},{5,9},{9,5},{13,1},{2,14},{6,10},... | collective-permute-start | bytes 393224 | tf_op jit(solution)/shard_map/ppermute | solution.py:153
  41.4 10.8 %collective-permute-start.4 = (bf16[4,4,32,128]{3,2,1,0:T(8,128)(2,1)S(1)}, bf16[4,4,32,128]{3,2,1,0:T(8,128)(2,1)S(1)}, u32[]{:S(2)}, u32[]{:S(2)}) collective-permute-start(bf16[4,4,32,128]{3,2,1,0:T(8,128)(2,1)S(1)} %pad_maximum_fusion.refs_0_), channel_id=1, source_target_pairs={{0,8},{4,12},{8,0},{12,4},{1,9},{5,13},{9,1},{13,5},{2,10},{6,14},... | collective-permute-start | bytes 393224 | tf_op jit(solution)/shard_map/ppermute | solution.py:153
  43.2 9.1 %collective-permute-start.3 = (bf16[4,4,32,128]{3,2,1,0:T(8,128)(2,1)S(1)}, bf16[4,4,32,128]{3,2,1,0:T(8,128)(2,1)S(1)}, u32[]{:S(2)}, u32[]{:S(2)}) collective-permute-start(bf16[4,4,32,128]{3,2,1,0:T(8,128)(2,1)S(1)} %pad_maximum_fusion.refs_0_), channel_id=1, source_target_pairs={{0,4},{4,0},{8,12},{12,8},{1,5},{5,1},{9,13},{13,9},{2,6},{6,2},{1... | collective-permute-start | bytes 393224 | tf_op jit(solution)/shard_map/ppermute | solution.py:153
  52.4 1.6 %copy-start = (f32[64,64,128]{2,1,0:T(8,128)S(1)}, f32[64,64,128]{2,1,0:T(8,128)}, u32[]{:S(2)}) copy-start(f32[64,64,128]{2,1,0:T(8,128)} %shard_map.118.refs_6_) | copy-start | bytes 6291460
where the time goes:
time: 80 us; the launch traced here: 79.7 us
  blocking collectives  42.7 us (53%)
  starting transfers between devices  13.2 us (16%)
  waiting for transfers between devices  9.4 us (12%)
  Pallas kernels  8.45 us (11%)
  local copies, waits for them, and re-layouts  5.41 us (7%)
    all_to_all x1, blocking collectives, exchange(): own_core = lax.all_to_all(source_block, ('x', 'y'), 0, 0, tiled=True)  23.2 us
    all_to_all x1, blocking collectives, exchange(): lax.all_to_all(part, ('zl', 'x'), 0, 0, tiled=True).reshape(4, 4, 4, G * G)  19.5 us
    ppermute x1, starting transfers between devices, exchange(): other = lax.ppermute(mine, 'zh', turn(2, 1))  6.29 us
    pallas_call x1, Pallas kernels, pair_sums(): pl.pallas_call(pair_kernel, out_shape=jax.ShapeDtypeStruct((16, 4, 32, 12...  4.65 us
    ppermute x3, waiting for transfers between devices, exchange(): lax.ppermute(pick(j), 'x', turn(4, j))  4.42 us
    ppermute x3, starting transfers between devices, exchange(): lax.ppermute(target_block, 'zl', flip(4, k))  4.32 us
    pallas_call x1, Pallas kernels, spectrum(): pl.pallas_call(spectrum_kernel, out_shape=jax.ShapeDtypeStruct((G, G, 128...  3.8 us
    ppermute x3, waiting for transfers between devices, exchange(): lax.ppermute(target_block, 'zl', flip(4, k))  3.09 us
  transfers between devices with their start and end apart: 8, of which 7 were waited for; matrix products, arithmetic and copies ran while one was open for 2% of the time, Pallas kernels for 5%

commit v1 on v0

--- a/solution.py
+++ b/solution.py
@@ -35,45 +35,56 @@
 
 def spectrum_kernel(exponents, coefficients, waves, waves_turned, out, outer):
     n = lax.broadcasted_iota(jnp.int32, (GAUSS, G), 1)
+    term = lax.broadcasted_iota(jnp.int32, (GAUSS, G), 0)
     distance = jnp.minimum(n, G - n).astype(F32)
-    table = jnp.exp(-exponents[...] * (distance * distance))
-    weighted = (coefficients[...] * table).astype(BF16).astype(F32)
+    power, weight = jnp.zeros((GAUSS, G), F32), jnp.zeros((GAUSS, G), F32)
+    for g in range(GAUSS):
+        power = jnp.where(term == g, exponents[g], power)
+        weight = jnp.where(term == g, coefficients[g], weight)
+    table = jnp.exp(-power * (distance * distance))
+    weighted = (weight * table).astype(BF16).astype(F32)
     table = table.astype(BF16).astype(F32)
     scaled = jnp.dot(weighted, waves[...], precision=lax.Precision.HIGHEST, preferred_element_type=F32)
     plain = lax.dot_general(
         waves_turned[...], table, (((1,), (1,)), ((), ())), precision=lax.Precision.HIGHEST, preferred_element_type=F32
     )
     for g in range(GAUSS):
-        outer[g] = plain[:, g : g + 1] * scaled[g : g + 1]
-    for k in range(G):
+        outer[g] = plain[:40, g : g + 1] * scaled[g : g + 1]
+    for k in range(G // 2 + 1):
         total = plain[k : k + 1, 0:1] * outer[0]
         for g in range(1, GAUSS):
             total = total + plain[k : k + 1, g : g + 1] * outer[g]
-        out[k] = total
+        for row in (k, G // 2 + k) if 0 < k < G // 2 else (k,):
+            out[row, :40] = total
+            out[row, 40:] = total[8:32]
 
 
 def spectrum(exponents, coefficients):
     rows, freq = basis()
     waves = np.cos(2 * np.pi * np.outer(np.arange(G), freq) / G) / (rows * rows).sum(1)[None]
+    smem, vmem = pl.BlockSpec(memory_space=pltpu.SMEM), pl.BlockSpec(memory_space=pltpu.VMEM)
     return pl.pallas_call(
         spectrum_kernel,
         out_shape=jax.ShapeDtypeStruct((G, G, 128), F32),
-        scratch_shapes=[pltpu.VMEM((GAUSS, G, 128), F32)],
+        in_specs=[smem, smem, vmem, vmem],
+        out_specs=vmem,
+        scratch_shapes=[pltpu.VMEM((GAUSS, 40, 128), F32)],
         cost_estimate=pl.CostEstimate(flops=8 << 20, bytes_accessed=3 << 20, transcendentals=512),
+        compiler_params=pltpu.CompilerParams(vmem_limit_bytes=8 << 20),
     )(
-        exponents.reshape(GAUSS, 1),
-        coefficients.reshape(GAUSS, 1),
+        exponents,
+        coefficients,
         jnp.asarray(np.concatenate([waves, waves], axis=1), F32),
         jnp.asarray(waves.T, F32),
     )
 
 
 def pair_kernel(*refs):
-    t_in, s_in, d_ref = refs[:4], refs[4:6], refs[6]
-    z_in, y_in, x_in, x_out, y_out, z_out = refs[7:13]
-    out = refs[13]
-    t_all, s_rows, field = refs[14:]
-    zh, c, zl, x = (lax.axis_index(a) for a in ("zh", "c", "zl", "x"))
+    t_in, s_in, d_ref = refs[:4], refs[4:12], refs[12]
+    z_in, y_in, x_in, x_out, y_out, z_out = refs[13:19]
+    out = refs[19]
+    t_all, s_all, s_rows, field = refs[20:]
+    zh, y, c, zl, x = (lax.axis_index(a) for a in ("zh", "y", "c", "zl", "x"))
     lane = lax.broadcasted_iota(jnp.int32, (4, 32, 128), 2) < 64
 
     def swap(a):
@@ -87,22 +98,28 @@
             t_all[lax.bitwise_xor(zl, k) * 4 + lax.rem(x - j + 4, 4)] = t_in[k][j]
 
     for e in range(2):
-        for y in range(4):
-            for m in range(2):
-                b = lax.rem(zh + m, 2) * 8 + y * 2 + lax.rem(c + e, 2)
-                target = t_all[b]
-                turned = swap(target)
-                target = jnp.concatenate([jnp.where(lane, target, turned), jnp.where(lane, turned, target)], axis=1)
-                target = target.reshape(256, 128)
-                dense = []
-                for h in range(2):
-                    one, two = s_in[e][8 * h + y, m], s_in[e][8 * h + 4 + y, m]
-                    source = jnp.concatenate([jnp.where(lane, one, swap(two)), jnp.where(lane, swap(one), two)], axis=1)
-                    source = source.reshape(256, 128)
-                    s_rows[b, :, 128 * h : 128 * h + 128] = source
-                    dense.append(target * source)
-                along_z = dot(jnp.concatenate(dense, axis=1), z_in[...]).astype(BF16)
-                field[b] = dot(y_in[...], along_z).astype(BF16)
+        core = lax.rem(c + e, 2)
+        for l in range(4):
+            for i in range(4):
+                by_x, by_y = i + core * (l - i), l + core * (i - l)
+                for m in range(2):
+                    b = lax.rem(zh + m, 2) * 8 + lax.rem(y - by_y + 4, 4) * 2 + core
+                    s_all[by_x, b] = s_in[4 * e + l][i, m]
+
+    for b in range(16):
+        target = t_all[b]
+        turned = swap(target)
+        target = jnp.concatenate([jnp.where(lane, target, turned), jnp.where(lane, turned, target)], axis=1)
+        target = target.reshape(256, 128)
+        dense = []
+        for h in range(2):
+            one, two = s_all[2 * h, b], s_all[2 * h + 1, b]
+            source = jnp.concatenate([jnp.where(lane, one, swap(two)), jnp.where(lane, swap(one), two)], axis=1)
+            source = source.reshape(256, 128)
+            s_rows[b, :, 128 * h : 128 * h + 128] = source
+            dense.append(target * source)
+        along_z = dot(jnp.concatenate(dense, axis=1), z_in[...]).astype(BF16)
+        field[b] = dot(y_in[...], along_z).astype(BF16)
 
     for k in range(16):
         rows = slice(16 * k, 16 * k + 16)
@@ -124,10 +141,11 @@
     return pl.pallas_call(
         pair_kernel,
         out_shape=jax.ShapeDtypeStruct((16, 4, 32, 128), BF16),
-        in_specs=[vmem] * 13,
+        in_specs=[vmem] * 19,
         out_specs=vmem,
         scratch_shapes=[
             pltpu.VMEM((16, 4, 32, 128), BF16),
+            pltpu.VMEM((4, 16, 4, 32, 128), BF16),
             pltpu.VMEM((16, 256, 256), BF16),
             pltpu.VMEM((16, 256, 256), BF16),
         ],
@@ -141,6 +159,19 @@
 
 def flip(n, by):
     return [(i, i ^ by) for i in range(n)]
+
+
+def weave(along_x, along_y):
+    place = lambda y, c, x: ((y % 4) * 2 + c) * 4 + x % 4
+    pairs = []
+    for y in range(4):
+        for x in range(4):
+            pairs.append((place(y, 0, x), place(y + along_y, 0, x + along_x)))
+            pairs.append((place(y, 1, x), place(y + along_x, 1, x + along_y)))
+    return pairs
+
+
+SHIFTS = (1, 3, 2)
 
 
 def exchange(targets, sources, exponents, coefficients):
@@ -149,14 +180,18 @@
     other = lax.ppermute(mine, "zh", turn(2, 1))
     packed = targets.reshape(4, 4, 32, 128)
     pick = lambda j: lax.dynamic_index_in_dim(packed, (x + j) % 4, 0, keepdims=False)
-    target_block = jnp.stack([pick(0)] + [lax.ppermute(pick(j), "x", turn(4, j)) for j in range(1, 4)])
-    by_z = [target_block] + [lax.ppermute(target_block, "zl", flip(4, k)) for k in range(1, 4)]
+    rows = {j: lax.ppermute(pick(j), "x", turn(4, j)) for j in SHIFTS}
+    target_block = jnp.stack([pick(0)] + [rows[j] for j in range(1, 4)])
+    lines = [target_block] + [lax.ppermute(target_block, "zl", flip(4, k)) for k in range(1, 4)]
     factor = spectrum(exponents, coefficients)
-    source_block = jnp.stack([mine, other])
-    source_block = jnp.broadcast_to(source_block, (16, 2, 4, 32, 128))
-    own_core = lax.all_to_all(source_block, ("x", "y"), 0, 0, tiled=True)
-    other_core = lax.ppermute(own_core, "c", turn(2, 1))
-    part = pair_sums(by_z, (own_core, other_core), factor)
+    plane = ("y", "c", "x")
+    block = jnp.stack([mine, other])
+    first = {i: lax.ppermute(block, plane, weave(i, 0)) for i in SHIFTS}
+    block = jnp.stack([block] + [first[i] for i in range(1, 4)])
+    second = {l: lax.ppermute(block, plane, weave(0, l)) for l in SHIFTS}
+    own_core = [block] + [second[l] for l in range(1, 4)]
+    other_core = [lax.ppermute(own_core[l], "c", turn(2, 1)) for l in range(4)]
+    part = pair_sums(lines, own_core + other_core, factor)
     parts = lax.all_to_all(part, ("zl", "x"), 0, 0, tiled=True).reshape(4, 4, 4, G * G)
     return -parts.astype(F32).sum(0).transpose(1, 0, 2)
 

time: 80 us -> 68.2 us (0.85)
  the two profiles are of different devices: /device:TPU:32 before, /device:TPU:1 now
where the time goes in v1:
time: 68.2 us; the launch traced here: 67.2 us
  starting transfers between devices  29.1 us (43%)
  blocking collectives  18.9 us (28%)
  waiting for transfers between devices  6.79 us (10%)
  local copies, waits for them, and re-layouts  5.98 us (9%)
  Pallas kernels  5.88 us (9%)
    all_to_all x1, blocking collectives, exchange(): lax.all_to_all(part, ('zl', 'x'), 0, 0, tiled=True).reshape(4, 4, 4, G * G)  18.9 us
    ppermute x1, starting transfers between devices, exchange(): other = lax.ppermute(mine, 'zh', turn(2, 1))  7.73 us
    ppermute x3, waiting for transfers between devices, exchange(): lax.ppermute(target_block, 'zl', flip(4, k))  5.9 us
    ppermute x3, starting transfers between devices, exchange(): first = {i: lax.ppermute(block, plane, weave(i, 0)) for i in SHIFTS}  5.68 us
    pallas_call x1, Pallas kernels, pair_sums(): pl.pallas_call(pair_kernel, out_shape=jax.ShapeDtypeStruct((16, 4, 32, 12...  4.51 us
    ppermute x4, starting transfers between devices, exchange(): other_core = [lax.ppermute(own_core[l], 'c', turn(2, 1)) for l in range(4)]  4.47 us
    ppermute x3, starting transfers between devices, exchange(): lax.ppermute(target_block, 'zl', flip(4, k))  4.12 us
    unnamed x21, local copies, waits for them, and re-layouts  3.69 us
  transfers between devices with their start and end apart: 17, of which 4 were waited for; matrix products, arithmetic and copies ran while one was open for 2% of the time, Pallas kernels for 2%

profile of v1, /device:TPU:1, one launch (start us, length us, event | category | flops | bytes accessed | tf_op | source)
XLA Modules:
  0.0 67.2 jit_solution(12543503858763046868)
XLA Ops:
  0.0 0.0 copy-start.3
  0.0 0.0 copy-start.4
  0.0 0.0 copy-start.5
  0.0 0.8 %copy.18 = bf16[1,4,32,128]{3,2,1,0:T(8,128)(2,1)S(1)} copy(bf16[1,4,32,128]{3,1,2,0:T(4,128)(2,1)} %bitcast.33) | data formatting | bytes 65536
  0.9 7.7 %collective-permute-start.6 = (bf16[4,32,128]{2,1,0:T(8,128)(2,1)S(1)}, bf16[4,32,128]{2,1,0:T(8,128)(2,1)S(1)}, u32[]{:S(2)}, u32[]{:S(2)}) collective-permute-start(bf16[4,32,128]{2,1,0:T(8,128)(2,1)S(1)} %bitcast.29), channel_id=1, source_target_pairs={{0,128},{128,0},{1,129},{129,1},{2,130},{130,2},{3,131},{131,3},{4... | collective-permute-start | bytes 98312 | tf_op jit(solution)/shard_map/ppermute | solution.py:180
  8.6 1.1 %reshape.9 = bf16[4,4,32,128]{3,2,1,0:T(8,128)(2,1)S(1)} reshape(bf16[4,4,4096]{2,1,0:T(4,128)(2,1)} %param.12) | data formatting | bytes 262144 | tf_op jit(solution)/shard_map/reshape | solution.py:181
  9.7 0.2 collective-permute-done.6
  9.9 3.0 %collective-permute-start.8 = (bf16[2,4,32,128]{3,2,1,0:T(8,128)(2,1)S(1)}, bf16[2,4,32,128]{3,2,1,0:T(8,128)(2,1)S(1)}, u32[]{:S(2)}, u32[]{:S(2)}) collective-permute-start(bf16[2,4,32,128]{3,2,1,0:T(8,128)(2,1)S(1)} %get-tuple-element.10), channel_id=1, source_target_pairs={{0,2},{16,80},{1,3},{17,81},{2,0},{18,82},{3,1},{19,83},{32,34},{4... | collective-permute-start | bytes 196616 | tf_op jit(solution)/shard_map/ppermute | solution.py:189
  12.9 0.4 collective-permute-start.7
  13.3 2.3 %collective-permute-start.9 = (bf16[2,4,32,128]{3,2,1,0:T(8,128)(2,1)S(1)}, bf16[2,4,32,128]{3,2,1,0:T(8,128)(2,1)S(1)}, u32[]{:S(2)}, u32[]{:S(2)}) collective-permute-start(bf16[2,4,32,128]{3,2,1,0:T(8,128)(2,1)S(1)} %get-tuple-element.10), channel_id=1, source_target_pairs={{0,3},{16,112},{1,0},{17,113},{2,1},{18,114},{3,2},{19,115},{32,35... | collective-permute-start | bytes 196616 | tf_op jit(solution)/shard_map/ppermute | solution.py:189
  15.6 2.6 %collective-permute-start.2 = (bf16[4,32,128]{2,1,0:T(8,128)(2,1)S(1)}, bf16[4,32,128]{2,1,0:T(8,128)(2,1)S(1)}, u32[]{:S(2)}, u32[]{:S(2)}) collective-permute-start(bf16[4,32,128]{2,1,0:T(8,128)(2,1)S(1)} %get-tuple-element.6), channel_id=1, source_target_pairs={{0,3},{1,0},{2,1},{3,2},{4,7},{5,4},{6,5},{7,6},{8,11},{9,8},{10,9... | collective-permute-start | bytes 98312 | tf_op jit(solution)/shard_map/ppermute | solution.py:183
  18.2 0.5 collective-permute-start.1
  18.7 0.0 collective-permute-done.8
  18.7 0.6 collective-permute-start
  19.3 0.0 collective-permute-done.7
  19.3 0.0 collective-permute-done.9
  19.4 2.1 %collective-permute-start.12 = (bf16[4,2,4,32,128]{4,3,2,1,0:T(8,128)(2,1)S(1)}, bf16[4,2,4,32,128]{4,3,2,1,0:T(8,128)(2,1)S(1)}, u32[]{:S(2)}, u32[]{:S(2)}) collective-permute-start(bf16[4,2,4,32,128]{4,3,2,1,0:T(8,128)(2,1)S(1)} %pad_maximum_fusion.refs_4_), channel_id=1, source_target_pairs={{0,96},{16,19},{1,97},{17,16},{2,98},{18,17},{3,99},{19,18},{32,0}... | collective-permute-start | bytes 786440 | tf_op jit(solution)/shard_map/ppermute | solution.py:191
  21.5 1.2 %collective-permute-start.11 = (bf16[4,2,4,32,128]{4,3,2,1,0:T(8,128)(2,1)S(1)}, bf16[4,2,4,32,128]{4,3,2,1,0:T(8,128)(2,1)S(1)}, u32[]{:S(2)}, u32[]{:S(2)}) collective-permute-start(bf16[4,2,4,32,128]{4,3,2,1,0:T(8,128)(2,1)S(1)} %pad_maximum_fusion.refs_4_), channel_id=1, source_target_pairs={{0,64},{16,18},{1,65},{17,19},{2,66},{18,16},{3,67},{19,17},{32,96... | collective-permute-start | bytes 786440 | tf_op jit(solution)/shard_map/ppermute | solution.py:191
  22.7 0.0 collective-permute-done.2
  22.7 0.0 collective-permute-start.10
  22.7 0.0 collective-permute-done.1
  22.8 0.6 collective-permute-done
  23.4 2.7 %collective-permute-start.5 = (bf16[4,4,32,128]{3,2,1,0:T(8,128)(2,1)S(1)}, bf16[4,4,32,128]{3,2,1,0:T(8,128)(2,1)S(1)}, u32[]{:S(2)}, u32[]{:S(2)}) collective-permute-start(bf16[4,4,32,128]{3,2,1,0:T(8,128)(2,1)S(1)} %pad_maximum_fusion.1.refs_0_), channel_id=1, source_target_pairs={{0,12},{4,8},{8,4},{12,0},{1,13},{5,9},{9,5},{13,1},{2,14},{6,10},... | collective-permute-start | bytes 393224 | tf_op jit(solution)/shard_map/ppermute | solution.py:185
  26.1 0.0 collective-permute-start.4
  26.1 3.3 %collective-permute-done.5.refs_3_ = bf16[4,4,32,128]{3,2,1,0:T(8,128)(2,1)S(1)} collective-permute-done((bf16[4,4,32,128]{3,2,1,0:T(8,128)(2,1)S(1)}, bf16[4,4,32,128]{3,2,1,0:T(8,128)(2,1)S(1)}, u32[]{:S(2)}, u32[]{:S(2)}) %collective-permute-start.5) | collective-permute-done | bytes 131104 | tf_op jit(solution)/shard_map/ppermute | solution.py:185
  29.4 3.3 %collective-permute-start.13 = (bf16[4,2,4,32,128]{4,3,2,1,0:T(8,128)(2,1)S(1)}, bf16[4,2,4,32,128]{4,3,2,1,0:T(8,128)(2,1)S(1)}, u32[]{:S(2)}, u32[]{:S(2)}) collective-permute-start(bf16[4,2,4,32,128]{4,3,2,1,0:T(8,128)(2,1)S(1)} %pad_maximum_fusion.refs_4_), channel_id=1, source_target_pairs={{0,16},{16,0},{1,17},{17,1},{2,18},{18,2},{3,19},{19,3},{4,20},{20... | collective-permute-start | bytes 786440 | tf_op jit(solution)/shard_map/ppermute | solution.py:193
  32.7 0.0 collective-permute-done.12.refs_7_
  32.7 0.0 collective-permute-start.16
  32.7 0.0 collective-permute-done.11.refs_6_
  32.7 0.5 collective-permute-start.15
  33.2 0.0 collective-permute-done.10.refs_5_
  33.2 0.7 collective-permute-start.14
  33.9 2.6 %collective-permute-done.4.refs_2_ = bf16[4,4,32,128]{3,2,1,0:T(8,128)(2,1)S(1)} collective-permute-done((bf16[4,4,32,128]{3,2,1,0:T(8,128)(2,1)S(1)}, bf16[4,4,32,128]{3,2,1,0:T(8,128)(2,1)S(1)}, u32[]{:S(2)}, u32[]{:S(2)}) %collective-permute-start.4) | collective-permute-done | bytes 131104 | tf_op jit(solution)/shard_map/ppermute | solution.py:185
  36.5 1.4 %collective-permute-start.3 = (bf16[4,4,32,128]{3,2,1,0:T(8,128)(2,1)S(1)}, bf16[4,4,32,128]{3,2,1,0:T(8,128)(2,1)S(1)}, u32[]{:S(2)}, u32[]{:S(2)}) collective-permute-start(bf16[4,4,32,128]{3,2,1,0:T(8,128)(2,1)S(1)} %pad_maximum_fusion.1.refs_0_), channel_id=1, source_target_pairs={{0,4},{4,0},{8,12},{12,8},{1,5},{5,1},{9,13},{13,9},{2,6},{6,2},{1... | collective-permute-start | bytes 393224 | tf_op jit(solution)/shard_map/ppermute | solution.py:185
  37.9 0.8 %copy-done.6 = f32[64,64]{1,0:T(8,128)S(1)} copy-done((f32[64,64]{1,0:T(8,128)S(1)}, f32[64,64]{1,0:T(8,128)}, u32[]{:S(2)}) %copy-start.6) | copy-done | bytes 16408
  38.7 0.8 %copy-done.7 = f32[64,128]{1,0:T(8,128)S(1)} copy-done((f32[64,128]{1,0:T(8,128)S(1)}, f32[64,128]{1,0:T(8,128)}, u32[]{:S(2)}) %copy-start.7) | copy-done | bytes 32792
  39.4 0.7 copy-done.8
  40.1 0.7 copy-done.9
  40.7 1.4 %shard_map.118.refs_12_ = f32[64,64,128]{2,1,0:T(8,128)S(1)} custom-call(f32[8]{0:T(128)S(1)} %copy-done.8, f32[8]{0:T(128)S(1)} %copy-done.9, f32[64,128]{1,0:T(8,128)S(1)} %copy-done.7, f32[64,64]{1,0:T(8,128)S(1)} %copy-done.6), custom_call_target="tpu_custom_call" | custom-call | flops 8388608 | bytes 3145728 | tf_op jit(solution)/shard_map/pallas_call | solution.py:66
  42.1 0.0 collective-permute-done.3.refs_1_
  42.1 0.0 collective-permute-done.16.refs_11_
  42.2 0.0 collective-permute-done.15.refs_10_
  42.2 4.5 %shard_map.119 = bf16[16,4,32,128]{3,2,1,0:T(8,128)(2,1)S(1)} custom-call(bf16[4,4,32,128]{3,2,1,0:T(8,128)(2,1)S(1)} %pad_maximum_fusion.1.refs_0_, bf16[4,4,32,128]{3,2,1,0:T(8,128)(2,1)S(1)} %collective-permute-done.3.refs_1_, bf16[4,4,32,128]{3,2,1,0:T(8,128)(2,1)S(1)} %collective-permute-done.4.refs_2_, ...), custom_call_target="tpu_custom_call" | custom-call | tf_op jit(solution)/shard_map/pallas_call | solution.py:141
  46.8 18.9 %all_to_all.5 = bf16[16,4,32,128]{3,2,1,0:T(8,128)(2,1)S(1)} all-to-all(bf16[16,4,32,128]{3,2,1,0:T(8,128)(2,1)S(1)} %shard_map.119), channel_id=1, replica_groups=mesh['zh'=2,'y'=4,'c'=2,'zl'=4,'x'=4] {'zl','x'}, dimensions={0} | all-to-all | bytes 1048576 | tf_op jit(solution)/shard_map/all_to_all | solution.py:195
  65.6 0.4 reshape.11
  66.0 0.3 reduce_sum.9
  66.3 0.1 negate_bitcast_fusion
  66.4 0.9 %copy.13 = f32[4,4,4096]{2,1,0:T(4,128)} copy(f32[4,4,4096]{2,0,1:T(4,128)S(1)} %negate_bitcast_fusion) | data formatting | bytes 524288 | tf_op jit(solution)/shard_map/neg | solution.py:196
  (19 shorter events, 0.1 us)
Async XLA Ops:
  0.0 42.2 %copy-start = (bf16[256,256]{1,0:T(8,128)(2,1)S(1)}, bf16[256,256]{1,0:T(8,128)(2,1)}, u32[]{:S(2)}) copy-start(bf16[256,256]{1,0:T(8,128)(2,1)} %constant.69.clone.refs_18_) | copy-start | bytes 393220
  0.0 42.2 %copy-start.1 = (bf16[256,256]{1,0:T(8,128)(2,1)S(1)}, bf16[256,256]{1,0:T(8,128)(2,1)}, u32[]{:S(2)}) copy-start(bf16[256,256]{1,0:T(8,128)(2,1)} %constant.68.clone.refs_17_) | copy-start | bytes 393220
  0.0 42.2 %copy-start.2 = (bf16[256,256]{1,0:T(8,128)(2,1)S(1)}, bf16[256,256]{1,0:T(8,128)(2,1)}, u32[]{:S(2)}) copy-start(bf16[256,256]{1,0:T(8,128)(2,1)} %constant.67.clone.refs_16_) | copy-start | bytes 393220
  0.0 42.2 %copy-start.3 = (bf16[256,256]{1,0:T(8,128)(2,1)S(1)}, bf16[256,256]{1,0:T(8,128)(2,1)}, u32[]{:S(2)}) copy-start(bf16[256,256]{1,0:T(8,128)(2,1)} %constant.66.clone.refs_15_) | copy-start | bytes 393220
  0.0 42.2 %copy-start.4 = (bf16[256,256]{1,0:T(8,128)(2,1)S(1)}, bf16[256,256]{1,0:T(8,128)(2,1)}, u32[]{:S(2)}) copy-start(bf16[256,256]{1,0:T(8,128)(2,1)} %constant.65.clone.refs_14_) | copy-start | bytes 393220
  0.0 42.2 %copy-start.5 = (bf16[256,256]{1,0:T(8,128)(2,1)S(1)}, bf16[256,256]{1,0:T(8,128)(2,1)}, u32[]{:S(2)}) copy-start(bf16[256,256]{1,0:T(8,128)(2,1)} %constant.64.clone.refs_13_) | copy-start | bytes 393220
  0.9 9.0 %collective-permute-start.6 = (bf16[4,32,128]{2,1,0:T(8,128)(2,1)S(1)}, bf16[4,32,128]{2,1,0:T(8,128)(2,1)S(1)}, u32[]{:S(2)}, u32[]{:S(2)}) collective-permute-start(bf16[4,32,128]{2,1,0:T(8,128)(2,1)S(1)} %bitcast.29), channel_id=1, source_target_pairs={{0,128},{128,0},{1,129},{129,1},{2,130},{130,2},{3,131},{131,3},{4... | collective-permute-start | bytes 98312 | tf_op jit(solution)/shard_map/ppermute | solution.py:180
  9.9 8.8 %collective-permute-start.8 = (bf16[2,4,32,128]{3,2,1,0:T(8,128)(2,1)S(1)}, bf16[2,4,32,128]{3,2,1,0:T(8,128)(2,1)S(1)}, u32[]{:S(2)}, u32[]{:S(2)}) collective-permute-start(bf16[2,4,32,128]{3,2,1,0:T(8,128)(2,1)S(1)} %get-tuple-element.10), channel_id=1, source_target_pairs={{0,2},{16,80},{1,3},{17,81},{2,0},{18,82},{3,1},{19,83},{32,34},{4... | collective-permute-start | bytes 196616 | tf_op jit(solution)/shard_map/ppermute | solution.py:189
  12.9 6.4 %collective-permute-start.7 = (bf16[2,4,32,128]{3,2,1,0:T(8,128)(2,1)S(1)}, bf16[2,4,32,128]{3,2,1,0:T(8,128)(2,1)S(1)}, u32[]{:S(2)}, u32[]{:S(2)}) collective-permute-start(bf16[2,4,32,128]{3,2,1,0:T(8,128)(2,1)S(1)} %get-tuple-element.10), channel_id=1, source_target_pairs={{0,1},{16,48},{1,2},{17,49},{2,3},{18,50},{3,0},{19,51},{32,33},{4... | collective-permute-start | bytes 196616 | tf_op jit(solution)/shard_map/ppermute | solution.py:189
  13.3 6.0 %collective-permute-start.9 = (bf16[2,4,32,128]{3,2,1,0:T(8,128)(2,1)S(1)}, bf16[2,4,32,128]{3,2,1,0:T(8,128)(2,1)S(1)}, u32[]{:S(2)}, u32[]{:S(2)}) collective-permute-start(bf16[2,4,32,128]{3,2,1,0:T(8,128)(2,1)S(1)} %get-tuple-element.10), channel_id=1, source_target_pairs={{0,3},{16,112},{1,0},{17,113},{2,1},{18,114},{3,2},{19,115},{32,35... | collective-permute-start | bytes 196616 | tf_op jit(solution)/shard_map/ppermute | solution.py:189
  15.6 7.1 %collective-permute-start.2 = (bf16[4,32,128]{2,1,0:T(8,128)(2,1)S(1)}, bf16[4,32,128]{2,1,0:T(8,128)(2,1)S(1)}, u32[]{:S(2)}, u32[]{:S(2)}) collective-permute-start(bf16[4,32,128]{2,1,0:T(8,128)(2,1)S(1)} %get-tuple-element.6), channel_id=1, source_target_pairs={{0,3},{1,0},{2,1},{3,2},{4,7},{5,4},{6,5},{7,6},{8,11},{9,8},{10,9... | collective-permute-start | bytes 98312 | tf_op jit(solution)/shard_map/ppermute | solution.py:183
  18.2 4.6 %collective-permute-start.1 = (bf16[4,32,128]{2,1,0:T(8,128)(2,1)S(1)}, bf16[4,32,128]{2,1,0:T(8,128)(2,1)S(1)}, u32[]{:S(2)}, u32[]{:S(2)}) collective-permute-start(bf16[4,32,128]{2,1,0:T(8,128)(2,1)S(1)} %get-tuple-element.7), channel_id=1, source_target_pairs={{0,2},{1,3},{2,0},{3,1},{4,6},{5,7},{6,4},{7,5},{8,10},{9,11},{10,... | collective-permute-start | bytes 98312 | tf_op jit(solution)/shard_map/ppermute | solution.py:183
  18.7 4.7 %collective-permute-start = (bf16[4,32,128]{2,1,0:T(8,128)(2,1)S(1)}, bf16[4,32,128]{2,1,0:T(8,128)(2,1)S(1)}, u32[]{:S(2)}, u32[]{:S(2)}) collective-permute-start(bf16[4,32,128]{2,1,0:T(8,128)(2,1)S(1)} %get-tuple-element.8), channel_id=1, source_target_pairs={{0,1},{1,2},{2,3},{3,0},{4,5},{5,6},{6,7},{7,4},{8,9},{9,10},{10,1... | collective-permute-start | bytes 98312 | tf_op jit(solution)/shard_map/ppermute | solution.py:183
  19.4 13.4 %collective-permute-start.12 = (bf16[4,2,4,32,128]{4,3,2,1,0:T(8,128)(2,1)S(1)}, bf16[4,2,4,32,128]{4,3,2,1,0:T(8,128)(2,1)S(1)}, u32[]{:S(2)}, u32[]{:S(2)}) collective-permute-start(bf16[4,2,4,32,128]{4,3,2,1,0:T(8,128)(2,1)S(1)} %pad_maximum_fusion.refs_4_), channel_id=1, source_target_pairs={{0,96},{16,19},{1,97},{17,16},{2,98},{18,17},{3,99},{19,18},{32,0}... | collective-permute-start | bytes 786440 | tf_op jit(solution)/shard_map/ppermute | solution.py:191
  21.5 11.2 %collective-permute-start.11 = (bf16[4,2,4,32,128]{4,3,2,1,0:T(8,128)(2,1)S(1)}, bf16[4,2,4,32,128]{4,3,2,1,0:T(8,128)(2,1)S(1)}, u32[]{:S(2)}, u32[]{:S(2)}) collective-permute-start(bf16[4,2,4,32,128]{4,3,2,1,0:T(8,128)(2,1)S(1)} %pad_maximum_fusion.refs_4_), channel_id=1, source_target_pairs={{0,64},{16,18},{1,65},{17,19},{2,66},{18,16},{3,67},{19,17},{32,96... | collective-permute-start | bytes 786440 | tf_op jit(solution)/shard_map/ppermute | solution.py:191
  22.7 10.5 %collective-permute-start.10 = (bf16[4,2,4,32,128]{4,3,2,1,0:T(8,128)(2,1)S(1)}, bf16[4,2,4,32,128]{4,3,2,1,0:T(8,128)(2,1)S(1)}, u32[]{:S(2)}, u32[]{:S(2)}) collective-permute-start(bf16[4,2,4,32,128]{4,3,2,1,0:T(8,128)(2,1)S(1)} %pad_maximum_fusion.refs_4_), channel_id=1, source_target_pairs={{0,32},{16,17},{1,33},{17,18},{2,34},{18,19},{3,35},{19,16},{32,64... | collective-permute-start | bytes 786440 | tf_op jit(solution)/shard_map/ppermute | solution.py:191
  23.4 6.0 %collective-permute-start.5 = (bf16[4,4,32,128]{3,2,1,0:T(8,128)(2,1)S(1)}, bf16[4,4,32,128]{3,2,1,0:T(8,128)(2,1)S(1)}, u32[]{:S(2)}, u32[]{:S(2)}) collective-permute-start(bf16[4,4,32,128]{3,2,1,0:T(8,128)(2,1)S(1)} %pad_maximum_fusion.1.refs_0_), channel_id=1, source_target_pairs={{0,12},{4,8},{8,4},{12,0},{1,13},{5,9},{9,5},{13,1},{2,14},{6,10},... | collective-permute-start | bytes 393224 | tf_op jit(solution)/shard_map/ppermute | solution.py:185
  26.1 10.4 %collective-permute-start.4 = (bf16[4,4,32,128]{3,2,1,0:T(8,128)(2,1)S(1)}, bf16[4,4,32,128]{3,2,1,0:T(8,128)(2,1)S(1)}, u32[]{:S(2)}, u32[]{:S(2)}) collective-permute-start(bf16[4,4,32,128]{3,2,1,0:T(8,128)(2,1)S(1)} %pad_maximum_fusion.1.refs_0_), channel_id=1, source_target_pairs={{0,8},{4,12},{8,0},{12,4},{1,9},{5,13},{9,1},{13,5},{2,10},{6,14},... | collective-permute-start | bytes 393224 | tf_op jit(solution)/shard_map/ppermute | solution.py:185
  29.4 12.7 %collective-permute-start.13 = (bf16[4,2,4,32,128]{4,3,2,1,0:T(8,128)(2,1)S(1)}, bf16[4,2,4,32,128]{4,3,2,1,0:T(8,128)(2,1)S(1)}, u32[]{:S(2)}, u32[]{:S(2)}) collective-permute-start(bf16[4,2,4,32,128]{4,3,2,1,0:T(8,128)(2,1)S(1)} %pad_maximum_fusion.refs_4_), channel_id=1, source_target_pairs={{0,16},{16,0},{1,17},{17,1},{2,18},{18,2},{3,19},{19,3},{4,20},{20... | collective-permute-start | bytes 786440 | tf_op jit(solution)/shard_map/ppermute | solution.py:193
  32.7 9.4 %collective-permute-start.16 = (bf16[4,2,4,32,128]{4,3,2,1,0:T(8,128)(2,1)S(1)}, bf16[4,2,4,32,128]{4,3,2,1,0:T(8,128)(2,1)S(1)}, u32[]{:S(2)}, u32[]{:S(2)}) collective-permute-start(bf16[4,2,4,32,128]{4,3,2,1,0:T(8,128)(2,1)S(1)} %collective-permute-done.12.refs_7_), channel_id=1, source_target_pairs={{0,16},{16,0},{1,17},{17,1},{2,18},{18,2},{3,19},{19,3},{4,20},{20... | collective-permute-start | bytes 786440 | tf_op jit(solution)/shard_map/ppermute | solution.py:193
  32.7 9.4 %collective-permute-start.15 = (bf16[4,2,4,32,128]{4,3,2,1,0:T(8,128)(2,1)S(1)}, bf16[4,2,4,32,128]{4,3,2,1,0:T(8,128)(2,1)S(1)}, u32[]{:S(2)}, u32[]{:S(2)}) collective-permute-start(bf16[4,2,4,32,128]{4,3,2,1,0:T(8,128)(2,1)S(1)} %collective-permute-done.11.refs_6_), channel_id=1, source_target_pairs={{0,16},{16,0},{1,17},{17,1},{2,18},{18,2},{3,19},{19,3},{4,20},{20... | collective-permute-start | bytes 786440 | tf_op jit(solution)/shard_map/ppermute | solution.py:193
  33.2 8.9 %collective-permute-start.14 = (bf16[4,2,4,32,128]{4,3,2,1,0:T(8,128)(2,1)S(1)}, bf16[4,2,4,32,128]{4,3,2,1,0:T(8,128)(2,1)S(1)}, u32[]{:S(2)}, u32[]{:S(2)}) collective-permute-start(bf16[4,2,4,32,128]{4,3,2,1,0:T(8,128)(2,1)S(1)} %collective-permute-done.10.refs_5_), channel_id=1, source_target_pairs={{0,16},{16,0},{1,17},{17,1},{2,18},{18,2},{3,19},{19,3},{4,20},{20... | collective-permute-start | bytes 786440 | tf_op jit(solution)/shard_map/ppermute | solution.py:193
  36.5 5.6 %collective-permute-start.3 = (bf16[4,4,32,128]{3,2,1,0:T(8,128)(2,1)S(1)}, bf16[4,4,32,128]{3,2,1,0:T(8,128)(2,1)S(1)}, u32[]{:S(2)}, u32[]{:S(2)}) collective-permute-start(bf16[4,4,32,128]{3,2,1,0:T(8,128)(2,1)S(1)} %pad_maximum_fusion.1.refs_0_), channel_id=1, source_target_pairs={{0,4},{4,0},{8,12},{12,8},{1,5},{5,1},{9,13},{13,9},{2,6},{6,2},{1... | collective-permute-start | bytes 393224 | tf_op jit(solution)/shard_map/ppermute | solution.py:185
  37.9 0.8 %copy-start.6 = (f32[64,64]{1,0:T(8,128)S(1)}, f32[64,64]{1,0:T(8,128)}, u32[]{:S(2)}) copy-start(f32[64,64]{1,0:T(8,128)} %constant.63.clone.waves_turned) | copy-start | bytes 49156
  38.7 0.8 %copy-start.7 = (f32[64,128]{1,0:T(8,128)S(1)}, f32[64,128]{1,0:T(8,128)}, u32[]{:S(2)}) copy-start(f32[64,128]{1,0:T(8,128)} %constant.62.clone.waves) | copy-start | bytes 98308
  39.4 0.7 copy-start.8
  40.1 0.7 copy-start.9

commit v2 on v1

--- a/solution.py
+++ b/solution.py
@@ -171,17 +171,16 @@
     return pairs
 
 
-SHIFTS = (1, 3, 2)
+SHIFTS = (2, 1, 3)
 
 
 def exchange(targets, sources, exponents, coefficients):
     x = lax.axis_index("x")
+    pick = lambda j: lax.dynamic_index_in_dim(targets, (x + j) % 4, 0, keepdims=False)
+    rows = {j: lax.ppermute(pick(j), "x", turn(4, j)) for j in SHIFTS}
     mine = sources.reshape(4, 32, 128)
     other = lax.ppermute(mine, "zh", turn(2, 1))
-    packed = targets.reshape(4, 4, 32, 128)
-    pick = lambda j: lax.dynamic_index_in_dim(packed, (x + j) % 4, 0, keepdims=False)
-    rows = {j: lax.ppermute(pick(j), "x", turn(4, j)) for j in SHIFTS}
-    target_block = jnp.stack([pick(0)] + [rows[j] for j in range(1, 4)])
+    target_block = jnp.stack([pick(0)] + [rows[j] for j in range(1, 4)]).reshape(4, 4, 32, 128)
     lines = [target_block] + [lax.ppermute(target_block, "zl", flip(4, k)) for k in range(1, 4)]
     factor = spectrum(exponents, coefficients)
     plane = ("y", "c", "x")

time: 68.2 us -> 69.9 us (1.025)
  the two profiles are of different devices: /device:TPU:1 before, /device:TPU:24 now
where the time goes in v2:
time: 69.9 us; the launch traced here: 69.6 us
  starting transfers between devices  23.9 us (34%)
  blocking collectives  20.5 us (29%)
  waiting for transfers between devices  12.9 us (18%)
  Pallas kernels  5.88 us (8%)
  local copies, waits for them, and re-layouts  5.82 us (8%)
    all_to_all x1, blocking collectives, exchange(): lax.all_to_all(part, ('zl', 'x'), 0, 0, tiled=True).reshape(4, 4, 4, G * G)  20.5 us
    ppermute x3, waiting for transfers between devices, exchange(): lax.ppermute(target_block, 'zl', flip(4, k))  9.69 us
    ppermute x1, starting transfers between devices, exchange(): other = lax.ppermute(mine, 'zh', turn(2, 1))  7.19 us
    ppermute x3, starting transfers between devices, exchange(): rows = {j: lax.ppermute(pick(j), 'x', turn(4, j)) for j in SHIFTS}  5.13 us
    pallas_call x1, Pallas kernels, pair_sums(): pl.pallas_call(pair_kernel, out_shape=jax.ShapeDtypeStruct((16, 4, 32, 12...  4.51 us
    ppermute x3, starting transfers between devices, exchange(): second = {l: lax.ppermute(block, plane, weave(0, l)) for l in SHIFTS}  3.94 us
    ppermute x3, starting transfers between devices, exchange(): first = {i: lax.ppermute(block, plane, weave(i, 0)) for i in SHIFTS}  3.84 us
    unnamed x24, local copies, waits for them, and re-layouts  3.72 us
  transfers between devices with their start and end apart: 17, of which 7 were waited for; matrix products, arithmetic and copies ran while one was open for 1% of the time, Pallas kernels for 2%

profile of v2, /device:TPU:24, one launch (start us, length us, event | category | flops | bytes accessed | tf_op | source)
XLA Modules:
  0.0 69.6 jit_solution(10028738504574138218)
XLA Ops:
  0.0 0.0 copy-start.3
  0.0 0.0 copy-start.4
  0.0 0.0 copy-start.5
  0.0 0.8 %copy.26 = bf16[1,4,32,128]{3,2,1,0:T(8,128)(2,1)S(1)} copy(bf16[1,4,32,128]{3,1,2,0:T(4,128)(2,1)} %bitcast.48) | data formatting | bytes 65536
  0.9 7.2 %collective-permute-start.6 = (bf16[4,32,128]{2,1,0:T(8,128)(2,1)S(1)}, bf16[4,32,128]{2,1,0:T(8,128)(2,1)S(1)}, u32[]{:S(2)}, u32[]{:S(2)}) collective-permute-start(bf16[4,32,128]{2,1,0:T(8,128)(2,1)S(1)} %bitcast.44), channel_id=1, source_target_pairs={{0,128},{128,0},{1,129},{129,1},{2,130},{130,2},{3,131},{131,3},{4... | collective-permute-start | bytes 98312 | tf_op jit(solution)/shard_map/ppermute | solution.py:182
  8.1 0.9 %dynamic-slice_bitcast_fusion = (bf16[4,4096]{1,0:T(4,128)(2,1)S(1)}, bf16[4,4096]{1,0:T(4,128)(2,1)S(1)}, bf16[1,4,32,128]{3,1,2,0:T(4,128)(2,1)S(1)}, bf16[4,4096]{1,0:T(4,128)(2,1)S(1)}) fusion(bf16[4,4,4096]{2,1,0:T(4,128)(2,1)} %param.12, s32[]{:T(128)S(6)} %select_n.39, s32[]{:T(128)S(6)} %select_n.35, s32[]{:T(128)S(6)} %select_n.33, s32[]{:T(128)S(6)} %select_n.37), kind=kLoop, calls=%fused_computation.7 | loop fusion | bytes 262160 | tf_op jit(solution)/shard_map/jit(dynamic_index_in_dim)/squeeze | solution.py:179
  8.9 2.8 %collective-permute-start.2 = (bf16[4,4096]{1,0:T(4,128)(2,1)S(1)}, bf16[4,4096]{1,0:T(4,128)(2,1)S(1)}, u32[]{:S(2)}, u32[]{:S(2)}) collective-permute-start(bf16[4,4096]{1,0:T(4,128)(2,1)S(1)} %get-tuple-element.5), channel_id=1, source_target_pairs={{0,3},{1,0},{2,1},{3,2},{4,7},{5,4},{6,5},{7,6},{8,11},{9,8},{10,9... | collective-permute-start | bytes 98312 | tf_op jit(solution)/shard_map/ppermute | solution.py:180
  11.8 0.0 collective-permute-start
  11.8 2.3 %collective-permute-start.1 = (bf16[4,4096]{1,0:T(4,128)(2,1)S(1)}, bf16[4,4096]{1,0:T(4,128)(2,1)S(1)}, u32[]{:S(2)}, u32[]{:S(2)}) collective-permute-start(bf16[4,4096]{1,0:T(4,128)(2,1)S(1)} %get-tuple-element.8), channel_id=1, source_target_pairs={{0,2},{1,3},{2,0},{3,1},{4,6},{5,7},{6,4},{7,5},{8,10},{9,11},{10,... | collective-permute-start | bytes 98312 | tf_op jit(solution)/shard_map/ppermute | solution.py:180
  14.1 0.0 collective-permute-done.6
  14.1 1.3 %collective-permute-start.8 = (bf16[2,4,32,128]{3,2,1,0:T(8,128)(2,1)S(1)}, bf16[2,4,32,128]{3,2,1,0:T(8,128)(2,1)S(1)}, u32[]{:S(2)}, u32[]{:S(2)}) collective-permute-start(bf16[2,4,32,128]{3,2,1,0:T(8,128)(2,1)S(1)} %get-tuple-element.10), channel_id=1, source_target_pairs={{0,2},{16,80},{1,3},{17,81},{2,0},{18,82},{3,1},{19,83},{32,34},{4... | collective-permute-start | bytes 196616 | tf_op jit(solution)/shard_map/ppermute | solution.py:188
  15.4 0.8 %collective-permute-start.7 = (bf16[2,4,32,128]{3,2,1,0:T(8,128)(2,1)S(1)}, bf16[2,4,32,128]{3,2,1,0:T(8,128)(2,1)S(1)}, u32[]{:S(2)}, u32[]{:S(2)}) collective-permute-start(bf16[2,4,32,128]{3,2,1,0:T(8,128)(2,1)S(1)} %get-tuple-element.10), channel_id=1, source_target_pairs={{0,1},{16,48},{1,2},{17,49},{2,3},{18,50},{3,0},{19,51},{32,33},{4... | collective-permute-start | bytes 196616 | tf_op jit(solution)/shard_map/ppermute | solution.py:188
  16.2 0.7 %collective-permute-done = bf16[4,4096]{1,0:T(4,128)(2,1)S(1)} collective-permute-done((bf16[4,4096]{1,0:T(4,128)(2,1)S(1)}, bf16[4,4096]{1,0:T(4,128)(2,1)S(1)}, u32[]{:S(2)}, u32[]{:S(2)}) %collective-permute-start) | collective-permute-done | bytes 32800 | tf_op jit(solution)/shard_map/ppermute | solution.py:180
  16.9 1.8 %collective-permute-start.9 = (bf16[2,4,32,128]{3,2,1,0:T(8,128)(2,1)S(1)}, bf16[2,4,32,128]{3,2,1,0:T(8,128)(2,1)S(1)}, u32[]{:S(2)}, u32[]{:S(2)}) collective-permute-start(bf16[2,4,32,128]{3,2,1,0:T(8,128)(2,1)S(1)} %get-tuple-element.10), channel_id=1, source_target_pairs={{0,3},{16,112},{1,0},{17,113},{2,1},{18,114},{3,2},{19,115},{32,35... | collective-permute-start | bytes 196616 | tf_op jit(solution)/shard_map/ppermute | solution.py:188
  18.7 0.0 collective-permute-done.1
  18.7 1.2 %collective-permute-done.8 = bf16[2,4,32,128]{3,2,1,0:T(8,128)(2,1)S(1)} collective-permute-done((bf16[2,4,32,128]{3,2,1,0:T(8,128)(2,1)S(1)}, bf16[2,4,32,128]{3,2,1,0:T(8,128)(2,1)S(1)}, u32[]{:S(2)}, u32[]{:S(2)}) %collective-permute-start.8) | collective-permute-done | bytes 65568 | tf_op jit(solution)/shard_map/ppermute | solution.py:188
  19.9 0.9 %collective-permute-done.7 = bf16[2,4,32,128]{3,2,1,0:T(8,128)(2,1)S(1)} collective-permute-done((bf16[2,4,32,128]{3,2,1,0:T(8,128)(2,1)S(1)}, bf16[2,4,32,128]{3,2,1,0:T(8,128)(2,1)S(1)}, u32[]{:S(2)}, u32[]{:S(2)}) %collective-permute-start.7) | collective-permute-done | bytes 65568 | tf_op jit(solution)/shard_map/ppermute | solution.py:188
  20.9 0.3 collective-permute-done.9
  21.2 0.8 %collective-permute-start.12 = (bf16[4,2,4,32,128]{4,3,2,1,0:T(8,128)(2,1)S(1)}, bf16[4,2,4,32,128]{4,3,2,1,0:T(8,128)(2,1)S(1)}, u32[]{:S(2)}, u32[]{:S(2)}) collective-permute-start(bf16[4,2,4,32,128]{4,3,2,1,0:T(8,128)(2,1)S(1)} %pad_maximum_fusion.refs_4_), channel_id=1, source_target_pairs={{0,96},{16,19},{1,97},{17,16},{2,98},{18,17},{3,99},{19,18},{32,0}... | collective-permute-start | bytes 786440 | tf_op jit(solution)/shard_map/ppermute | solution.py:190
  22.0 0.9 %collective-permute-start.11 = (bf16[4,2,4,32,128]{4,3,2,1,0:T(8,128)(2,1)S(1)}, bf16[4,2,4,32,128]{4,3,2,1,0:T(8,128)(2,1)S(1)}, u32[]{:S(2)}, u32[]{:S(2)}) collective-permute-start(bf16[4,2,4,32,128]{4,3,2,1,0:T(8,128)(2,1)S(1)} %pad_maximum_fusion.refs_4_), channel_id=1, source_target_pairs={{0,64},{16,18},{1,65},{17,19},{2,66},{18,16},{3,67},{19,17},{32,96... | collective-permute-start | bytes 786440 | tf_op jit(solution)/shard_map/ppermute | solution.py:190
  23.0 2.2 %collective-permute-start.10 = (bf16[4,2,4,32,128]{4,3,2,1,0:T(8,128)(2,1)S(1)}, bf16[4,2,4,32,128]{4,3,2,1,0:T(8,128)(2,1)S(1)}, u32[]{:S(2)}, u32[]{:S(2)}) collective-permute-start(bf16[4,2,4,32,128]{4,3,2,1,0:T(8,128)(2,1)S(1)} %pad_maximum_fusion.refs_4_), channel_id=1, source_target_pairs={{0,32},{16,17},{1,33},{17,18},{2,34},{18,19},{3,35},{19,16},{32,64... | collective-permute-start | bytes 786440 | tf_op jit(solution)/shard_map/ppermute | solution.py:190
  25.1 0.0 collective-permute-done.2
  25.2 2.0 %collective-permute-start.5 = (bf16[4,4,32,128]{3,2,1,0:T(8,128)(2,1)S(1)}, bf16[4,4,32,128]{3,2,1,0:T(8,128)(2,1)S(1)}, u32[]{:S(2)}, u32[]{:S(2)}) collective-permute-start(bf16[4,4,32,128]{3,2,1,0:T(8,128)(2,1)S(1)} %bitcast_dynamic-update-slice_fusion.refs_0_), channel_id=1, source_target_pairs={{0,12},{4,8},{8,4},{12,0},{1,13},{5,9},{9,5},{13,1},{2,14},{6,10},... | collective-permute-start | bytes 393224 | tf_op jit(solution)/shard_map/ppermute | solution.py:184
  27.2 0.6 collective-permute-start.4
  27.7 4.6 %collective-permute-done.5.refs_3_ = bf16[4,4,32,128]{3,2,1,0:T(8,128)(2,1)S(1)} collective-permute-done((bf16[4,4,32,128]{3,2,1,0:T(8,128)(2,1)S(1)}, bf16[4,4,32,128]{3,2,1,0:T(8,128)(2,1)S(1)}, u32[]{:S(2)}, u32[]{:S(2)}) %collective-permute-start.5) | collective-permute-done | bytes 131104 | tf_op jit(solution)/shard_map/ppermute | solution.py:184
  32.3 0.0 collective-permute-start.13
  32.3 0.0 collective-permute-done.12.refs_7_
  32.3 0.5 collective-permute-start.16
  32.8 0.1 collective-permute-start.15
  32.9 0.0 collective-permute-done.10.refs_5_
  32.9 0.4 collective-permute-start.14
  33.4 4.5 %collective-permute-done.4.refs_2_ = bf16[4,4,32,128]{3,2,1,0:T(8,128)(2,1)S(1)} collective-permute-done((bf16[4,4,32,128]{3,2,1,0:T(8,128)(2,1)S(1)}, bf16[4,4,32,128]{3,2,1,0:T(8,128)(2,1)S(1)}, u32[]{:S(2)}, u32[]{:S(2)}) %collective-permute-start.4) | collective-permute-done | bytes 131104 | tf_op jit(solution)/shard_map/ppermute | solution.py:184
  37.9 0.2 collective-permute-start.3
  38.1 0.8 %copy-done.6 = f32[64,64]{1,0:T(8,128)S(1)} copy-done((f32[64,64]{1,0:T(8,128)S(1)}, f32[64,64]{1,0:T(8,128)}, u32[]{:S(2)}) %copy-start.6) | copy-done | bytes 16408
  38.9 0.8 %copy-done.7 = f32[64,128]{1,0:T(8,128)S(1)} copy-done((f32[64,128]{1,0:T(8,128)S(1)}, f32[64,128]{1,0:T(8,128)}, u32[]{:S(2)}) %copy-start.7) | copy-done | bytes 32792
  39.6 0.7 copy-done.8
  40.3 0.7 copy-done.9
  40.9 1.4 %shard_map.118.refs_12_ = f32[64,64,128]{2,1,0:T(8,128)S(1)} custom-call(f32[8]{0:T(128)S(1)} %copy-done.8, f32[8]{0:T(128)S(1)} %copy-done.9, f32[64,128]{1,0:T(8,128)S(1)} %copy-done.7, f32[64,64]{1,0:T(8,128)S(1)} %copy-done.6), custom_call_target="tpu_custom_call" | custom-call | flops 8388608 | bytes 3145728 | tf_op jit(solution)/shard_map/pallas_call | solution.py:66
  42.3 0.6 collective-permute-done.3.refs_1_
  42.9 0.0 collective-permute-done.16.refs_11_
  42.9 0.0 collective-permute-done.15.refs_10_
  42.9 0.0 collective-permute-done.14.refs_9_
  43.0 4.5 %shard_map.119 = bf16[16,4,32,128]{3,2,1,0:T(8,128)(2,1)S(1)} custom-call(bf16[4,4,32,128]{3,2,1,0:T(8,128)(2,1)S(1)} %bitcast_dynamic-update-slice_fusion.refs_0_, bf16[4,4,32,128]{3,2,1,0:T(8,128)(2,1)S(1)} %collective-permute-done.3.refs_1_, bf16[4,4,32,128]{3,2,1,0:T(8,128)(2,1)S(1)} %collective-permute-done.4.refs_2_, ...), custom_call_target="tpu_custom_call" | custom-call | tf_op jit(solution)/shard_map/pallas_call | solution.py:141
  47.5 20.5 %all_to_all.5 = bf16[16,4,32,128]{3,2,1,0:T(8,128)(2,1)S(1)} all-to-all(bf16[16,4,32,128]{3,2,1,0:T(8,128)(2,1)S(1)} %shard_map.119), channel_id=1, replica_groups=mesh['zh'=2,'y'=4,'c'=2,'zl'=4,'x'=4] {'zl','x'}, dimensions={0} | all-to-all | bytes 1048576 | tf_op jit(solution)/shard_map/all_to_all | solution.py:194
  68.0 0.4 reshape.15
  68.3 0.3 reduce_sum.9
  68.6 0.1 negate_bitcast_fusion
  68.7 0.9 %copy.13 = f32[4,4,4096]{2,1,0:T(4,128)} copy(f32[4,4,4096]{2,0,1:T(4,128)S(1)} %negate_bitcast_fusion) | data formatting | bytes 524288 | tf_op jit(solution)/shard_map/neg | solution.py:195
  (21 shorter events, 0.1 us)
Async XLA Ops:
  0.0 42.9 %copy-start = (bf16[256,256]{1,0:T(8,128)(2,1)S(1)}, bf16[256,256]{1,0:T(8,128)(2,1)}, u32[]{:S(2)}) copy-start(bf16[256,256]{1,0:T(8,128)(2,1)} %constant.69.clone.refs_18_) | copy-start | bytes 393220
  0.0 42.9 %copy-start.1 = (bf16[256,256]{1,0:T(8,128)(2,1)S(1)}, bf16[256,256]{1,0:T(8,128)(2,1)}, u32[]{:S(2)}) copy-start(bf16[256,256]{1,0:T(8,128)(2,1)} %constant.68.clone.refs_17_) | copy-start | bytes 393220
  0.0 42.9 %copy-start.2 = (bf16[256,256]{1,0:T(8,128)(2,1)S(1)}, bf16[256,256]{1,0:T(8,128)(2,1)}, u32[]{:S(2)}) copy-start(bf16[256,256]{1,0:T(8,128)(2,1)} %constant.67.clone.refs_16_) | copy-start | bytes 393220
  0.0 42.9 %copy-start.3 = (bf16[256,256]{1,0:T(8,128)(2,1)S(1)}, bf16[256,256]{1,0:T(8,128)(2,1)}, u32[]{:S(2)}) copy-start(bf16[256,256]{1,0:T(8,128)(2,1)} %constant.66.clone.refs_15_) | copy-start | bytes 393220
  0.0 42.9 %copy-start.4 = (bf16[256,256]{1,0:T(8,128)(2,1)S(1)}, bf16[256,256]{1,0:T(8,128)(2,1)}, u32[]{:S(2)}) copy-start(bf16[256,256]{1,0:T(8,128)(2,1)} %constant.65.clone.refs_14_) | copy-start | bytes 393220
  0.0 42.9 %copy-start.5 = (bf16[256,256]{1,0:T(8,128)(2,1)S(1)}, bf16[256,256]{1,0:T(8,128)(2,1)}, u32[]{:S(2)}) copy-start(bf16[256,256]{1,0:T(8,128)(2,1)} %constant.64.clone.refs_13_) | copy-start | bytes 393220
  0.9 13.2 %collective-permute-start.6 = (bf16[4,32,128]{2,1,0:T(8,128)(2,1)S(1)}, bf16[4,32,128]{2,1,0:T(8,128)(2,1)S(1)}, u32[]{:S(2)}, u32[]{:S(2)}) collective-permute-start(bf16[4,32,128]{2,1,0:T(8,128)(2,1)S(1)} %bitcast.44), channel_id=1, source_target_pairs={{0,128},{128,0},{1,129},{129,1},{2,130},{130,2},{3,131},{131,3},{4... | collective-permute-start | bytes 98312 | tf_op jit(solution)/shard_map/ppermute | solution.py:182
  8.9 16.2 %collective-permute-start.2 = (bf16[4,4096]{1,0:T(4,128)(2,1)S(1)}, bf16[4,4096]{1,0:T(4,128)(2,1)S(1)}, u32[]{:S(2)}, u32[]{:S(2)}) collective-permute-start(bf16[4,4096]{1,0:T(4,128)(2,1)S(1)} %get-tuple-element.5), channel_id=1, source_target_pairs={{0,3},{1,0},{2,1},{3,2},{4,7},{5,4},{6,5},{7,6},{8,11},{9,8},{10,9... | collective-permute-start | bytes 98312 | tf_op jit(solution)/shard_map/ppermute | solution.py:180
  11.8 5.1 %collective-permute-start = (bf16[4,4096]{1,0:T(4,128)(2,1)S(1)}, bf16[4,4096]{1,0:T(4,128)(2,1)S(1)}, u32[]{:S(2)}, u32[]{:S(2)}) collective-permute-start(bf16[4,4096]{1,0:T(4,128)(2,1)S(1)} %get-tuple-element.6), channel_id=1, source_target_pairs={{0,1},{1,2},{2,3},{3,0},{4,5},{5,6},{6,7},{7,4},{8,9},{9,10},{10,1... | collective-permute-start | bytes 98312 | tf_op jit(solution)/shard_map/ppermute | solution.py:180
  11.8 6.9 %collective-permute-start.1 = (bf16[4,4096]{1,0:T(4,128)(2,1)S(1)}, bf16[4,4096]{1,0:T(4,128)(2,1)S(1)}, u32[]{:S(2)}, u32[]{:S(2)}) collective-permute-start(bf16[4,4096]{1,0:T(4,128)(2,1)S(1)} %get-tuple-element.8), channel_id=1, source_target_pairs={{0,2},{1,3},{2,0},{3,1},{4,6},{5,7},{6,4},{7,5},{8,10},{9,11},{10,... | collective-permute-start | bytes 98312 | tf_op jit(solution)/shard_map/ppermute | solution.py:180
  14.1 5.9 %collective-permute-start.8 = (bf16[2,4,32,128]{3,2,1,0:T(8,128)(2,1)S(1)}, bf16[2,4,32,128]{3,2,1,0:T(8,128)(2,1)S(1)}, u32[]{:S(2)}, u32[]{:S(2)}) collective-permute-start(bf16[2,4,32,128]{3,2,1,0:T(8,128)(2,1)S(1)} %get-tuple-element.10), channel_id=1, source_target_pairs={{0,2},{16,80},{1,3},{17,81},{2,0},{18,82},{3,1},{19,83},{32,34},{4... | collective-permute-start | bytes 196616 | tf_op jit(solution)/shard_map/ppermute | solution.py:188
  15.4 5.5 %collective-permute-start.7 = (bf16[2,4,32,128]{3,2,1,0:T(8,128)(2,1)S(1)}, bf16[2,4,32,128]{3,2,1,0:T(8,128)(2,1)S(1)}, u32[]{:S(2)}, u32[]{:S(2)}) collective-permute-start(bf16[2,4,32,128]{3,2,1,0:T(8,128)(2,1)S(1)} %get-tuple-element.10), channel_id=1, source_target_pairs={{0,1},{16,48},{1,2},{17,49},{2,3},{18,50},{3,0},{19,51},{32,33},{4... | collective-permute-start | bytes 196616 | tf_op jit(solution)/shard_map/ppermute | solution.py:188
  16.9 4.3 %collective-permute-start.9 = (bf16[2,4,32,128]{3,2,1,0:T(8,128)(2,1)S(1)}, bf16[2,4,32,128]{3,2,1,0:T(8,128)(2,1)S(1)}, u32[]{:S(2)}, u32[]{:S(2)}) collective-permute-start(bf16[2,4,32,128]{3,2,1,0:T(8,128)(2,1)S(1)} %get-tuple-element.10), channel_id=1, source_target_pairs={{0,3},{16,112},{1,0},{17,113},{2,1},{18,114},{3,2},{19,115},{32,35... | collective-permute-start | bytes 196616 | tf_op jit(solution)/shard_map/ppermute | solution.py:188
  21.2 11.1 %collective-permute-start.12 = (bf16[4,2,4,32,128]{4,3,2,1,0:T(8,128)(2,1)S(1)}, bf16[4,2,4,32,128]{4,3,2,1,0:T(8,128)(2,1)S(1)}, u32[]{:S(2)}, u32[]{:S(2)}) collective-permute-start(bf16[4,2,4,32,128]{4,3,2,1,0:T(8,128)(2,1)S(1)} %pad_maximum_fusion.refs_4_), channel_id=1, source_target_pairs={{0,96},{16,19},{1,97},{17,16},{2,98},{18,17},{3,99},{19,18},{32,0}... | collective-permute-start | bytes 786440 | tf_op jit(solution)/shard_map/ppermute | solution.py:190
  22.0 10.8 %collective-permute-start.11 = (bf16[4,2,4,32,128]{4,3,2,1,0:T(8,128)(2,1)S(1)}, bf16[4,2,4,32,128]{4,3,2,1,0:T(8,128)(2,1)S(1)}, u32[]{:S(2)}, u32[]{:S(2)}) collective-permute-start(bf16[4,2,4,32,128]{4,3,2,1,0:T(8,128)(2,1)S(1)} %pad_maximum_fusion.refs_4_), channel_id=1, source_target_pairs={{0,64},{16,18},{1,65},{17,19},{2,66},{18,16},{3,67},{19,17},{32,96... | collective-permute-start | bytes 786440 | tf_op jit(solution)/shard_map/ppermute | solution.py:190
  23.0 10.0 %collective-permute-start.10 = (bf16[4,2,4,32,128]{4,3,2,1,0:T(8,128)(2,1)S(1)}, bf16[4,2,4,32,128]{4,3,2,1,0:T(8,128)(2,1)S(1)}, u32[]{:S(2)}, u32[]{:S(2)}) collective-permute-start(bf16[4,2,4,32,128]{4,3,2,1,0:T(8,128)(2,1)S(1)} %pad_maximum_fusion.refs_4_), channel_id=1, source_target_pairs={{0,32},{16,17},{1,33},{17,18},{2,34},{18,19},{3,35},{19,16},{32,64... | collective-permute-start | bytes 786440 | tf_op jit(solution)/shard_map/ppermute | solution.py:190
  25.2 7.2 %collective-permute-start.5 = (bf16[4,4,32,128]{3,2,1,0:T(8,128)(2,1)S(1)}, bf16[4,4,32,128]{3,2,1,0:T(8,128)(2,1)S(1)}, u32[]{:S(2)}, u32[]{:S(2)}) collective-permute-start(bf16[4,4,32,128]{3,2,1,0:T(8,128)(2,1)S(1)} %bitcast_dynamic-update-slice_fusion.refs_0_), channel_id=1, source_target_pairs={{0,12},{4,8},{8,4},{12,0},{1,13},{5,9},{9,5},{13,1},{2,14},{6,10},... | collective-permute-start | bytes 393224 | tf_op jit(solution)/shard_map/ppermute | solution.py:184
  27.2 10.7 %collective-permute-start.4 = (bf16[4,4,32,128]{3,2,1,0:T(8,128)(2,1)S(1)}, bf16[4,4,32,128]{3,2,1,0:T(8,128)(2,1)S(1)}, u32[]{:S(2)}, u32[]{:S(2)}) collective-permute-start(bf16[4,4,32,128]{3,2,1,0:T(8,128)(2,1)S(1)} %bitcast_dynamic-update-slice_fusion.refs_0_), channel_id=1, source_target_pairs={{0,8},{4,12},{8,0},{12,4},{1,9},{5,13},{9,1},{13,5},{2,10},{6,14},... | collective-permute-start | bytes 393224 | tf_op jit(solution)/shard_map/ppermute | solution.py:184
  32.3 10.5 %collective-permute-start.13 = (bf16[4,2,4,32,128]{4,3,2,1,0:T(8,128)(2,1)S(1)}, bf16[4,2,4,32,128]{4,3,2,1,0:T(8,128)(2,1)S(1)}, u32[]{:S(2)}, u32[]{:S(2)}) collective-permute-start(bf16[4,2,4,32,128]{4,3,2,1,0:T(8,128)(2,1)S(1)} %pad_maximum_fusion.refs_4_), channel_id=1, source_target_pairs={{0,16},{16,0},{1,17},{17,1},{2,18},{18,2},{3,19},{19,3},{4,20},{20... | collective-permute-start | bytes 786440 | tf_op jit(solution)/shard_map/ppermute | solution.py:192
  32.3 10.5 %collective-permute-start.16 = (bf16[4,2,4,32,128]{4,3,2,1,0:T(8,128)(2,1)S(1)}, bf16[4,2,4,32,128]{4,3,2,1,0:T(8,128)(2,1)S(1)}, u32[]{:S(2)}, u32[]{:S(2)}) collective-permute-start(bf16[4,2,4,32,128]{4,3,2,1,0:T(8,128)(2,1)S(1)} %collective-permute-done.12.refs_7_), channel_id=1, source_target_pairs={{0,16},{16,0},{1,17},{17,1},{2,18},{18,2},{3,19},{19,3},{4,20},{20... | collective-permute-start | bytes 786440 | tf_op jit(solution)/shard_map/ppermute | solution.py:192
  32.8 10.0 %collective-permute-start.15 = (bf16[4,2,4,32,128]{4,3,2,1,0:T(8,128)(2,1)S(1)}, bf16[4,2,4,32,128]{4,3,2,1,0:T(8,128)(2,1)S(1)}, u32[]{:S(2)}, u32[]{:S(2)}) collective-permute-start(bf16[4,2,4,32,128]{4,3,2,1,0:T(8,128)(2,1)S(1)} %collective-permute-done.11.refs_6_), channel_id=1, source_target_pairs={{0,16},{16,0},{1,17},{17,1},{2,18},{18,2},{3,19},{19,3},{4,20},{20... | collective-permute-start | bytes 786440 | tf_op jit(solution)/shard_map/ppermute | solution.py:192
  32.9 9.9 %collective-permute-start.14 = (bf16[4,2,4,32,128]{4,3,2,1,0:T(8,128)(2,1)S(1)}, bf16[4,2,4,32,128]{4,3,2,1,0:T(8,128)(2,1)S(1)}, u32[]{:S(2)}, u32[]{:S(2)}) collective-permute-start(bf16[4,2,4,32,128]{4,3,2,1,0:T(8,128)(2,1)S(1)} %collective-permute-done.10.refs_5_), channel_id=1, source_target_pairs={{0,16},{16,0},{1,17},{17,1},{2,18},{18,2},{3,19},{19,3},{4,20},{20... | collective-permute-start | bytes 786440 | tf_op jit(solution)/shard_map/ppermute | solution.py:192
  37.9 5.0 %collective-permute-start.3 = (bf16[4,4,32,128]{3,2,1,0:T(8,128)(2,1)S(1)}, bf16[4,4,32,128]{3,2,1,0:T(8,128)(2,1)S(1)}, u32[]{:S(2)}, u32[]{:S(2)}) collective-permute-start(bf16[4,4,32,128]{3,2,1,0:T(8,128)(2,1)S(1)} %bitcast_dynamic-update-slice_fusion.refs_0_), channel_id=1, source_target_pairs={{0,4},{4,0},{8,12},{12,8},{1,5},{5,1},{9,13},{13,9},{2,6},{6,2},{1... | collective-permute-start | bytes 393224 | tf_op jit(solution)/shard_map/ppermute | solution.py:184
  38.1 0.8 %copy-start.6 = (f32[64,64]{1,0:T(8,128)S(1)}, f32[64,64]{1,0:T(8,128)}, u32[]{:S(2)}) copy-start(f32[64,64]{1,0:T(8,128)} %constant.63.clone.waves_turned) | copy-start | bytes 49156
  38.9 0.8 %copy-start.7 = (f32[64,128]{1,0:T(8,128)S(1)}, f32[64,128]{1,0:T(8,128)}, u32[]{:S(2)}) copy-start(f32[64,128]{1,0:T(8,128)} %constant.62.clone.waves) | copy-start | bytes 98308
  39.6 0.7 copy-start.8
  40.3 0.7 copy-start.9

commit v3 on v1

--- a/solution.py
+++ b/solution.py
@@ -33,7 +33,13 @@
     return [jnp.asarray(m, BF16) for m in (z_in, y_in, x_in, x_in.T, y_in.T, z_in.T)]
 
 
-def spectrum_kernel(exponents, coefficients, waves, waves_turned, out, outer):
+def waves():
+    rows, freq = basis()
+    table = np.cos(2 * np.pi * np.outer(np.arange(G), freq) / G) / (rows * rows).sum(1)[None]
+    return jnp.asarray(np.concatenate([table, table], axis=1), F32)
+
+
+def spectrum(exponents, coefficients, table, out, outer):
     n = lax.broadcasted_iota(jnp.int32, (GAUSS, G), 1)
     term = lax.broadcasted_iota(jnp.int32, (GAUSS, G), 0)
     distance = jnp.minimum(n, G - n).astype(F32)
@@ -41,13 +47,15 @@
     for g in range(GAUSS):
         power = jnp.where(term == g, exponents[g], power)
         weight = jnp.where(term == g, coefficients[g], weight)
-    table = jnp.exp(-power * (distance * distance))
-    weighted = (weight * table).astype(BF16).astype(F32)
-    table = table.astype(BF16).astype(F32)
-    scaled = jnp.dot(weighted, waves[...], precision=lax.Precision.HIGHEST, preferred_element_type=F32)
-    plain = lax.dot_general(
-        waves_turned[...], table, (((1,), (1,)), ((), ())), precision=lax.Precision.HIGHEST, preferred_element_type=F32
-    )
+    kernel = jnp.exp(-power * (distance * distance))
+    weighted = (weight * kernel).astype(BF16).astype(F32)
+    kernel = kernel.astype(BF16).astype(F32)
+    scaled, plain = jnp.zeros((GAUSS, 128), F32), jnp.zeros((GAUSS, 128), F32)
+    for k in range(G):
+        row = table[k : k + 1]
+        scaled = scaled + weighted[:, k : k + 1] * row
+        plain = plain + kernel[:, k : k + 1] * row
+    plain = plain.T
     for g in range(GAUSS):
         outer[g] = plain[:40, g : g + 1] * scaled[g : g + 1]
     for k in range(G // 2 + 1):
@@ -59,31 +67,10 @@
             out[row, 40:] = total[8:32]
 
 
-def spectrum(exponents, coefficients):
-    rows, freq = basis()
-    waves = np.cos(2 * np.pi * np.outer(np.arange(G), freq) / G) / (rows * rows).sum(1)[None]
-    smem, vmem = pl.BlockSpec(memory_space=pltpu.SMEM), pl.BlockSpec(memory_space=pltpu.VMEM)
-    return pl.pallas_call(
-        spectrum_kernel,
-        out_shape=jax.ShapeDtypeStruct((G, G, 128), F32),
-        in_specs=[smem, smem, vmem, vmem],
-        out_specs=vmem,
-        scratch_shapes=[pltpu.VMEM((GAUSS, 40, 128), F32)],
-        cost_estimate=pl.CostEstimate(flops=8 << 20, bytes_accessed=3 << 20, transcendentals=512),
-        compiler_params=pltpu.CompilerParams(vmem_limit_bytes=8 << 20),
-    )(
-        exponents,
-        coefficients,
-        jnp.asarray(np.concatenate([waves, waves], axis=1), F32),
-        jnp.asarray(waves.T, F32),
-    )
-
-
 def pair_kernel(*refs):
-    t_in, s_in, d_ref = refs[:4], refs[4:12], refs[12]
-    z_in, y_in, x_in, x_out, y_out, z_out = refs[13:19]
-    out = refs[19]
-    t_all, s_all, s_rows, field = refs[20:]
+    t_in, s_in = refs[:4], refs[4:12]
+    exponents, coefficients, table, z_in, y_in, x_in, x_out, y_out, z_out, out = refs[12:22]
+    t_all, s_all, s_rows, field, d_ref, outer = refs[22:]
     zh, y, c, zl, x = (lax.axis_index(a) for a in ("zh", "y", "c", "zl", "x"))
     lane = lax.broadcasted_iota(jnp.int32, (4, 32, 128), 2) < 64
 
@@ -93,6 +80,7 @@
     def dot(a, b):
         return jnp.dot(a, b, preferred_element_type=F32)
 
+    spectrum(exponents, coefficients, table, d_ref, outer)
     for k in range(4):
         for j in range(4):
             t_all[lax.bitwise_xor(zl, k) * 4 + lax.rem(x - j + 4, 4)] = t_in[k][j]
@@ -136,21 +124,23 @@
         out[b] = jnp.where(lane, terms[:, :32], terms[:, 32:]).astype(out.dtype)
 
 
-def pair_sums(targets, sources, factor):
-    vmem = pl.BlockSpec(memory_space=pltpu.VMEM)
+def pair_sums(targets, sources, exponents, coefficients):
+    vmem, smem = pl.BlockSpec(memory_space=pltpu.VMEM), pl.BlockSpec(memory_space=pltpu.SMEM)
     return pl.pallas_call(
         pair_kernel,
         out_shape=jax.ShapeDtypeStruct((16, 4, 32, 128), BF16),
-        in_specs=[vmem] * 19,
+        in_specs=[vmem] * 12 + [smem] * 2 + [vmem] * 7,
         out_specs=vmem,
         scratch_shapes=[
             pltpu.VMEM((16, 4, 32, 128), BF16),
             pltpu.VMEM((4, 16, 4, 32, 128), BF16),
             pltpu.VMEM((16, 256, 256), BF16),
             pltpu.VMEM((16, 256, 256), BF16),
+            pltpu.VMEM((G, G, 128), F32),
+            pltpu.VMEM((GAUSS, 40, 128), F32),
         ],
         compiler_params=pltpu.CompilerParams(vmem_limit_bytes=24 << 20),
-    )(*targets, *sources, factor, *basis_blocks())
+    )(*targets, *sources, exponents, coefficients, waves(), *basis_blocks())
 
 
 def turn(n, by):
@@ -171,7 +161,7 @@
     return pairs
 
 
-SHIFTS = (1, 3, 2)
+SHIFTS = (2, 1, 3)
 
 
 def exchange(targets, sources, exponents, coefficients):
@@ -183,7 +173,6 @@
     rows = {j: lax.ppermute(pick(j), "x", turn(4, j)) for j in SHIFTS}
     target_block = jnp.stack([pick(0)] + [rows[j] for j in range(1, 4)])
     lines = [target_block] + [lax.ppermute(target_block, "zl", flip(4, k)) for k in range(1, 4)]
-    factor = spectrum(exponents, coefficients)
     plane = ("y", "c", "x")
     block = jnp.stack([mine, other])
     first = {i: lax.ppermute(block, plane, weave(i, 0)) for i in SHIFTS}
@@ -191,7 +180,7 @@
     second = {l: lax.ppermute(block, plane, weave(0, l)) for l in SHIFTS}
     own_core = [block] + [second[l] for l in range(1, 4)]
     other_core = [lax.ppermute(own_core[l], "c", turn(2, 1)) for l in range(4)]
-    part = pair_sums(lines, own_core + other_core, factor)
+    part = pair_sums(lines, own_core + other_core, exponents, coefficients)
     parts = lax.all_to_all(part, ("zl", "x"), 0, 0, tiled=True).reshape(4, 4, 4, G * G)
     return -parts.astype(F32).sum(0).transpose(1, 0, 2)
 

time: 68.2 us -> 68.4 us (level)
  local copies, waits for them, and re-layouts: 5.98 us -> 2.24 us
  waiting for transfers between devices: 6.79 us -> 10.2 us
    unnamed x21, local copies, waits for them, and re-layouts: 3.69 us -> 0.85 us
    ppermute x3, waiting for transfers between devices: 5.9 us -> 8.46 us  [exchange(): lax.ppermute(target_block, 'zl', flip(4, k))]
    pallas_call x1 -> x0, Pallas kernels: 1.37 us -> none  [spectrum(): pl.pallas_call(spectrum_kernel, out_shape=jax.ShapeDtypeStruct((G, G, 128...]
    reshape x1, local copies, waits for them, and re-layouts: 1.06 us -> 0.15 us  [exchange(): packed = targets.reshape(4, 4, 32, 128)]
    ppermute x1, waiting for transfers between devices: 0.22 us -> 1.12 us  [exchange(): other = lax.ppermute(mine, 'zh', turn(2, 1))]
    pallas_call x1, Pallas kernels: 4.51 us -> 5.36 us  [pair_sums(): pl.pallas_call(pair_kernel, out_shape=jax.ShapeDtypeStruct((16, 4, 32, 12...]
  transfers between devices with their start and end apart: 17 -> 17, of which waited for: 4 -> 5; matrix products, arithmetic and copies ran while one was open for 2% -> 0% of each run, Pallas kernels for 2% -> 0%
where the time goes in v3:
time: 68.4 us; the launch traced here: 67 us
  starting transfers between devices  29.1 us (43%)
  blocking collectives  19.5 us (29%)
  waiting for transfers between devices  10.2 us (15%)
  Pallas kernels  5.36 us (8%)
  local copies, waits for them, and re-layouts  2.24 us (3%)
    all_to_all x1, blocking collectives, exchange(): lax.all_to_all(part, ('zl', 'x'), 0, 0, tiled=True).reshape(4, 4, 4, G * G)  19.5 us
    ppermute x3, waiting for transfers between devices, exchange(): lax.ppermute(target_block, 'zl', flip(4, k))  8.46 us
    ppermute x1, starting transfers between devices, exchange(): other = lax.ppermute(mine, 'zh', turn(2, 1))  7.73 us
    ppermute x3, starting transfers between devices, exchange(): first = {i: lax.ppermute(block, plane, weave(i, 0)) for i in SHIFTS}  5.68 us
    pallas_call x1, Pallas kernels, pair_sums(): pl.pallas_call(pair_kernel, out_shape=jax.ShapeDtypeStruct((16, 4, 32, 12...  5.36 us
    ppermute x4, starting transfers between devices, exchange(): other_core = [lax.ppermute(own_core[l], 'c', turn(2, 1)) for l in range(4)]  4.52 us
    ppermute x3, starting transfers between devices, exchange(): lax.ppermute(target_block, 'zl', flip(4, k))  4.13 us
    ppermute x3, starting transfers between devices, exchange(): rows = {j: lax.ppermute(pick(j), 'x', turn(4, j)) for j in SHIFTS}  3.68 us
  transfers between devices with their start and end apart: 17, of which 5 were waited for; matrix products, arithmetic and copies ran while one was open for 0% of the time, Pallas kernels for 0%

profile of v3, /device:TPU:1, one launch (start us, length us, event | category | flops | bytes accessed | tf_op | source)
XLA Modules:
  0.0 67.0 jit_solution(16331250415540311813)
XLA Ops:
  0.0 0.8 %copy.17 = bf16[1,4,32,128]{3,2,1,0:T(8,128)(2,1)S(1)} copy(bf16[1,4,32,128]{3,1,2,0:T(4,128)(2,1)} %bitcast.33) | data formatting | bytes 65536
  0.8 7.7 %collective-permute-start.6 = (bf16[4,32,128]{2,1,0:T(8,128)(2,1)S(1)}, bf16[4,32,128]{2,1,0:T(8,128)(2,1)S(1)}, u32[]{:S(2)}, u32[]{:S(2)}) collective-permute-start(bf16[4,32,128]{2,1,0:T(8,128)(2,1)S(1)} %bitcast.29), channel_id=1, source_target_pairs={{0,128},{128,0},{1,129},{129,1},{2,130},{130,2},{3,131},{131,3},{4... | collective-permute-start | bytes 98312 | tf_op jit(solution)/shard_map/ppermute | solution.py:170
  8.5 0.0 copy-done.9
  8.5 0.2 reshape.9
  8.7 1.1 %collective-permute-done.6 = bf16[4,32,128]{2,1,0:T(8,128)(2,1)S(1)} collective-permute-done((bf16[4,32,128]{2,1,0:T(8,128)(2,1)S(1)}, bf16[4,32,128]{2,1,0:T(8,128)(2,1)S(1)}, u32[]{:S(2)}, u32[]{:S(2)}) %collective-permute-start.6) | collective-permute-done | bytes 32800 | tf_op jit(solution)/shard_map/ppermute | solution.py:170
  9.8 3.0 %collective-permute-start.8 = (bf16[2,4,32,128]{3,2,1,0:T(8,128)(2,1)S(1)}, bf16[2,4,32,128]{3,2,1,0:T(8,128)(2,1)S(1)}, u32[]{:S(2)}, u32[]{:S(2)}) collective-permute-start(bf16[2,4,32,128]{3,2,1,0:T(8,128)(2,1)S(1)} %get-tuple-element.10), channel_id=1, source_target_pairs={{0,2},{16,80},{1,3},{17,81},{2,0},{18,82},{3,1},{19,83},{32,34},{4... | collective-permute-start | bytes 196616 | tf_op jit(solution)/shard_map/ppermute | solution.py:178
  12.8 0.4 collective-permute-start.7
  13.2 2.3 %collective-permute-start.9 = (bf16[2,4,32,128]{3,2,1,0:T(8,128)(2,1)S(1)}, bf16[2,4,32,128]{3,2,1,0:T(8,128)(2,1)S(1)}, u32[]{:S(2)}, u32[]{:S(2)}) collective-permute-start(bf16[2,4,32,128]{3,2,1,0:T(8,128)(2,1)S(1)} %get-tuple-element.10), channel_id=1, source_target_pairs={{0,3},{16,112},{1,0},{17,113},{2,1},{18,114},{3,2},{19,115},{32,35... | collective-permute-start | bytes 196616 | tf_op jit(solution)/shard_map/ppermute | solution.py:178
  15.5 2.6 %collective-permute-start.2 = (bf16[4,32,128]{2,1,0:T(8,128)(2,1)S(1)}, bf16[4,32,128]{2,1,0:T(8,128)(2,1)S(1)}, u32[]{:S(2)}, u32[]{:S(2)}) collective-permute-start(bf16[4,32,128]{2,1,0:T(8,128)(2,1)S(1)} %get-tuple-element.6), channel_id=1, source_target_pairs={{0,3},{1,0},{2,1},{3,2},{4,7},{5,4},{6,5},{7,6},{8,11},{9,8},{10,9... | collective-permute-start | bytes 98312 | tf_op jit(solution)/shard_map/ppermute | solution.py:173
  18.1 0.5 collective-permute-start.1
  18.6 0.0 collective-permute-done.8
  18.6 0.6 collective-permute-start
  19.2 0.0 collective-permute-done.7
  19.2 0.0 collective-permute-done.9
  19.2 0.0 copy-start.3
  19.3 0.0 copy-start.4
  19.3 0.0 copy-start.5
  19.3 0.0 copy-start.7
  19.3 0.0 copy-start.8
  19.3 2.1 %collective-permute-start.12 = (bf16[4,2,4,32,128]{4,3,2,1,0:T(8,128)(2,1)S(1)}, bf16[4,2,4,32,128]{4,3,2,1,0:T(8,128)(2,1)S(1)}, u32[]{:S(2)}, u32[]{:S(2)}) collective-permute-start(bf16[4,2,4,32,128]{4,3,2,1,0:T(8,128)(2,1)S(1)} %pad_maximum_fusion.refs_4_), channel_id=1, source_target_pairs={{0,96},{16,19},{1,97},{17,16},{2,98},{18,17},{3,99},{19,18},{32,0}... | collective-permute-start | bytes 786440 | tf_op jit(solution)/shard_map/ppermute | solution.py:180
  21.5 1.2 %collective-permute-start.11 = (bf16[4,2,4,32,128]{4,3,2,1,0:T(8,128)(2,1)S(1)}, bf16[4,2,4,32,128]{4,3,2,1,0:T(8,128)(2,1)S(1)}, u32[]{:S(2)}, u32[]{:S(2)}) collective-permute-start(bf16[4,2,4,32,128]{4,3,2,1,0:T(8,128)(2,1)S(1)} %pad_maximum_fusion.refs_4_), channel_id=1, source_target_pairs={{0,64},{16,18},{1,65},{17,19},{2,66},{18,16},{3,67},{19,17},{32,96... | collective-permute-start | bytes 786440 | tf_op jit(solution)/shard_map/ppermute | solution.py:180
  22.7 0.0 collective-permute-done.2
  22.7 0.0 collective-permute-start.10
  22.7 0.0 collective-permute-done.1
  22.7 0.6 collective-permute-done
  23.3 2.7 %collective-permute-start.5 = (bf16[4,4,32,128]{3,2,1,0:T(8,128)(2,1)S(1)}, bf16[4,4,32,128]{3,2,1,0:T(8,128)(2,1)S(1)}, u32[]{:S(2)}, u32[]{:S(2)}) collective-permute-start(bf16[4,4,32,128]{3,2,1,0:T(8,128)(2,1)S(1)} %pad_maximum_fusion.1.refs_0_), channel_id=1, source_target_pairs={{0,12},{4,8},{8,4},{12,0},{1,13},{5,9},{9,5},{13,1},{2,14},{6,10},... | collective-permute-start | bytes 393224 | tf_op jit(solution)/shard_map/ppermute | solution.py:175
  26.1 0.0 collective-permute-start.4
  26.1 3.3 %collective-permute-done.5.refs_3_ = bf16[4,4,32,128]{3,2,1,0:T(8,128)(2,1)S(1)} collective-permute-done((bf16[4,4,32,128]{3,2,1,0:T(8,128)(2,1)S(1)}, bf16[4,4,32,128]{3,2,1,0:T(8,128)(2,1)S(1)}, u32[]{:S(2)}, u32[]{:S(2)}) %collective-permute-start.5) | collective-permute-done | bytes 131104 | tf_op jit(solution)/shard_map/ppermute | solution.py:175
  29.3 3.3 %collective-permute-start.13 = (bf16[4,2,4,32,128]{4,3,2,1,0:T(8,128)(2,1)S(1)}, bf16[4,2,4,32,128]{4,3,2,1,0:T(8,128)(2,1)S(1)}, u32[]{:S(2)}, u32[]{:S(2)}) collective-permute-start(bf16[4,2,4,32,128]{4,3,2,1,0:T(8,128)(2,1)S(1)} %pad_maximum_fusion.refs_4_), channel_id=1, source_target_pairs={{0,16},{16,0},{1,17},{17,1},{2,18},{18,2},{3,19},{19,3},{4,20},{20... | collective-permute-start | bytes 786440 | tf_op jit(solution)/shard_map/ppermute | solution.py:182
  32.6 0.0 collective-permute-done.12.refs_7_
  32.6 0.0 collective-permute-start.16
  32.6 0.0 collective-permute-done.11.refs_6_
  32.6 0.5 collective-permute-start.15
  33.2 0.0 collective-permute-done.10.refs_5_
  33.2 0.7 %collective-permute-start.14 = (bf16[4,2,4,32,128]{4,3,2,1,0:T(8,128)(2,1)S(1)}, bf16[4,2,4,32,128]{4,3,2,1,0:T(8,128)(2,1)S(1)}, u32[]{:S(2)}, u32[]{:S(2)}) collective-permute-start(bf16[4,2,4,32,128]{4,3,2,1,0:T(8,128)(2,1)S(1)} %collective-permute-done.10.refs_5_), channel_id=1, source_target_pairs={{0,16},{16,0},{1,17},{17,1},{2,18},{18,2},{3,19},{19,3},{4,20},{20... | collective-permute-start | bytes 786440 | tf_op jit(solution)/shard_map/ppermute | solution.py:182
  33.9 2.6 %collective-permute-done.4.refs_2_ = bf16[4,4,32,128]{3,2,1,0:T(8,128)(2,1)S(1)} collective-permute-done((bf16[4,4,32,128]{3,2,1,0:T(8,128)(2,1)S(1)}, bf16[4,4,32,128]{3,2,1,0:T(8,128)(2,1)S(1)}, u32[]{:S(2)}, u32[]{:S(2)}) %collective-permute-start.4) | collective-permute-done | bytes 131104 | tf_op jit(solution)/shard_map/ppermute | solution.py:175
  36.4 1.4 %collective-permute-start.3 = (bf16[4,4,32,128]{3,2,1,0:T(8,128)(2,1)S(1)}, bf16[4,4,32,128]{3,2,1,0:T(8,128)(2,1)S(1)}, u32[]{:S(2)}, u32[]{:S(2)}) collective-permute-start(bf16[4,4,32,128]{3,2,1,0:T(8,128)(2,1)S(1)} %pad_maximum_fusion.1.refs_0_), channel_id=1, source_target_pairs={{0,4},{4,0},{8,12},{12,8},{1,5},{5,1},{9,13},{13,9},{2,6},{6,2},{1... | collective-permute-start | bytes 393224 | tf_op jit(solution)/shard_map/ppermute | solution.py:175
  37.9 2.6 %collective-permute-done.3.refs_1_ = bf16[4,4,32,128]{3,2,1,0:T(8,128)(2,1)S(1)} collective-permute-done((bf16[4,4,32,128]{3,2,1,0:T(8,128)(2,1)S(1)}, bf16[4,4,32,128]{3,2,1,0:T(8,128)(2,1)S(1)}, u32[]{:S(2)}, u32[]{:S(2)}) %collective-permute-start.3) | collective-permute-done | bytes 131104 | tf_op jit(solution)/shard_map/ppermute | solution.py:175
  40.5 0.0 collective-permute-done.13.refs_8_
  40.5 0.0 collective-permute-done.16.refs_11_
  40.5 0.0 collective-permute-done.15.refs_10_
  40.5 0.0 collective-permute-done.14.refs_9_
  40.6 5.4 %shard_map.109 = bf16[16,4,32,128]{3,2,1,0:T(8,128)(2,1)S(1)} custom-call(bf16[4,4,32,128]{3,2,1,0:T(8,128)(2,1)S(1)} %pad_maximum_fusion.1.refs_0_, bf16[4,4,32,128]{3,2,1,0:T(8,128)(2,1)S(1)} %collective-permute-done.3.refs_1_, bf16[4,4,32,128]{3,2,1,0:T(8,128)(2,1)S(1)} %collective-permute-done.4.refs_2_, ...), custom_call_target="tpu_custom_call" | custom-call | tf_op jit(solution)/shard_map/pallas_call | solution.py:129
  45.9 19.5 %all_to_all.5 = bf16[16,4,32,128]{3,2,1,0:T(8,128)(2,1)S(1)} all-to-all(bf16[16,4,32,128]{3,2,1,0:T(8,128)(2,1)S(1)} %shard_map.109), channel_id=1, replica_groups=mesh['zh'=2,'y'=4,'c'=2,'zl'=4,'x'=4] {'zl','x'}, dimensions={0} | all-to-all | bytes 1048576 | tf_op jit(solution)/shard_map/all_to_all | solution.py:184
  65.4 0.4 reshape.11
  65.8 0.3 reduce_sum.9
  66.1 0.1 negate_bitcast_fusion
  66.1 0.9 %copy.12 = f32[4,4,4096]{2,1,0:T(4,128)} copy(f32[4,4,4096]{2,0,1:T(4,128)S(1)} %negate_bitcast_fusion) | data formatting | bytes 524288 | tf_op jit(solution)/shard_map/neg | solution.py:185
  (18 shorter events, 0.1 us)
Async XLA Ops:
  0.0 8.5 %copy-start.9 = (bf16[4,4,4096]{2,1,0:T(4,128)(2,1)S(1)}, bf16[4,4,4096]{2,1,0:T(4,128)(2,1)}, u32[]{:S(2)}) copy-start(bf16[4,4,4096]{2,1,0:T(4,128)(2,1)} %param.11) | copy-start | bytes 393220
  0.8 9.0 %collective-permute-start.6 = (bf16[4,32,128]{2,1,0:T(8,128)(2,1)S(1)}, bf16[4,32,128]{2,1,0:T(8,128)(2,1)S(1)}, u32[]{:S(2)}, u32[]{:S(2)}) collective-permute-start(bf16[4,32,128]{2,1,0:T(8,128)(2,1)S(1)} %bitcast.29), channel_id=1, source_target_pairs={{0,128},{128,0},{1,129},{129,1},{2,130},{130,2},{3,131},{131,3},{4... | collective-permute-start | bytes 98312 | tf_op jit(solution)/shard_map/ppermute | solution.py:170
  9.8 8.8 %collective-permute-start.8 = (bf16[2,4,32,128]{3,2,1,0:T(8,128)(2,1)S(1)}, bf16[2,4,32,128]{3,2,1,0:T(8,128)(2,1)S(1)}, u32[]{:S(2)}, u32[]{:S(2)}) collective-permute-start(bf16[2,4,32,128]{3,2,1,0:T(8,128)(2,1)S(1)} %get-tuple-element.10), channel_id=1, source_target_pairs={{0,2},{16,80},{1,3},{17,81},{2,0},{18,82},{3,1},{19,83},{32,34},{4... | collective-permute-start | bytes 196616 | tf_op jit(solution)/shard_map/ppermute | solution.py:178
  12.8 6.4 %collective-permute-start.7 = (bf16[2,4,32,128]{3,2,1,0:T(8,128)(2,1)S(1)}, bf16[2,4,32,128]{3,2,1,0:T(8,128)(2,1)S(1)}, u32[]{:S(2)}, u32[]{:S(2)}) collective-permute-start(bf16[2,4,32,128]{3,2,1,0:T(8,128)(2,1)S(1)} %get-tuple-element.10), channel_id=1, source_target_pairs={{0,1},{16,48},{1,2},{17,49},{2,3},{18,50},{3,0},{19,51},{32,33},{4... | collective-permute-start | bytes 196616 | tf_op jit(solution)/shard_map/ppermute | solution.py:178
  13.2 6.0 %collective-permute-start.9 = (bf16[2,4,32,128]{3,2,1,0:T(8,128)(2,1)S(1)}, bf16[2,4,32,128]{3,2,1,0:T(8,128)(2,1)S(1)}, u32[]{:S(2)}, u32[]{:S(2)}) collective-permute-start(bf16[2,4,32,128]{3,2,1,0:T(8,128)(2,1)S(1)} %get-tuple-element.10), channel_id=1, source_target_pairs={{0,3},{16,112},{1,0},{17,113},{2,1},{18,114},{3,2},{19,115},{32,35... | collective-permute-start | bytes 196616 | tf_op jit(solution)/shard_map/ppermute | solution.py:178
  15.5 25.0 %copy-start.6 = (f32[64,128]{1,0:T(8,128)S(1)}, f32[64,128]{1,0:T(8,128)}, u32[]{:S(2)}) copy-start(f32[64,128]{1,0:T(8,128)} %constant.60.clone.refs_14_) | copy-start | bytes 98308
  15.5 7.2 %collective-permute-start.2 = (bf16[4,32,128]{2,1,0:T(8,128)(2,1)S(1)}, bf16[4,32,128]{2,1,0:T(8,128)(2,1)S(1)}, u32[]{:S(2)}, u32[]{:S(2)}) collective-permute-start(bf16[4,32,128]{2,1,0:T(8,128)(2,1)S(1)} %get-tuple-element.6), channel_id=1, source_target_pairs={{0,3},{1,0},{2,1},{3,2},{4,7},{5,4},{6,5},{7,6},{8,11},{9,8},{10,9... | collective-permute-start | bytes 98312 | tf_op jit(solution)/shard_map/ppermute | solution.py:173
  18.1 4.6 %collective-permute-start.1 = (bf16[4,32,128]{2,1,0:T(8,128)(2,1)S(1)}, bf16[4,32,128]{2,1,0:T(8,128)(2,1)S(1)}, u32[]{:S(2)}, u32[]{:S(2)}) collective-permute-start(bf16[4,32,128]{2,1,0:T(8,128)(2,1)S(1)} %get-tuple-element.7), channel_id=1, source_target_pairs={{0,2},{1,3},{2,0},{3,1},{4,6},{5,7},{6,4},{7,5},{8,10},{9,11},{10,... | collective-permute-start | bytes 98312 | tf_op jit(solution)/shard_map/ppermute | solution.py:173
  18.6 4.7 %collective-permute-start = (bf16[4,32,128]{2,1,0:T(8,128)(2,1)S(1)}, bf16[4,32,128]{2,1,0:T(8,128)(2,1)S(1)}, u32[]{:S(2)}, u32[]{:S(2)}) collective-permute-start(bf16[4,32,128]{2,1,0:T(8,128)(2,1)S(1)} %get-tuple-element.8), channel_id=1, source_target_pairs={{0,1},{1,2},{2,3},{3,0},{4,5},{5,6},{6,7},{7,4},{8,9},{9,10},{10,1... | collective-permute-start | bytes 98312 | tf_op jit(solution)/shard_map/ppermute | solution.py:173
  19.2 21.3 %copy-start.2 = (bf16[256,256]{1,0:T(8,128)(2,1)S(1)}, bf16[256,256]{1,0:T(8,128)(2,1)}, u32[]{:S(2)}) copy-start(bf16[256,256]{1,0:T(8,128)(2,1)} %constant.64.clone.refs_18_) | copy-start | bytes 393220
  19.2 21.3 %copy-start.3 = (bf16[256,256]{1,0:T(8,128)(2,1)S(1)}, bf16[256,256]{1,0:T(8,128)(2,1)}, u32[]{:S(2)}) copy-start(bf16[256,256]{1,0:T(8,128)(2,1)} %constant.63.clone.refs_17_) | copy-start | bytes 393220
  19.3 21.3 %copy-start.4 = (bf16[256,256]{1,0:T(8,128)(2,1)S(1)}, bf16[256,256]{1,0:T(8,128)(2,1)}, u32[]{:S(2)}) copy-start(bf16[256,256]{1,0:T(8,128)(2,1)} %constant.62.clone.refs_16_) | copy-start | bytes 393220
  19.3 21.3 %copy-start.5 = (bf16[256,256]{1,0:T(8,128)(2,1)S(1)}, bf16[256,256]{1,0:T(8,128)(2,1)}, u32[]{:S(2)}) copy-start(bf16[256,256]{1,0:T(8,128)(2,1)} %constant.61.clone.refs_15_) | copy-start | bytes 393220
  19.3 21.3 %copy-start.7 = (f32[8]{0:T(128)S(1)}, f32[8]{0:T(128)}, u32[]{:S(2)}) copy-start(f32[8]{0:T(128)} %refs_12_.1) | copy-start | bytes 100
  19.3 21.3 %copy-start.8 = (f32[8]{0:T(128)S(1)}, f32[8]{0:T(128)}, u32[]{:S(2)}) copy-start(f32[8]{0:T(128)} %refs_13_.1) | copy-start | bytes 100
  19.3 13.3 %collective-permute-start.12 = (bf16[4,2,4,32,128]{4,3,2,1,0:T(8,128)(2,1)S(1)}, bf16[4,2,4,32,128]{4,3,2,1,0:T(8,128)(2,1)S(1)}, u32[]{:S(2)}, u32[]{:S(2)}) collective-permute-start(bf16[4,2,4,32,128]{4,3,2,1,0:T(8,128)(2,1)S(1)} %pad_maximum_fusion.refs_4_), channel_id=1, source_target_pairs={{0,96},{16,19},{1,97},{17,16},{2,98},{18,17},{3,99},{19,18},{32,0}... | collective-permute-start | bytes 786440 | tf_op jit(solution)/shard_map/ppermute | solution.py:180
  21.5 11.2 %collective-permute-start.11 = (bf16[4,2,4,32,128]{4,3,2,1,0:T(8,128)(2,1)S(1)}, bf16[4,2,4,32,128]{4,3,2,1,0:T(8,128)(2,1)S(1)}, u32[]{:S(2)}, u32[]{:S(2)}) collective-permute-start(bf16[4,2,4,32,128]{4,3,2,1,0:T(8,128)(2,1)S(1)} %pad_maximum_fusion.refs_4_), channel_id=1, source_target_pairs={{0,64},{16,18},{1,65},{17,19},{2,66},{18,16},{3,67},{19,17},{32,96... | collective-permute-start | bytes 786440 | tf_op jit(solution)/shard_map/ppermute | solution.py:180
  22.7 10.4 %collective-permute-start.10 = (bf16[4,2,4,32,128]{4,3,2,1,0:T(8,128)(2,1)S(1)}, bf16[4,2,4,32,128]{4,3,2,1,0:T(8,128)(2,1)S(1)}, u32[]{:S(2)}, u32[]{:S(2)}) collective-permute-start(bf16[4,2,4,32,128]{4,3,2,1,0:T(8,128)(2,1)S(1)} %pad_maximum_fusion.refs_4_), channel_id=1, source_target_pairs={{0,32},{16,17},{1,33},{17,18},{2,34},{18,19},{3,35},{19,16},{32,64... | collective-permute-start | bytes 786440 | tf_op jit(solution)/shard_map/ppermute | solution.py:180
  23.3 17.3 %copy-start = (bf16[256,256]{1,0:T(8,128)(2,1)S(1)}, bf16[256,256]{1,0:T(8,128)(2,1)}, u32[]{:S(2)}) copy-start(bf16[256,256]{1,0:T(8,128)(2,1)} %constant.66.clone.refs_20_) | copy-start | bytes 393220
  23.3 17.3 %copy-start.1 = (bf16[256,256]{1,0:T(8,128)(2,1)S(1)}, bf16[256,256]{1,0:T(8,128)(2,1)}, u32[]{:S(2)}) copy-start(bf16[256,256]{1,0:T(8,128)(2,1)} %constant.65.clone.refs_19_) | copy-start | bytes 393220
  23.3 6.0 %collective-permute-start.5 = (bf16[4,4,32,128]{3,2,1,0:T(8,128)(2,1)S(1)}, bf16[4,4,32,128]{3,2,1,0:T(8,128)(2,1)S(1)}, u32[]{:S(2)}, u32[]{:S(2)}) collective-permute-start(bf16[4,4,32,128]{3,2,1,0:T(8,128)(2,1)S(1)} %pad_maximum_fusion.1.refs_0_), channel_id=1, source_target_pairs={{0,12},{4,8},{8,4},{12,0},{1,13},{5,9},{9,5},{13,1},{2,14},{6,10},... | collective-permute-start | bytes 393224 | tf_op jit(solution)/shard_map/ppermute | solution.py:175
  26.1 10.4 %collective-permute-start.4 = (bf16[4,4,32,128]{3,2,1,0:T(8,128)(2,1)S(1)}, bf16[4,4,32,128]{3,2,1,0:T(8,128)(2,1)S(1)}, u32[]{:S(2)}, u32[]{:S(2)}) collective-permute-start(bf16[4,4,32,128]{3,2,1,0:T(8,128)(2,1)S(1)} %pad_maximum_fusion.1.refs_0_), channel_id=1, source_target_pairs={{0,8},{4,12},{8,0},{12,4},{1,9},{5,13},{9,1},{13,5},{2,10},{6,14},... | collective-permute-start | bytes 393224 | tf_op jit(solution)/shard_map/ppermute | solution.py:175
  29.3 11.1 %collective-permute-start.13 = (bf16[4,2,4,32,128]{4,3,2,1,0:T(8,128)(2,1)S(1)}, bf16[4,2,4,32,128]{4,3,2,1,0:T(8,128)(2,1)S(1)}, u32[]{:S(2)}, u32[]{:S(2)}) collective-permute-start(bf16[4,2,4,32,128]{4,3,2,1,0:T(8,128)(2,1)S(1)} %pad_maximum_fusion.refs_4_), channel_id=1, source_target_pairs={{0,16},{16,0},{1,17},{17,1},{2,18},{18,2},{3,19},{19,3},{4,20},{20... | collective-permute-start | bytes 786440 | tf_op jit(solution)/shard_map/ppermute | solution.py:182
  32.6 7.8 %collective-permute-start.16 = (bf16[4,2,4,32,128]{4,3,2,1,0:T(8,128)(2,1)S(1)}, bf16[4,2,4,32,128]{4,3,2,1,0:T(8,128)(2,1)S(1)}, u32[]{:S(2)}, u32[]{:S(2)}) collective-permute-start(bf16[4,2,4,32,128]{4,3,2,1,0:T(8,128)(2,1)S(1)} %collective-permute-done.12.refs_7_), channel_id=1, source_target_pairs={{0,16},{16,0},{1,17},{17,1},{2,18},{18,2},{3,19},{19,3},{4,20},{20... | collective-permute-start | bytes 786440 | tf_op jit(solution)/shard_map/ppermute | solution.py:182
  32.6 7.8 %collective-permute-start.15 = (bf16[4,2,4,32,128]{4,3,2,1,0:T(8,128)(2,1)S(1)}, bf16[4,2,4,32,128]{4,3,2,1,0:T(8,128)(2,1)S(1)}, u32[]{:S(2)}, u32[]{:S(2)}) collective-permute-start(bf16[4,2,4,32,128]{4,3,2,1,0:T(8,128)(2,1)S(1)} %collective-permute-done.11.refs_6_), channel_id=1, source_target_pairs={{0,16},{16,0},{1,17},{17,1},{2,18},{18,2},{3,19},{19,3},{4,20},{20... | collective-permute-start | bytes 786440 | tf_op jit(solution)/shard_map/ppermute | solution.py:182
  33.2 7.3 %collective-permute-start.14 = (bf16[4,2,4,32,128]{4,3,2,1,0:T(8,128)(2,1)S(1)}, bf16[4,2,4,32,128]{4,3,2,1,0:T(8,128)(2,1)S(1)}, u32[]{:S(2)}, u32[]{:S(2)}) collective-permute-start(bf16[4,2,4,32,128]{4,3,2,1,0:T(8,128)(2,1)S(1)} %collective-permute-done.10.refs_5_), channel_id=1, source_target_pairs={{0,16},{16,0},{1,17},{17,1},{2,18},{18,2},{3,19},{19,3},{4,20},{20... | collective-permute-start | bytes 786440 | tf_op jit(solution)/shard_map/ppermute | solution.py:182
  36.4 4.0 %collective-permute-start.3 = (bf16[4,4,32,128]{3,2,1,0:T(8,128)(2,1)S(1)}, bf16[4,4,32,128]{3,2,1,0:T(8,128)(2,1)S(1)}, u32[]{:S(2)}, u32[]{:S(2)}) collective-permute-start(bf16[4,4,32,128]{3,2,1,0:T(8,128)(2,1)S(1)} %pad_maximum_fusion.1.refs_0_), channel_id=1, source_target_pairs={{0,4},{4,0},{8,12},{12,8},{1,5},{5,1},{9,13},{13,9},{2,6},{6,2},{1... | collective-permute-start | bytes 393224 | tf_op jit(solution)/shard_map/ppermute | solution.py:175

commit v4 on v3

--- a/solution.py
+++ b/solution.py
@@ -68,9 +68,9 @@
 
 
 def pair_kernel(*refs):
-    t_in, s_in = refs[:4], refs[4:12]
-    exponents, coefficients, table, z_in, y_in, x_in, x_out, y_out, z_out, out = refs[12:22]
-    t_all, s_all, s_rows, field, d_ref, outer = refs[22:]
+    t_in, s_in = refs[:4], refs[4:14]
+    exponents, coefficients, table, z_in, y_in, x_in, x_out, y_out, z_out, out = refs[14:24]
+    t_all, s_all, s_rows, field, d_ref, outer = refs[24:]
     zh, y, c, zl, x = (lax.axis_index(a) for a in ("zh", "y", "c", "zl", "x"))
     lane = lax.broadcasted_iota(jnp.int32, (4, 32, 128), 2) < 64
 
@@ -90,9 +90,10 @@
         for l in range(4):
             for i in range(4):
                 by_x, by_y = i + core * (l - i), l + core * (i - l)
+                came = s_in[5 * e + (0, 1, 3 + i // 2, 2)[l]]
                 for m in range(2):
                     b = lax.rem(zh + m, 2) * 8 + lax.rem(y - by_y + 4, 4) * 2 + core
-                    s_all[by_x, b] = s_in[4 * e + l][i, m]
+                    s_all[by_x, b] = came[i % 2 if l == 2 else i, m]
 
     for b in range(16):
         target = t_all[b]
@@ -129,7 +130,7 @@
     return pl.pallas_call(
         pair_kernel,
         out_shape=jax.ShapeDtypeStruct((16, 4, 32, 128), BF16),
-        in_specs=[vmem] * 12 + [smem] * 2 + [vmem] * 7,
+        in_specs=[vmem] * 14 + [smem] * 2 + [vmem] * 7,
         out_specs=vmem,
         scratch_shapes=[
             pltpu.VMEM((16, 4, 32, 128), BF16),
@@ -177,9 +178,11 @@
     block = jnp.stack([mine, other])
     first = {i: lax.ppermute(block, plane, weave(i, 0)) for i in SHIFTS}
     block = jnp.stack([block] + [first[i] for i in range(1, 4)])
-    second = {l: lax.ppermute(block, plane, weave(0, l)) for l in SHIFTS}
-    own_core = [block] + [second[l] for l in range(1, 4)]
-    other_core = [lax.ppermute(own_core[l], "c", turn(2, 1)) for l in range(4)]
+    second = {l: lax.ppermute(block, plane, weave(0, l)) for l in (1, 3)}
+    halves = {1: second[1][:2], 3: second[3][2:]}
+    third = {l: lax.ppermute(halves[l], plane, weave(0, l)) for l in (1, 3)}
+    own_core = [block, second[1], second[3], third[1], third[3]]
+    other_core = [lax.ppermute(value, "c", turn(2, 1)) for value in own_core]
     part = pair_sums(lines, own_core + other_core, exponents, coefficients)
     parts = lax.all_to_all(part, ("zl", "x"), 0, 0, tiled=True).reshape(4, 4, 4, G * G)
     return -parts.astype(F32).sum(0).transpose(1, 0, 2)

time: 68.4 us -> 68.9 us (level); the launches traced: 67 us -> 68.6 us
  blocking collectives: 19.5 us -> 21.5 us
  waiting for transfers between devices: 10.2 us -> 9.29 us
    ppermute x3, waiting for transfers between devices: 8.46 us -> 5.18 us  [exchange(): lax.ppermute(target_block, 'zl', flip(4, k))]
    all_to_all x1, blocking collectives: 19.5 us -> 21.5 us  [exchange(): lax.all_to_all(part, ('zl', 'x'), 0, 0, tiled=True).reshape(4, 4, 4, G * G)]
    ppermute x3, waiting for transfers between devices: 0.57 us -> 1.85 us  [exchange(): rows = {j: lax.ppermute(pick(j), 'x', turn(4, j)) for j in SHIFTS}]
    ppermute x7 -> x9, waiting for transfers between devices: 0.02 us -> 1.13 us  [the longest x5 1.12 us: exchange(): other_core = [lax.ppermute(value, 'c', turn(2, 1)) for value in own_core]]
    ppermute x7 -> x9, starting transfers between devices: 7.91 us -> 8.91 us  [the longest x5 4.5 us: exchange(): other_core = [lax.ppermute(value, 'c', turn(2, 1)) for value in own_core]]
  transfers between devices with their start and end apart: 17 -> 19, of which waited for: 5 -> 6; matrix products, arithmetic and copies ran while one was open for 0% -> 0% of each run, Pallas kernels for 0% -> 0%
where the time goes in v4:
time: 68.9 us; the launch traced here: 68.6 us
  starting transfers between devices  29.6 us (43%)
  blocking collectives  21.5 us (31%)
  waiting for transfers between devices  9.29 us (13%)
  Pallas kernels  5.37 us (8%)
  local copies, waits for them, and re-layouts  2.26 us (3%)
    all_to_all x1, blocking collectives, exchange(): lax.all_to_all(part, ('zl', 'x'), 0, 0, tiled=True).reshape(4, 4, 4, G * G)  21.5 us
    ppermute x1, starting transfers between devices, exchange(): other = lax.ppermute(mine, 'zh', turn(2, 1))  7.73 us
    ppermute x3, starting transfers between devices, exchange(): first = {i: lax.ppermute(block, plane, weave(i, 0)) for i in SHIFTS}  5.68 us
    pallas_call x1, Pallas kernels, pair_sums(): pl.pallas_call(pair_kernel, out_shape=jax.ShapeDtypeStruct((16, 4, 32, 12...  5.37 us
    ppermute x3, waiting for transfers between devices, exchange(): lax.ppermute(target_block, 'zl', flip(4, k))  5.18 us
    ppermute x5, starting transfers between devices, exchange(): other_core = [lax.ppermute(value, 'c', turn(2, 1)) for value in own_core]  4.5 us
    ppermute x3, starting transfers between devices, exchange(): rows = {j: lax.ppermute(pick(j), 'x', turn(4, j)) for j in SHIFTS}  3.68 us
    ppermute x3, starting transfers between devices, exchange(): lax.ppermute(target_block, 'zl', flip(4, k))  3.63 us
  transfers between devices with their start and end apart: 19, of which 6 were waited for; matrix products, arithmetic and copies ran while one was open for 0% of the time, Pallas kernels for 0%

profile of v4, /device:TPU:1, one launch (start us, length us, event | category | flops | bytes accessed | tf_op | source)
XLA Modules:
  0.0 68.6 jit_solution(2463157085719669567)
XLA Ops:
  0.0 0.8 %copy.17 = bf16[1,4,32,128]{3,2,1,0:T(8,128)(2,1)S(1)} copy(bf16[1,4,32,128]{3,1,2,0:T(4,128)(2,1)} %bitcast.33) | data formatting | bytes 65536
  0.8 7.7 %collective-permute-start.6 = (bf16[4,32,128]{2,1,0:T(8,128)(2,1)S(1)}, bf16[4,32,128]{2,1,0:T(8,128)(2,1)S(1)}, u32[]{:S(2)}, u32[]{:S(2)}) collective-permute-start(bf16[4,32,128]{2,1,0:T(8,128)(2,1)S(1)} %bitcast.29), channel_id=1, source_target_pairs={{0,128},{128,0},{1,129},{129,1},{2,130},{130,2},{3,131},{131,3},{4... | collective-permute-start | bytes 98312 | tf_op jit(solution)/shard_map/ppermute | solution.py:171
  8.5 0.2 reshape.9
  8.7 1.1 %collective-permute-done.6 = bf16[4,32,128]{2,1,0:T(8,128)(2,1)S(1)} collective-permute-done((bf16[4,32,128]{2,1,0:T(8,128)(2,1)S(1)}, bf16[4,32,128]{2,1,0:T(8,128)(2,1)S(1)}, u32[]{:S(2)}, u32[]{:S(2)}) %collective-permute-start.6) | collective-permute-done | bytes 32800 | tf_op jit(solution)/shard_map/ppermute | solution.py:171
  9.8 3.0 %collective-permute-start.8 = (bf16[2,4,32,128]{3,2,1,0:T(8,128)(2,1)S(1)}, bf16[2,4,32,128]{3,2,1,0:T(8,128)(2,1)S(1)}, u32[]{:S(2)}, u32[]{:S(2)}) collective-permute-start(bf16[2,4,32,128]{3,2,1,0:T(8,128)(2,1)S(1)} %get-tuple-element.10), channel_id=1, source_target_pairs={{0,2},{16,80},{1,3},{17,81},{2,0},{18,82},{3,1},{19,83},{32,34},{4... | collective-permute-start | bytes 196616 | tf_op jit(solution)/shard_map/ppermute | solution.py:179
  12.8 0.4 collective-permute-start.7
  13.2 2.3 %collective-permute-start.9 = (bf16[2,4,32,128]{3,2,1,0:T(8,128)(2,1)S(1)}, bf16[2,4,32,128]{3,2,1,0:T(8,128)(2,1)S(1)}, u32[]{:S(2)}, u32[]{:S(2)}) collective-permute-start(bf16[2,4,32,128]{3,2,1,0:T(8,128)(2,1)S(1)} %get-tuple-element.10), channel_id=1, source_target_pairs={{0,3},{16,112},{1,0},{17,113},{2,1},{18,114},{3,2},{19,115},{32,35... | collective-permute-start | bytes 196616 | tf_op jit(solution)/shard_map/ppermute | solution.py:179
  15.5 2.6 %collective-permute-start.2 = (bf16[4,32,128]{2,1,0:T(8,128)(2,1)S(1)}, bf16[4,32,128]{2,1,0:T(8,128)(2,1)S(1)}, u32[]{:S(2)}, u32[]{:S(2)}) collective-permute-start(bf16[4,32,128]{2,1,0:T(8,128)(2,1)S(1)} %get-tuple-element.6), channel_id=1, source_target_pairs={{0,3},{1,0},{2,1},{3,2},{4,7},{5,4},{6,5},{7,6},{8,11},{9,8},{10,9... | collective-permute-start | bytes 98312 | tf_op jit(solution)/shard_map/ppermute | solution.py:174
  18.1 0.5 collective-permute-start.1
  18.6 0.0 collective-permute-done.8
  18.6 0.6 collective-permute-start
  19.2 0.0 collective-permute-done.7
  19.2 0.0 collective-permute-done.9
  19.2 0.0 copy-start.7
  19.2 0.0 copy-start.8
  19.3 2.1 %collective-permute-start.11 = (bf16[4,2,4,32,128]{4,3,2,1,0:T(8,128)(2,1)S(1)}, bf16[4,2,4,32,128]{4,3,2,1,0:T(8,128)(2,1)S(1)}, u32[]{:S(2)}, u32[]{:S(2)}) collective-permute-start(bf16[4,2,4,32,128]{4,3,2,1,0:T(8,128)(2,1)S(1)} %pad_maximum_fusion.refs_4_), channel_id=1, source_target_pairs={{0,96},{16,19},{1,97},{17,16},{2,98},{18,17},{3,99},{19,18},{32,0}... | collective-permute-start | bytes 786440 | tf_op jit(solution)/shard_map/ppermute | solution.py:181
  21.5 0.0 collective-permute-start.10
  21.5 0.0 collective-permute-done.2
  21.5 1.2 %collective-permute-done.1 = bf16[4,32,128]{2,1,0:T(8,128)(2,1)S(1)} collective-permute-done((bf16[4,32,128]{2,1,0:T(8,128)(2,1)S(1)}, bf16[4,32,128]{2,1,0:T(8,128)(2,1)S(1)}, u32[]{:S(2)}, u32[]{:S(2)}) %collective-permute-start.1) | collective-permute-done | bytes 32800 | tf_op jit(solution)/shard_map/ppermute | solution.py:174
  22.7 0.6 collective-permute-done
  23.3 2.7 %collective-permute-start.5 = (bf16[4,4,32,128]{3,2,1,0:T(8,128)(2,1)S(1)}, bf16[4,4,32,128]{3,2,1,0:T(8,128)(2,1)S(1)}, u32[]{:S(2)}, u32[]{:S(2)}) collective-permute-start(bf16[4,4,32,128]{3,2,1,0:T(8,128)(2,1)S(1)} %pad_maximum_fusion.1.refs_0_), channel_id=1, source_target_pairs={{0,12},{4,8},{8,4},{12,0},{1,13},{5,9},{9,5},{13,1},{2,14},{6,10},... | collective-permute-start | bytes 393224 | tf_op jit(solution)/shard_map/ppermute | solution.py:176
  26.1 0.0 collective-permute-start.4
  26.1 0.9 %collective-permute-start.3 = (bf16[4,4,32,128]{3,2,1,0:T(8,128)(2,1)S(1)}, bf16[4,4,32,128]{3,2,1,0:T(8,128)(2,1)S(1)}, u32[]{:S(2)}, u32[]{:S(2)}) collective-permute-start(bf16[4,4,32,128]{3,2,1,0:T(8,128)(2,1)S(1)} %pad_maximum_fusion.1.refs_0_), channel_id=1, source_target_pairs={{0,4},{4,0},{8,12},{12,8},{1,5},{5,1},{9,13},{13,9},{2,6},{6,2},{1... | collective-permute-start | bytes 393224 | tf_op jit(solution)/shard_map/ppermute | solution.py:176
  27.0 0.0 collective-permute-done.11.refs_6_
  27.0 2.0 %collective-permute-start.14 = (bf16[4,2,4,32,128]{4,3,2,1,0:T(8,128)(2,1)S(1)}, bf16[4,2,4,32,128]{4,3,2,1,0:T(8,128)(2,1)S(1)}, u32[]{:S(2)}, u32[]{:S(2)}) collective-permute-start(bf16[4,2,4,32,128]{4,3,2,1,0:T(8,128)(2,1)S(1)} %pad_maximum_fusion.refs_4_), channel_id=1, source_target_pairs={{0,16},{16,0},{1,17},{17,1},{2,18},{18,2},{3,19},{19,3},{4,20},{20... | collective-permute-start | bytes 786440 | tf_op jit(solution)/shard_map/ppermute | solution.py:185
  29.0 0.0 copy-start
  29.0 0.0 copy-start.1
  29.0 0.0 collective-permute-done.10.refs_5_
  29.0 2.2 %collective-permute-start.13 = (bf16[2,2,4,32,128]{4,3,2,1,0:T(8,128)(2,1)S(1)}, bf16[2,2,4,32,128]{4,3,2,1,0:T(8,128)(2,1)S(1)}, u32[]{:S(2)}, u32[]{:S(2)}) collective-permute-start(bf16[2,2,4,32,128]{4,3,2,1,0:T(8,128)(2,1)S(1)} %slice.9), channel_id=1, source_target_pairs={{0,96},{16,19},{1,97},{17,16},{2,98},{18,17},{3,99},{19,18},{32,0}... | collective-permute-start | bytes 393224 | tf_op jit(solution)/shard_map/ppermute | solution.py:183
  31.2 0.0 collective-permute-done.5.refs_3_
  31.2 0.1 collective-permute-start.12
  31.3 5.2 %collective-permute-done.4.refs_2_ = bf16[4,4,32,128]{3,2,1,0:T(8,128)(2,1)S(1)} collective-permute-done((bf16[4,4,32,128]{3,2,1,0:T(8,128)(2,1)S(1)}, bf16[4,4,32,128]{3,2,1,0:T(8,128)(2,1)S(1)}, u32[]{:S(2)}, u32[]{:S(2)}) %collective-permute-start.4) | collective-permute-done | bytes 131104 | tf_op jit(solution)/shard_map/ppermute | solution.py:176
  36.4 1.8 %collective-permute-start.16 = (bf16[4,2,4,32,128]{4,3,2,1,0:T(8,128)(2,1)S(1)}, bf16[4,2,4,32,128]{4,3,2,1,0:T(8,128)(2,1)S(1)}, u32[]{:S(2)}, u32[]{:S(2)}) collective-permute-start(bf16[4,2,4,32,128]{4,3,2,1,0:T(8,128)(2,1)S(1)} %collective-permute-done.11.refs_6_), channel_id=1, source_target_pairs={{0,16},{16,0},{1,17},{17,1},{2,18},{18,2},{3,19},{19,3},{4,20},{20... | collective-permute-start | bytes 786440 | tf_op jit(solution)/shard_map/ppermute | solution.py:185
  38.2 0.0 collective-permute-done.3.refs_1_
  38.2 0.0 collective-permute-start.15
  38.2 0.0 collective-permute-done.13.refs_8_
  38.2 0.5 collective-permute-start.18
  38.7 0.3 collective-permute-start.17
  39.0 0.0 collective-permute-done.14.refs_9_
  39.0 0.9 %collective-permute-done.18.refs_13_ = bf16[2,2,4,32,128]{4,3,2,1,0:T(8,128)(2,1)S(1)} collective-permute-done((bf16[2,2,4,32,128]{4,3,2,1,0:T(8,128)(2,1)S(1)}, bf16[2,2,4,32,128]{4,3,2,1,0:T(8,128)(2,1)S(1)}, u32[]{:S(2)}, u32[]{:S(2)}) %collective-permute-start.18) | collective-permute-done | bytes 131104 | tf_op jit(solution)/shard_map/ppermute | solution.py:185
  39.9 0.0 collective-permute-done.16.refs_11_
  39.9 0.2 collective-permute-done.17.refs_12_
  40.2 5.4 %shard_map.109 = bf16[16,4,32,128]{3,2,1,0:T(8,128)(2,1)S(1)} custom-call(bf16[4,4,32,128]{3,2,1,0:T(8,128)(2,1)S(1)} %pad_maximum_fusion.1.refs_0_, bf16[4,4,32,128]{3,2,1,0:T(8,128)(2,1)S(1)} %collective-permute-done.3.refs_1_, bf16[4,4,32,128]{3,2,1,0:T(8,128)(2,1)S(1)} %collective-permute-done.4.refs_2_, ...), custom_call_target="tpu_custom_call" | custom-call | tf_op jit(solution)/shard_map/pallas_call | solution.py:130
  45.6 21.5 %all_to_all.5 = bf16[16,4,32,128]{3,2,1,0:T(8,128)(2,1)S(1)} all-to-all(bf16[16,4,32,128]{3,2,1,0:T(8,128)(2,1)S(1)} %shard_map.109), channel_id=1, replica_groups=mesh['zh'=2,'y'=4,'c'=2,'zl'=4,'x'=4] {'zl','x'}, dimensions={0} | all-to-all | bytes 1048576 | tf_op jit(solution)/shard_map/all_to_all | solution.py:187
  67.1 0.4 reshape.11
  67.4 0.3 reduce_sum.9
  67.7 0.1 negate_bitcast_fusion
  67.8 0.9 %copy.12 = f32[4,4,4096]{2,1,0:T(4,128)} copy(f32[4,4,4096]{2,0,1:T(4,128)S(1)} %negate_bitcast_fusion) | data formatting | bytes 524288 | tf_op jit(solution)/shard_map/neg | solution.py:188
  (24 shorter events, 0.1 us)
Async XLA Ops:
  0.0 8.5 %copy-start.9 = (bf16[4,4,4096]{2,1,0:T(4,128)(2,1)S(1)}, bf16[4,4,4096]{2,1,0:T(4,128)(2,1)}, u32[]{:S(2)}) copy-start(bf16[4,4,4096]{2,1,0:T(4,128)(2,1)} %param.11) | copy-start | bytes 393220
  0.8 9.0 %collective-permute-start.6 = (bf16[4,32,128]{2,1,0:T(8,128)(2,1)S(1)}, bf16[4,32,128]{2,1,0:T(8,128)(2,1)S(1)}, u32[]{:S(2)}, u32[]{:S(2)}) collective-permute-start(bf16[4,32,128]{2,1,0:T(8,128)(2,1)S(1)} %bitcast.29), channel_id=1, source_target_pairs={{0,128},{128,0},{1,129},{129,1},{2,130},{130,2},{3,131},{131,3},{4... | collective-permute-start | bytes 98312 | tf_op jit(solution)/shard_map/ppermute | solution.py:171
  9.8 8.8 %collective-permute-start.8 = (bf16[2,4,32,128]{3,2,1,0:T(8,128)(2,1)S(1)}, bf16[2,4,32,128]{3,2,1,0:T(8,128)(2,1)S(1)}, u32[]{:S(2)}, u32[]{:S(2)}) collective-permute-start(bf16[2,4,32,128]{3,2,1,0:T(8,128)(2,1)S(1)} %get-tuple-element.10), channel_id=1, source_target_pairs={{0,2},{16,80},{1,3},{17,81},{2,0},{18,82},{3,1},{19,83},{32,34},{4... | collective-permute-start | bytes 196616 | tf_op jit(solution)/shard_map/ppermute | solution.py:179
  12.8 6.4 %collective-permute-start.7 = (bf16[2,4,32,128]{3,2,1,0:T(8,128)(2,1)S(1)}, bf16[2,4,32,128]{3,2,1,0:T(8,128)(2,1)S(1)}, u32[]{:S(2)}, u32[]{:S(2)}) collective-permute-start(bf16[2,4,32,128]{3,2,1,0:T(8,128)(2,1)S(1)} %get-tuple-element.10), channel_id=1, source_target_pairs={{0,1},{16,48},{1,2},{17,49},{2,3},{18,50},{3,0},{19,51},{32,33},{4... | collective-permute-start | bytes 196616 | tf_op jit(solution)/shard_map/ppermute | solution.py:179
  13.2 6.0 %collective-permute-start.9 = (bf16[2,4,32,128]{3,2,1,0:T(8,128)(2,1)S(1)}, bf16[2,4,32,128]{3,2,1,0:T(8,128)(2,1)S(1)}, u32[]{:S(2)}, u32[]{:S(2)}) collective-permute-start(bf16[2,4,32,128]{3,2,1,0:T(8,128)(2,1)S(1)} %get-tuple-element.10), channel_id=1, source_target_pairs={{0,3},{16,112},{1,0},{17,113},{2,1},{18,114},{3,2},{19,115},{32,35... | collective-permute-start | bytes 196616 | tf_op jit(solution)/shard_map/ppermute | solution.py:179
  15.5 5.9 %collective-permute-start.2 = (bf16[4,32,128]{2,1,0:T(8,128)(2,1)S(1)}, bf16[4,32,128]{2,1,0:T(8,128)(2,1)S(1)}, u32[]{:S(2)}, u32[]{:S(2)}) collective-permute-start(bf16[4,32,128]{2,1,0:T(8,128)(2,1)S(1)} %get-tuple-element.6), channel_id=1, source_target_pairs={{0,3},{1,0},{2,1},{3,2},{4,7},{5,4},{6,5},{7,6},{8,11},{9,8},{10,9... | collective-permute-start | bytes 98312 | tf_op jit(solution)/shard_map/ppermute | solution.py:174
  18.1 4.6 %collective-permute-start.1 = (bf16[4,32,128]{2,1,0:T(8,128)(2,1)S(1)}, bf16[4,32,128]{2,1,0:T(8,128)(2,1)S(1)}, u32[]{:S(2)}, u32[]{:S(2)}) collective-permute-start(bf16[4,32,128]{2,1,0:T(8,128)(2,1)S(1)} %get-tuple-element.7), channel_id=1, source_target_pairs={{0,2},{1,3},{2,0},{3,1},{4,6},{5,7},{6,4},{7,5},{8,10},{9,11},{10,... | collective-permute-start | bytes 98312 | tf_op jit(solution)/shard_map/ppermute | solution.py:174
  18.6 4.7 %collective-permute-start = (bf16[4,32,128]{2,1,0:T(8,128)(2,1)S(1)}, bf16[4,32,128]{2,1,0:T(8,128)(2,1)S(1)}, u32[]{:S(2)}, u32[]{:S(2)}) collective-permute-start(bf16[4,32,128]{2,1,0:T(8,128)(2,1)S(1)} %get-tuple-element.8), channel_id=1, source_target_pairs={{0,1},{1,2},{2,3},{3,0},{4,5},{5,6},{6,7},{7,4},{8,9},{9,10},{10,1... | collective-permute-start | bytes 98312 | tf_op jit(solution)/shard_map/ppermute | solution.py:174
  19.2 20.9 %copy-start.6 = (f32[64,128]{1,0:T(8,128)S(1)}, f32[64,128]{1,0:T(8,128)}, u32[]{:S(2)}) copy-start(f32[64,128]{1,0:T(8,128)} %constant.60.clone.refs_16_) | copy-start | bytes 98308
  19.2 20.9 %copy-start.7 = (f32[8]{0:T(128)S(1)}, f32[8]{0:T(128)}, u32[]{:S(2)}) copy-start(f32[8]{0:T(128)} %refs_14_.1) | copy-start | bytes 100
  19.2 20.9 %copy-start.8 = (f32[8]{0:T(128)S(1)}, f32[8]{0:T(128)}, u32[]{:S(2)}) copy-start(f32[8]{0:T(128)} %refs_15_.1) | copy-start | bytes 100
  19.3 7.7 %collective-permute-start.11 = (bf16[4,2,4,32,128]{4,3,2,1,0:T(8,128)(2,1)S(1)}, bf16[4,2,4,32,128]{4,3,2,1,0:T(8,128)(2,1)S(1)}, u32[]{:S(2)}, u32[]{:S(2)}) collective-permute-start(bf16[4,2,4,32,128]{4,3,2,1,0:T(8,128)(2,1)S(1)} %pad_maximum_fusion.refs_4_), channel_id=1, source_target_pairs={{0,96},{16,19},{1,97},{17,16},{2,98},{18,17},{3,99},{19,18},{32,0}... | collective-permute-start | bytes 786440 | tf_op jit(solution)/shard_map/ppermute | solution.py:181
  21.5 7.5 %collective-permute-start.10 = (bf16[4,2,4,32,128]{4,3,2,1,0:T(8,128)(2,1)S(1)}, bf16[4,2,4,32,128]{4,3,2,1,0:T(8,128)(2,1)S(1)}, u32[]{:S(2)}, u32[]{:S(2)}) collective-permute-start(bf16[4,2,4,32,128]{4,3,2,1,0:T(8,128)(2,1)S(1)} %pad_maximum_fusion.refs_4_), channel_id=1, source_target_pairs={{0,32},{16,17},{1,33},{17,18},{2,34},{18,19},{3,35},{19,16},{32,64... | collective-permute-start | bytes 786440 | tf_op jit(solution)/shard_map/ppermute | solution.py:181
  23.3 16.8 %copy-start.4 = (bf16[256,256]{1,0:T(8,128)(2,1)S(1)}, bf16[256,256]{1,0:T(8,128)(2,1)}, u32[]{:S(2)}) copy-start(bf16[256,256]{1,0:T(8,128)(2,1)} %constant.62.clone.refs_18_) | copy-start | bytes 393220
  23.3 16.8 %copy-start.5 = (bf16[256,256]{1,0:T(8,128)(2,1)S(1)}, bf16[256,256]{1,0:T(8,128)(2,1)}, u32[]{:S(2)}) copy-start(bf16[256,256]{1,0:T(8,128)(2,1)} %constant.61.clone.refs_17_) | copy-start | bytes 393220
  23.3 7.8 %collective-permute-start.5 = (bf16[4,4,32,128]{3,2,1,0:T(8,128)(2,1)S(1)}, bf16[4,4,32,128]{3,2,1,0:T(8,128)(2,1)S(1)}, u32[]{:S(2)}, u32[]{:S(2)}) collective-permute-start(bf16[4,4,32,128]{3,2,1,0:T(8,128)(2,1)S(1)} %pad_maximum_fusion.1.refs_0_), channel_id=1, source_target_pairs={{0,12},{4,8},{8,4},{12,0},{1,13},{5,9},{9,5},{13,1},{2,14},{6,10},... | collective-permute-start | bytes 393224 | tf_op jit(solution)/shard_map/ppermute | solution.py:176
  26.1 10.4 %collective-permute-start.4 = (bf16[4,4,32,128]{3,2,1,0:T(8,128)(2,1)S(1)}, bf16[4,4,32,128]{3,2,1,0:T(8,128)(2,1)S(1)}, u32[]{:S(2)}, u32[]{:S(2)}) collective-permute-start(bf16[4,4,32,128]{3,2,1,0:T(8,128)(2,1)S(1)} %pad_maximum_fusion.1.refs_0_), channel_id=1, source_target_pairs={{0,8},{4,12},{8,0},{12,4},{1,9},{5,13},{9,1},{13,5},{2,10},{6,14},... | collective-permute-start | bytes 393224 | tf_op jit(solution)/shard_map/ppermute | solution.py:176
  26.1 12.2 %collective-permute-start.3 = (bf16[4,4,32,128]{3,2,1,0:T(8,128)(2,1)S(1)}, bf16[4,4,32,128]{3,2,1,0:T(8,128)(2,1)S(1)}, u32[]{:S(2)}, u32[]{:S(2)}) collective-permute-start(bf16[4,4,32,128]{3,2,1,0:T(8,128)(2,1)S(1)} %pad_maximum_fusion.1.refs_0_), channel_id=1, source_target_pairs={{0,4},{4,0},{8,12},{12,8},{1,5},{5,1},{9,13},{13,9},{2,6},{6,2},{1... | collective-permute-start | bytes 393224 | tf_op jit(solution)/shard_map/ppermute | solution.py:176
  27.0 12.0 %collective-permute-start.14 = (bf16[4,2,4,32,128]{4,3,2,1,0:T(8,128)(2,1)S(1)}, bf16[4,2,4,32,128]{4,3,2,1,0:T(8,128)(2,1)S(1)}, u32[]{:S(2)}, u32[]{:S(2)}) collective-permute-start(bf16[4,2,4,32,128]{4,3,2,1,0:T(8,128)(2,1)S(1)} %pad_maximum_fusion.refs_4_), channel_id=1, source_target_pairs={{0,16},{16,0},{1,17},{17,1},{2,18},{18,2},{3,19},{19,3},{4,20},{20... | collective-permute-start | bytes 786440 | tf_op jit(solution)/shard_map/ppermute | solution.py:185
  28.9 11.2 %copy-start.2 = (bf16[256,256]{1,0:T(8,128)(2,1)S(1)}, bf16[256,256]{1,0:T(8,128)(2,1)}, u32[]{:S(2)}) copy-start(bf16[256,256]{1,0:T(8,128)(2,1)} %constant.64.clone.refs_20_) | copy-start | bytes 393220
  28.9 11.2 %copy-start.3 = (bf16[256,256]{1,0:T(8,128)(2,1)S(1)}, bf16[256,256]{1,0:T(8,128)(2,1)}, u32[]{:S(2)}) copy-start(bf16[256,256]{1,0:T(8,128)(2,1)} %constant.63.clone.refs_19_) | copy-start | bytes 393220
  29.0 11.2 %copy-start = (bf16[256,256]{1,0:T(8,128)(2,1)S(1)}, bf16[256,256]{1,0:T(8,128)(2,1)}, u32[]{:S(2)}) copy-start(bf16[256,256]{1,0:T(8,128)(2,1)} %constant.66.clone.refs_22_) | copy-start | bytes 393220
  29.0 11.2 %copy-start.1 = (bf16[256,256]{1,0:T(8,128)(2,1)S(1)}, bf16[256,256]{1,0:T(8,128)(2,1)}, u32[]{:S(2)}) copy-start(bf16[256,256]{1,0:T(8,128)(2,1)} %constant.65.clone.refs_21_) | copy-start | bytes 393220
  29.0 9.2 %collective-permute-start.13 = (bf16[2,2,4,32,128]{4,3,2,1,0:T(8,128)(2,1)S(1)}, bf16[2,2,4,32,128]{4,3,2,1,0:T(8,128)(2,1)S(1)}, u32[]{:S(2)}, u32[]{:S(2)}) collective-permute-start(bf16[2,2,4,32,128]{4,3,2,1,0:T(8,128)(2,1)S(1)} %slice.9), channel_id=1, source_target_pairs={{0,96},{16,19},{1,97},{17,16},{2,98},{18,17},{3,99},{19,18},{32,0}... | collective-permute-start | bytes 393224 | tf_op jit(solution)/shard_map/ppermute | solution.py:183
  31.2 7.6 %collective-permute-start.12 = (bf16[2,2,4,32,128]{4,3,2,1,0:T(8,128)(2,1)S(1)}, bf16[2,2,4,32,128]{4,3,2,1,0:T(8,128)(2,1)S(1)}, u32[]{:S(2)}, u32[]{:S(2)}) collective-permute-start(bf16[2,2,4,32,128]{4,3,2,1,0:T(8,128)(2,1)S(1)} %slice.8), channel_id=1, source_target_pairs={{0,32},{16,17},{1,33},{17,18},{2,34},{18,19},{3,35},{19,16},{32,64... | collective-permute-start | bytes 393224 | tf_op jit(solution)/shard_map/ppermute | solution.py:183
  36.4 3.5 %collective-permute-start.16 = (bf16[4,2,4,32,128]{4,3,2,1,0:T(8,128)(2,1)S(1)}, bf16[4,2,4,32,128]{4,3,2,1,0:T(8,128)(2,1)S(1)}, u32[]{:S(2)}, u32[]{:S(2)}) collective-permute-start(bf16[4,2,4,32,128]{4,3,2,1,0:T(8,128)(2,1)S(1)} %collective-permute-done.11.refs_6_), channel_id=1, source_target_pairs={{0,16},{16,0},{1,17},{17,1},{2,18},{18,2},{3,19},{19,3},{4,20},{20... | collective-permute-start | bytes 786440 | tf_op jit(solution)/shard_map/ppermute | solution.py:185
  38.2 1.9 %collective-permute-start.15 = (bf16[4,2,4,32,128]{4,3,2,1,0:T(8,128)(2,1)S(1)}, bf16[4,2,4,32,128]{4,3,2,1,0:T(8,128)(2,1)S(1)}, u32[]{:S(2)}, u32[]{:S(2)}) collective-permute-start(bf16[4,2,4,32,128]{4,3,2,1,0:T(8,128)(2,1)S(1)} %collective-permute-done.10.refs_5_), channel_id=1, source_target_pairs={{0,16},{16,0},{1,17},{17,1},{2,18},{18,2},{3,19},{19,3},{4,20},{20... | collective-permute-start | bytes 786440 | tf_op jit(solution)/shard_map/ppermute | solution.py:185
  38.2 1.7 %collective-permute-start.18 = (bf16[2,2,4,32,128]{4,3,2,1,0:T(8,128)(2,1)S(1)}, bf16[2,2,4,32,128]{4,3,2,1,0:T(8,128)(2,1)S(1)}, u32[]{:S(2)}, u32[]{:S(2)}) collective-permute-start(bf16[2,2,4,32,128]{4,3,2,1,0:T(8,128)(2,1)S(1)} %collective-permute-done.13.refs_8_), channel_id=1, source_target_pairs={{0,16},{16,0},{1,17},{17,1},{2,18},{18,2},{3,19},{19,3},{4,20},{20... | collective-permute-start | bytes 393224 | tf_op jit(solution)/shard_map/ppermute | solution.py:185
  38.7 1.4 %collective-permute-start.17 = (bf16[2,2,4,32,128]{4,3,2,1,0:T(8,128)(2,1)S(1)}, bf16[2,2,4,32,128]{4,3,2,1,0:T(8,128)(2,1)S(1)}, u32[]{:S(2)}, u32[]{:S(2)}) collective-permute-start(bf16[2,2,4,32,128]{4,3,2,1,0:T(8,128)(2,1)S(1)} %collective-permute-done.12.refs_7_), channel_id=1, source_target_pairs={{0,16},{16,0},{1,17},{17,1},{2,18},{18,2},{3,19},{19,3},{4,20},{20... | collective-permute-start | bytes 393224 | tf_op jit(solution)/shard_map/ppermute | solution.py:185

commit v5 on v3

--- a/solution.py
+++ b/solution.py
@@ -143,6 +143,29 @@
     )(*targets, *sources, exponents, coefficients, waves(), *basis_blocks())
 
 
+def gather_kernel(parts, out, rows):
+    for t in range(4):
+        total = parts[t].astype(F32)
+        for q in range(1, 4):
+            total = total + parts[4 * q + t].astype(F32)
+        rows[128 * t : 128 * t + 128] = -total.reshape(128, 128)
+    for p in range(4):
+        for r in range(32):
+            out[p, :, 128 * r : 128 * r + 128] = rows[pl.ds(32 * p + r, 4, stride=128)]
+
+
+def gathered(parts):
+    vmem = pl.BlockSpec(memory_space=pltpu.VMEM)
+    return pl.pallas_call(
+        gather_kernel,
+        out_shape=jax.ShapeDtypeStruct((4, 4, G * G), F32),
+        in_specs=[vmem],
+        out_specs=vmem,
+        scratch_shapes=[pltpu.VMEM((512, 128), F32)],
+        compiler_params=pltpu.CompilerParams(vmem_limit_bytes=8 << 20),
+    )(parts)
+
+
 def turn(n, by):
     return [(i, (i + by) % n) for i in range(n)]
 
@@ -181,8 +204,8 @@
     own_core = [block] + [second[l] for l in range(1, 4)]
     other_core = [lax.ppermute(own_core[l], "c", turn(2, 1)) for l in range(4)]
     part = pair_sums(lines, own_core + other_core, exponents, coefficients)
-    parts = lax.all_to_all(part, ("zl", "x"), 0, 0, tiled=True).reshape(4, 4, 4, G * G)
-    return -parts.astype(F32).sum(0).transpose(1, 0, 2)
+    parts = lax.all_to_all(part, ("zl", "x"), 0, 0, tiled=True)
+    return gathered(parts)
 
 
 def solution(mesh):

time: 68.4 us -> 67.7 us (0.990)
  local copies, waits for them, and re-layouts: 2.24 us -> 1.01 us
  Pallas kernels: 5.36 us -> 6.3 us
    pallas_call x0 -> x1, Pallas kernels: none -> 0.94 us  [gathered(): pl.pallas_call(gather_kernel, out_shape=jax.ShapeDtypeStruct((4, 4, G * G...]
    neg x1 -> x0, local copies, waits for them, and re-layouts: 0.87 us -> none  [exchange(): return -parts.astype(F32).sum(0).transpose(1, 0, 2)]
where the time goes in v5:
time: 67.7 us; the launch traced here: 66.4 us
  starting transfers between devices  29.1 us (43%)
  blocking collectives  19.5 us (29%)
  waiting for transfers between devices  10.2 us (15%)
  Pallas kernels  6.3 us (9%)
  local copies, waits for them, and re-layouts  1.01 us (1%)
    all_to_all x1, blocking collectives, exchange(): parts = lax.all_to_all(part, ('zl', 'x'), 0, 0, tiled=True)  19.5 us
    ppermute x3, waiting for transfers between devices, exchange(): lax.ppermute(target_block, 'zl', flip(4, k))  8.46 us
    ppermute x1, starting transfers between devices, exchange(): other = lax.ppermute(mine, 'zh', turn(2, 1))  7.73 us
    ppermute x3, starting transfers between devices, exchange(): first = {i: lax.ppermute(block, plane, weave(i, 0)) for i in SHIFTS}  5.68 us
    pallas_call x1, Pallas kernels, pair_sums(): pl.pallas_call(pair_kernel, out_shape=jax.ShapeDtypeStruct((16, 4, 32, 12...  5.36 us
    ppermute x4, starting transfers between devices, exchange(): other_core = [lax.ppermute(own_core[l], 'c', turn(2, 1)) for l in range(4)]  4.52 us
    ppermute x3, starting transfers between devices, exchange(): lax.ppermute(target_block, 'zl', flip(4, k))  4.13 us
    ppermute x3, starting transfers between devices, exchange(): rows = {j: lax.ppermute(pick(j), 'x', turn(4, j)) for j in SHIFTS}  3.68 us
  transfers between devices with their start and end apart: 17, of which 5 were waited for; matrix products, arithmetic and copies ran while one was open for 0% of the time, Pallas kernels for 0%

profile of v5, /device:TPU:1, one launch (start us, length us, event | category | flops | bytes accessed | tf_op | source)
XLA Modules:
  0.0 66.4 jit_solution(6023774842284077437)
XLA Ops:
  0.0 0.8 %copy.16 = bf16[1,4,32,128]{3,2,1,0:T(8,128)(2,1)S(1)} copy(bf16[1,4,32,128]{3,1,2,0:T(4,128)(2,1)} %bitcast.29) | data formatting | bytes 65536
  0.8 7.7 %collective-permute-start.6 = (bf16[4,32,128]{2,1,0:T(8,128)(2,1)S(1)}, bf16[4,32,128]{2,1,0:T(8,128)(2,1)S(1)}, u32[]{:S(2)}, u32[]{:S(2)}) collective-permute-start(bf16[4,32,128]{2,1,0:T(8,128)(2,1)S(1)} %bitcast.25), channel_id=1, source_target_pairs={{0,128},{128,0},{1,129},{129,1},{2,130},{130,2},{3,131},{131,3},{4... | collective-permute-start | bytes 98312 | tf_op jit(solution)/shard_map/ppermute | solution.py:193
  8.5 0.0 copy-done.9
  8.5 0.2 reshape.6
  8.7 1.1 %collective-permute-done.6 = bf16[4,32,128]{2,1,0:T(8,128)(2,1)S(1)} collective-permute-done((bf16[4,32,128]{2,1,0:T(8,128)(2,1)S(1)}, bf16[4,32,128]{2,1,0:T(8,128)(2,1)S(1)}, u32[]{:S(2)}, u32[]{:S(2)}) %collective-permute-start.6) | collective-permute-done | bytes 32800 | tf_op jit(solution)/shard_map/ppermute | solution.py:193
  9.8 3.0 %collective-permute-start.8 = (bf16[2,4,32,128]{3,2,1,0:T(8,128)(2,1)S(1)}, bf16[2,4,32,128]{3,2,1,0:T(8,128)(2,1)S(1)}, u32[]{:S(2)}, u32[]{:S(2)}) collective-permute-start(bf16[2,4,32,128]{3,2,1,0:T(8,128)(2,1)S(1)} %get-tuple-element.10), channel_id=1, source_target_pairs={{0,2},{16,80},{1,3},{17,81},{2,0},{18,82},{3,1},{19,83},{32,34},{4... | collective-permute-start | bytes 196616 | tf_op jit(solution)/shard_map/ppermute | solution.py:201
  12.8 0.4 collective-permute-start.7
  13.2 2.3 %collective-permute-start.9 = (bf16[2,4,32,128]{3,2,1,0:T(8,128)(2,1)S(1)}, bf16[2,4,32,128]{3,2,1,0:T(8,128)(2,1)S(1)}, u32[]{:S(2)}, u32[]{:S(2)}) collective-permute-start(bf16[2,4,32,128]{3,2,1,0:T(8,128)(2,1)S(1)} %get-tuple-element.10), channel_id=1, source_target_pairs={{0,3},{16,112},{1,0},{17,113},{2,1},{18,114},{3,2},{19,115},{32,35... | collective-permute-start | bytes 196616 | tf_op jit(solution)/shard_map/ppermute | solution.py:201
  15.5 2.6 %collective-permute-start.2 = (bf16[4,32,128]{2,1,0:T(8,128)(2,1)S(1)}, bf16[4,32,128]{2,1,0:T(8,128)(2,1)S(1)}, u32[]{:S(2)}, u32[]{:S(2)}) collective-permute-start(bf16[4,32,128]{2,1,0:T(8,128)(2,1)S(1)} %get-tuple-element.6), channel_id=1, source_target_pairs={{0,3},{1,0},{2,1},{3,2},{4,7},{5,4},{6,5},{7,6},{8,11},{9,8},{10,9... | collective-permute-start | bytes 98312 | tf_op jit(solution)/shard_map/ppermute | solution.py:196
  18.1 0.5 collective-permute-start.1
  18.6 0.0 collective-permute-done.8
  18.6 0.6 collective-permute-start
  19.2 0.0 collective-permute-done.7
  19.2 0.0 collective-permute-done.9
  19.2 0.0 copy-start.3
  19.3 0.0 copy-start.4
  19.3 0.0 copy-start.5
  19.3 0.0 copy-start.7
  19.3 0.0 copy-start.8
  19.3 2.1 %collective-permute-start.12 = (bf16[4,2,4,32,128]{4,3,2,1,0:T(8,128)(2,1)S(1)}, bf16[4,2,4,32,128]{4,3,2,1,0:T(8,128)(2,1)S(1)}, u32[]{:S(2)}, u32[]{:S(2)}) collective-permute-start(bf16[4,2,4,32,128]{4,3,2,1,0:T(8,128)(2,1)S(1)} %pad_maximum_fusion.refs_4_), channel_id=1, source_target_pairs={{0,96},{16,19},{1,97},{17,16},{2,98},{18,17},{3,99},{19,18},{32,0}... | collective-permute-start | bytes 786440 | tf_op jit(solution)/shard_map/ppermute | solution.py:203
  21.5 1.2 %collective-permute-start.11 = (bf16[4,2,4,32,128]{4,3,2,1,0:T(8,128)(2,1)S(1)}, bf16[4,2,4,32,128]{4,3,2,1,0:T(8,128)(2,1)S(1)}, u32[]{:S(2)}, u32[]{:S(2)}) collective-permute-start(bf16[4,2,4,32,128]{4,3,2,1,0:T(8,128)(2,1)S(1)} %pad_maximum_fusion.refs_4_), channel_id=1, source_target_pairs={{0,64},{16,18},{1,65},{17,19},{2,66},{18,16},{3,67},{19,17},{32,96... | collective-permute-start | bytes 786440 | tf_op jit(solution)/shard_map/ppermute | solution.py:203
  22.7 0.0 collective-permute-done.2
  22.7 0.0 collective-permute-start.10
  22.7 0.0 collective-permute-done.1
  22.7 0.6 collective-permute-done
  23.3 2.7 %collective-permute-start.5 = (bf16[4,4,32,128]{3,2,1,0:T(8,128)(2,1)S(1)}, bf16[4,4,32,128]{3,2,1,0:T(8,128)(2,1)S(1)}, u32[]{:S(2)}, u32[]{:S(2)}) collective-permute-start(bf16[4,4,32,128]{3,2,1,0:T(8,128)(2,1)S(1)} %pad_maximum_fusion.1.refs_0_), channel_id=1, source_target_pairs={{0,12},{4,8},{8,4},{12,0},{1,13},{5,9},{9,5},{13,1},{2,14},{6,10},... | collective-permute-start | bytes 393224 | tf_op jit(solution)/shard_map/ppermute | solution.py:198
  26.1 0.0 collective-permute-start.4
  26.1 3.3 %collective-permute-done.5.refs_3_ = bf16[4,4,32,128]{3,2,1,0:T(8,128)(2,1)S(1)} collective-permute-done((bf16[4,4,32,128]{3,2,1,0:T(8,128)(2,1)S(1)}, bf16[4,4,32,128]{3,2,1,0:T(8,128)(2,1)S(1)}, u32[]{:S(2)}, u32[]{:S(2)}) %collective-permute-start.5) | collective-permute-done | bytes 131104 | tf_op jit(solution)/shard_map/ppermute | solution.py:198
  29.3 3.3 %collective-permute-start.13 = (bf16[4,2,4,32,128]{4,3,2,1,0:T(8,128)(2,1)S(1)}, bf16[4,2,4,32,128]{4,3,2,1,0:T(8,128)(2,1)S(1)}, u32[]{:S(2)}, u32[]{:S(2)}) collective-permute-start(bf16[4,2,4,32,128]{4,3,2,1,0:T(8,128)(2,1)S(1)} %pad_maximum_fusion.refs_4_), channel_id=1, source_target_pairs={{0,16},{16,0},{1,17},{17,1},{2,18},{18,2},{3,19},{19,3},{4,20},{20... | collective-permute-start | bytes 786440 | tf_op jit(solution)/shard_map/ppermute | solution.py:205
  32.6 0.0 collective-permute-done.12.refs_7_
  32.6 0.0 collective-permute-start.16
  32.6 0.0 collective-permute-done.11.refs_6_
  32.6 0.5 collective-permute-start.15
  33.2 0.0 collective-permute-done.10.refs_5_
  33.2 0.7 %collective-permute-start.14 = (bf16[4,2,4,32,128]{4,3,2,1,0:T(8,128)(2,1)S(1)}, bf16[4,2,4,32,128]{4,3,2,1,0:T(8,128)(2,1)S(1)}, u32[]{:S(2)}, u32[]{:S(2)}) collective-permute-start(bf16[4,2,4,32,128]{4,3,2,1,0:T(8,128)(2,1)S(1)} %collective-permute-done.10.refs_5_), channel_id=1, source_target_pairs={{0,16},{16,0},{1,17},{17,1},{2,18},{18,2},{3,19},{19,3},{4,20},{20... | collective-permute-start | bytes 786440 | tf_op jit(solution)/shard_map/ppermute | solution.py:205
  33.9 2.6 %collective-permute-done.4.refs_2_ = bf16[4,4,32,128]{3,2,1,0:T(8,128)(2,1)S(1)} collective-permute-done((bf16[4,4,32,128]{3,2,1,0:T(8,128)(2,1)S(1)}, bf16[4,4,32,128]{3,2,1,0:T(8,128)(2,1)S(1)}, u32[]{:S(2)}, u32[]{:S(2)}) %collective-permute-start.4) | collective-permute-done | bytes 131104 | tf_op jit(solution)/shard_map/ppermute | solution.py:198
  36.4 1.4 %collective-permute-start.3 = (bf16[4,4,32,128]{3,2,1,0:T(8,128)(2,1)S(1)}, bf16[4,4,32,128]{3,2,1,0:T(8,128)(2,1)S(1)}, u32[]{:S(2)}, u32[]{:S(2)}) collective-permute-start(bf16[4,4,32,128]{3,2,1,0:T(8,128)(2,1)S(1)} %pad_maximum_fusion.1.refs_0_), channel_id=1, source_target_pairs={{0,4},{4,0},{8,12},{12,8},{1,5},{5,1},{9,13},{13,9},{2,6},{6,2},{1... | collective-permute-start | bytes 393224 | tf_op jit(solution)/shard_map/ppermute | solution.py:198
  37.9 2.6 %collective-permute-done.3.refs_1_ = bf16[4,4,32,128]{3,2,1,0:T(8,128)(2,1)S(1)} collective-permute-done((bf16[4,4,32,128]{3,2,1,0:T(8,128)(2,1)S(1)}, bf16[4,4,32,128]{3,2,1,0:T(8,128)(2,1)S(1)}, u32[]{:S(2)}, u32[]{:S(2)}) %collective-permute-start.3) | collective-permute-done | bytes 131104 | tf_op jit(solution)/shard_map/ppermute | solution.py:198
  40.5 0.0 collective-permute-done.13.refs_8_
  40.5 0.0 collective-permute-done.16.refs_11_
  40.5 0.0 collective-permute-done.15.refs_10_
  40.5 0.0 collective-permute-done.14.refs_9_
  40.5 0.0 copy-done.6
  40.5 0.0 copy-done.2
  40.5 0.0 copy-done.3
  40.6 5.4 %shard_map.109 = bf16[16,4,32,128]{3,2,1,0:T(8,128)(2,1)S(1)} custom-call(bf16[4,4,32,128]{3,2,1,0:T(8,128)(2,1)S(1)} %pad_maximum_fusion.1.refs_0_, bf16[4,4,32,128]{3,2,1,0:T(8,128)(2,1)S(1)} %collective-permute-done.3.refs_1_, bf16[4,4,32,128]{3,2,1,0:T(8,128)(2,1)S(1)} %collective-permute-done.4.refs_2_, ...), custom_call_target="tpu_custom_call" | custom-call | tf_op jit(solution)/shard_map/pallas_call | solution.py:129
  45.9 19.5 %all_to_all.5.parts = bf16[16,4,32,128]{3,2,1,0:T(8,128)(2,1)S(1)} all-to-all(bf16[16,4,32,128]{3,2,1,0:T(8,128)(2,1)S(1)} %shard_map.109), channel_id=1, replica_groups=mesh['zh'=2,'y'=4,'c'=2,'zl'=4,'x'=4] {'zl','x'}, dimensions={0} | all-to-all | bytes 1048576 | tf_op jit(solution)/shard_map/all_to_all | solution.py:207
  65.4 0.9 %shard_map.110 = f32[4,4,4096]{2,1,0:T(4,128)} custom-call(bf16[16,4,32,128]{3,2,1,0:T(8,128)(2,1)S(1)} %all_to_all.5.parts), custom_call_target="tpu_custom_call" | custom-call | tf_op jit(solution)/shard_map/pallas_call | solution.py:159
  (15 shorter events, 0.1 us)
Async XLA Ops:
  0.0 8.5 %copy-start.9 = (bf16[4,4,4096]{2,1,0:T(4,128)(2,1)S(1)}, bf16[4,4,4096]{2,1,0:T(4,128)(2,1)}, u32[]{:S(2)}) copy-start(bf16[4,4,4096]{2,1,0:T(4,128)(2,1)} %param.11) | copy-start | bytes 393220
  0.8 9.0 %collective-permute-start.6 = (bf16[4,32,128]{2,1,0:T(8,128)(2,1)S(1)}, bf16[4,32,128]{2,1,0:T(8,128)(2,1)S(1)}, u32[]{:S(2)}, u32[]{:S(2)}) collective-permute-start(bf16[4,32,128]{2,1,0:T(8,128)(2,1)S(1)} %bitcast.25), channel_id=1, source_target_pairs={{0,128},{128,0},{1,129},{129,1},{2,130},{130,2},{3,131},{131,3},{4... | collective-permute-start | bytes 98312 | tf_op jit(solution)/shard_map/ppermute | solution.py:193
  9.8 8.8 %collective-permute-start.8 = (bf16[2,4,32,128]{3,2,1,0:T(8,128)(2,1)S(1)}, bf16[2,4,32,128]{3,2,1,0:T(8,128)(2,1)S(1)}, u32[]{:S(2)}, u32[]{:S(2)}) collective-permute-start(bf16[2,4,32,128]{3,2,1,0:T(8,128)(2,1)S(1)} %get-tuple-element.10), channel_id=1, source_target_pairs={{0,2},{16,80},{1,3},{17,81},{2,0},{18,82},{3,1},{19,83},{32,34},{4... | collective-permute-start | bytes 196616 | tf_op jit(solution)/shard_map/ppermute | solution.py:201
  12.8 6.4 %collective-permute-start.7 = (bf16[2,4,32,128]{3,2,1,0:T(8,128)(2,1)S(1)}, bf16[2,4,32,128]{3,2,1,0:T(8,128)(2,1)S(1)}, u32[]{:S(2)}, u32[]{:S(2)}) collective-permute-start(bf16[2,4,32,128]{3,2,1,0:T(8,128)(2,1)S(1)} %get-tuple-element.10), channel_id=1, source_target_pairs={{0,1},{16,48},{1,2},{17,49},{2,3},{18,50},{3,0},{19,51},{32,33},{4... | collective-permute-start | bytes 196616 | tf_op jit(solution)/shard_map/ppermute | solution.py:201
  13.2 6.0 %collective-permute-start.9 = (bf16[2,4,32,128]{3,2,1,0:T(8,128)(2,1)S(1)}, bf16[2,4,32,128]{3,2,1,0:T(8,128)(2,1)S(1)}, u32[]{:S(2)}, u32[]{:S(2)}) collective-permute-start(bf16[2,4,32,128]{3,2,1,0:T(8,128)(2,1)S(1)} %get-tuple-element.10), channel_id=1, source_target_pairs={{0,3},{16,112},{1,0},{17,113},{2,1},{18,114},{3,2},{19,115},{32,35... | collective-permute-start | bytes 196616 | tf_op jit(solution)/shard_map/ppermute | solution.py:201
  15.5 25.0 %copy-start.6 = (f32[64,128]{1,0:T(8,128)S(1)}, f32[64,128]{1,0:T(8,128)}, u32[]{:S(2)}) copy-start(f32[64,128]{1,0:T(8,128)} %constant.58.clone.refs_14_) | copy-start | bytes 98308
  15.5 7.2 %collective-permute-start.2 = (bf16[4,32,128]{2,1,0:T(8,128)(2,1)S(1)}, bf16[4,32,128]{2,1,0:T(8,128)(2,1)S(1)}, u32[]{:S(2)}, u32[]{:S(2)}) collective-permute-start(bf16[4,32,128]{2,1,0:T(8,128)(2,1)S(1)} %get-tuple-element.6), channel_id=1, source_target_pairs={{0,3},{1,0},{2,1},{3,2},{4,7},{5,4},{6,5},{7,6},{8,11},{9,8},{10,9... | collective-permute-start | bytes 98312 | tf_op jit(solution)/shard_map/ppermute | solution.py:196
  18.1 4.6 %collective-permute-start.1 = (bf16[4,32,128]{2,1,0:T(8,128)(2,1)S(1)}, bf16[4,32,128]{2,1,0:T(8,128)(2,1)S(1)}, u32[]{:S(2)}, u32[]{:S(2)}) collective-permute-start(bf16[4,32,128]{2,1,0:T(8,128)(2,1)S(1)} %get-tuple-element.7), channel_id=1, source_target_pairs={{0,2},{1,3},{2,0},{3,1},{4,6},{5,7},{6,4},{7,5},{8,10},{9,11},{10,... | collective-permute-start | bytes 98312 | tf_op jit(solution)/shard_map/ppermute | solution.py:196
  18.6 4.7 %collective-permute-start = (bf16[4,32,128]{2,1,0:T(8,128)(2,1)S(1)}, bf16[4,32,128]{2,1,0:T(8,128)(2,1)S(1)}, u32[]{:S(2)}, u32[]{:S(2)}) collective-permute-start(bf16[4,32,128]{2,1,0:T(8,128)(2,1)S(1)} %get-tuple-element.8), channel_id=1, source_target_pairs={{0,1},{1,2},{2,3},{3,0},{4,5},{5,6},{6,7},{7,4},{8,9},{9,10},{10,1... | collective-permute-start | bytes 98312 | tf_op jit(solution)/shard_map/ppermute | solution.py:196
  19.2 21.3 %copy-start.2 = (bf16[256,256]{1,0:T(8,128)(2,1)S(1)}, bf16[256,256]{1,0:T(8,128)(2,1)}, u32[]{:S(2)}) copy-start(bf16[256,256]{1,0:T(8,128)(2,1)} %constant.62.clone.refs_18_) | copy-start | bytes 393220
  19.2 21.3 %copy-start.3 = (bf16[256,256]{1,0:T(8,128)(2,1)S(1)}, bf16[256,256]{1,0:T(8,128)(2,1)}, u32[]{:S(2)}) copy-start(bf16[256,256]{1,0:T(8,128)(2,1)} %constant.61.clone.refs_17_) | copy-start | bytes 393220
  19.3 21.3 %copy-start.4 = (bf16[256,256]{1,0:T(8,128)(2,1)S(1)}, bf16[256,256]{1,0:T(8,128)(2,1)}, u32[]{:S(2)}) copy-start(bf16[256,256]{1,0:T(8,128)(2,1)} %constant.60.clone.refs_16_) | copy-start | bytes 393220
  19.3 21.3 %copy-start.5 = (bf16[256,256]{1,0:T(8,128)(2,1)S(1)}, bf16[256,256]{1,0:T(8,128)(2,1)}, u32[]{:S(2)}) copy-start(bf16[256,256]{1,0:T(8,128)(2,1)} %constant.59.clone.refs_15_) | copy-start | bytes 393220
  19.3 21.3 %copy-start.7 = (f32[8]{0:T(128)S(1)}, f32[8]{0:T(128)}, u32[]{:S(2)}) copy-start(f32[8]{0:T(128)} %refs_12_.1) | copy-start | bytes 100
  19.3 21.3 %copy-start.8 = (f32[8]{0:T(128)S(1)}, f32[8]{0:T(128)}, u32[]{:S(2)}) copy-start(f32[8]{0:T(128)} %refs_13_.1) | copy-start | bytes 100
  19.3 13.3 %collective-permute-start.12 = (bf16[4,2,4,32,128]{4,3,2,1,0:T(8,128)(2,1)S(1)}, bf16[4,2,4,32,128]{4,3,2,1,0:T(8,128)(2,1)S(1)}, u32[]{:S(2)}, u32[]{:S(2)}) collective-permute-start(bf16[4,2,4,32,128]{4,3,2,1,0:T(8,128)(2,1)S(1)} %pad_maximum_fusion.refs_4_), channel_id=1, source_target_pairs={{0,96},{16,19},{1,97},{17,16},{2,98},{18,17},{3,99},{19,18},{32,0}... | collective-permute-start | bytes 786440 | tf_op jit(solution)/shard_map/ppermute | solution.py:203
  21.5 11.2 %collective-permute-start.11 = (bf16[4,2,4,32,128]{4,3,2,1,0:T(8,128)(2,1)S(1)}, bf16[4,2,4,32,128]{4,3,2,1,0:T(8,128)(2,1)S(1)}, u32[]{:S(2)}, u32[]{:S(2)}) collective-permute-start(bf16[4,2,4,32,128]{4,3,2,1,0:T(8,128)(2,1)S(1)} %pad_maximum_fusion.refs_4_), channel_id=1, source_target_pairs={{0,64},{16,18},{1,65},{17,19},{2,66},{18,16},{3,67},{19,17},{32,96... | collective-permute-start | bytes 786440 | tf_op jit(solution)/shard_map/ppermute | solution.py:203
  22.7 10.4 %collective-permute-start.10 = (bf16[4,2,4,32,128]{4,3,2,1,0:T(8,128)(2,1)S(1)}, bf16[4,2,4,32,128]{4,3,2,1,0:T(8,128)(2,1)S(1)}, u32[]{:S(2)}, u32[]{:S(2)}) collective-permute-start(bf16[4,2,4,32,128]{4,3,2,1,0:T(8,128)(2,1)S(1)} %pad_maximum_fusion.refs_4_), channel_id=1, source_target_pairs={{0,32},{16,17},{1,33},{17,18},{2,34},{18,19},{3,35},{19,16},{32,64... | collective-permute-start | bytes 786440 | tf_op jit(solution)/shard_map/ppermute | solution.py:203
  23.3 17.3 %copy-start = (bf16[256,256]{1,0:T(8,128)(2,1)S(1)}, bf16[256,256]{1,0:T(8,128)(2,1)}, u32[]{:S(2)}) copy-start(bf16[256,256]{1,0:T(8,128)(2,1)} %constant.64.clone.refs_20_) | copy-start | bytes 393220
  23.3 17.3 %copy-start.1 = (bf16[256,256]{1,0:T(8,128)(2,1)S(1)}, bf16[256,256]{1,0:T(8,128)(2,1)}, u32[]{:S(2)}) copy-start(bf16[256,256]{1,0:T(8,128)(2,1)} %constant.63.clone.refs_19_) | copy-start | bytes 393220
  23.3 6.0 %collective-permute-start.5 = (bf16[4,4,32,128]{3,2,1,0:T(8,128)(2,1)S(1)}, bf16[4,4,32,128]{3,2,1,0:T(8,128)(2,1)S(1)}, u32[]{:S(2)}, u32[]{:S(2)}) collective-permute-start(bf16[4,4,32,128]{3,2,1,0:T(8,128)(2,1)S(1)} %pad_maximum_fusion.1.refs_0_), channel_id=1, source_target_pairs={{0,12},{4,8},{8,4},{12,0},{1,13},{5,9},{9,5},{13,1},{2,14},{6,10},... | collective-permute-start | bytes 393224 | tf_op jit(solution)/shard_map/ppermute | solution.py:198
  26.1 10.4 %collective-permute-start.4 = (bf16[4,4,32,128]{3,2,1,0:T(8,128)(2,1)S(1)}, bf16[4,4,32,128]{3,2,1,0:T(8,128)(2,1)S(1)}, u32[]{:S(2)}, u32[]{:S(2)}) collective-permute-start(bf16[4,4,32,128]{3,2,1,0:T(8,128)(2,1)S(1)} %pad_maximum_fusion.1.refs_0_), channel_id=1, source_target_pairs={{0,8},{4,12},{8,0},{12,4},{1,9},{5,13},{9,1},{13,5},{2,10},{6,14},... | collective-permute-start | bytes 393224 | tf_op jit(solution)/shard_map/ppermute | solution.py:198
  29.3 11.1 %collective-permute-start.13 = (bf16[4,2,4,32,128]{4,3,2,1,0:T(8,128)(2,1)S(1)}, bf16[4,2,4,32,128]{4,3,2,1,0:T(8,128)(2,1)S(1)}, u32[]{:S(2)}, u32[]{:S(2)}) collective-permute-start(bf16[4,2,4,32,128]{4,3,2,1,0:T(8,128)(2,1)S(1)} %pad_maximum_fusion.refs_4_), channel_id=1, source_target_pairs={{0,16},{16,0},{1,17},{17,1},{2,18},{18,2},{3,19},{19,3},{4,20},{20... | collective-permute-start | bytes 786440 | tf_op jit(solution)/shard_map/ppermute | solution.py:205
  32.6 7.8 %collective-permute-start.16 = (bf16[4,2,4,32,128]{4,3,2,1,0:T(8,128)(2,1)S(1)}, bf16[4,2,4,32,128]{4,3,2,1,0:T(8,128)(2,1)S(1)}, u32[]{:S(2)}, u32[]{:S(2)}) collective-permute-start(bf16[4,2,4,32,128]{4,3,2,1,0:T(8,128)(2,1)S(1)} %collective-permute-done.12.refs_7_), channel_id=1, source_target_pairs={{0,16},{16,0},{1,17},{17,1},{2,18},{18,2},{3,19},{19,3},{4,20},{20... | collective-permute-start | bytes 786440 | tf_op jit(solution)/shard_map/ppermute | solution.py:205
  32.6 7.8 %collective-permute-start.15 = (bf16[4,2,4,32,128]{4,3,2,1,0:T(8,128)(2,1)S(1)}, bf16[4,2,4,32,128]{4,3,2,1,0:T(8,128)(2,1)S(1)}, u32[]{:S(2)}, u32[]{:S(2)}) collective-permute-start(bf16[4,2,4,32,128]{4,3,2,1,0:T(8,128)(2,1)S(1)} %collective-permute-done.11.refs_6_), channel_id=1, source_target_pairs={{0,16},{16,0},{1,17},{17,1},{2,18},{18,2},{3,19},{19,3},{4,20},{20... | collective-permute-start | bytes 786440 | tf_op jit(solution)/shard_map/ppermute | solution.py:205
  33.2 7.3 %collective-permute-start.14 = (bf16[4,2,4,32,128]{4,3,2,1,0:T(8,128)(2,1)S(1)}, bf16[4,2,4,32,128]{4,3,2,1,0:T(8,128)(2,1)S(1)}, u32[]{:S(2)}, u32[]{:S(2)}) collective-permute-start(bf16[4,2,4,32,128]{4,3,2,1,0:T(8,128)(2,1)S(1)} %collective-permute-done.10.refs_5_), channel_id=1, source_target_pairs={{0,16},{16,0},{1,17},{17,1},{2,18},{18,2},{3,19},{19,3},{4,20},{20... | collective-permute-start | bytes 786440 | tf_op jit(solution)/shard_map/ppermute | solution.py:205
  36.4 4.0 %collective-permute-start.3 = (bf16[4,4,32,128]{3,2,1,0:T(8,128)(2,1)S(1)}, bf16[4,4,32,128]{3,2,1,0:T(8,128)(2,1)S(1)}, u32[]{:S(2)}, u32[]{:S(2)}) collective-permute-start(bf16[4,4,32,128]{3,2,1,0:T(8,128)(2,1)S(1)} %pad_maximum_fusion.1.refs_0_), channel_id=1, source_target_pairs={{0,4},{4,0},{8,12},{12,8},{1,5},{5,1},{9,13},{13,9},{2,6},{6,2},{1... | collective-permute-start | bytes 393224 | tf_op jit(solution)/shard_map/ppermute | solution.py:198

commit v6 on v5

--- a/solution.py
+++ b/solution.py
@@ -30,7 +30,8 @@
     z_in = np.kron(four, rows.T)
     y_in = np.einsum("ky,ab->kbay", rows[:, parity], four).reshape(256, 256)
     x_in = np.einsum("kbx,ij->ikbjx", rows.reshape(G, 16, 4), four).reshape(256, 256)
-    return [jnp.asarray(m, BF16) for m in (z_in, y_in, x_in, x_in.T, y_in.T, z_in.T)]
+    twice = lambda m, axis: np.concatenate([m, m], axis=axis)
+    return [jnp.asarray(m, BF16) for m in (z_in, twice(y_in, 1), x_in, twice(x_in.T, 1), y_in.T, twice(z_in.T, 0))]
 
 
 def waves():
@@ -77,6 +78,18 @@
     def swap(a):
         return pltpu.roll(a, 64, 2)
 
+    def by_fours(step):
+        def four(group, carry):
+            for n in range(4):
+                step(4 * group + n)
+            return carry
+
+        lax.fori_loop(0, 4, four, 0)
+
+    def parts(a, axis):
+        high = a.astype(BF16)
+        return jnp.concatenate([high, (a - high.astype(F32)).astype(BF16)], axis=axis)
+
     def dot(a, b):
         return jnp.dot(a, b, preferred_element_type=F32)
 
@@ -94,7 +107,7 @@
                     b = lax.rem(zh + m, 2) * 8 + lax.rem(y - by_y + 4, 4) * 2 + core
                     s_all[by_x, b] = s_in[4 * e + l][i, m]
 
-    for b in range(16):
+    def enter(b):
         target = t_all[b]
         turned = swap(target)
         target = jnp.concatenate([jnp.where(lane, target, turned), jnp.where(lane, turned, target)], axis=1)
@@ -106,22 +119,26 @@
             source = source.reshape(256, 128)
             s_rows[b, :, 128 * h : 128 * h + 128] = source
             dense.append(target * source)
-        along_z = dot(jnp.concatenate(dense, axis=1), z_in[...]).astype(BF16)
-        field[b] = dot(y_in[...], along_z).astype(BF16)
+        along_z = dot(jnp.concatenate(dense, axis=1), z_in[...])
+        field[b] = dot(y_in[...], parts(along_z, 0)).astype(BF16)
+
+    by_fours(enter)
 
     for k in range(16):
         rows = slice(16 * k, 16 * k + 16)
         waves = dot(x_in[...], field[:, rows, :].reshape(256, 256))
         factor = d_ref[4 * k : 4 * k + 4].reshape(256, 128)
-        waves = (waves * jnp.concatenate([factor, factor], axis=1)).astype(BF16)
+        waves = parts(waves * jnp.concatenate([factor, factor], axis=1), 0)
         field[:, rows, :] = dot(x_out[...], waves).astype(BF16).reshape(16, 16, 256)
 
-    for b in range(16):
-        along_y = dot(y_out[...], field[b]).astype(BF16)
+    def leave(b):
+        along_y = parts(dot(y_out[...], field[b]), 1)
         terms = dot(along_y, z_out[...]) * s_rows[b].astype(F32)
         terms = (terms[:, :128] + terms[:, 128:]).reshape(4, G, 128)
         terms = terms + swap(terms)
         out[b] = jnp.where(lane, terms[:, :32], terms[:, 32:]).astype(out.dtype)
+
+    by_fours(leave)
 
 
 def pair_sums(targets, sources, exponents, coefficients):

time: 67.7 us -> 73.6 us (1.087)
  Pallas kernels: 6.3 us -> 12.2 us
    pallas_call x1, Pallas kernels: 5.36 us -> 11.3 us  [pair_sums(): pl.pallas_call(pair_kernel, out_shape=jax.ShapeDtypeStruct((16, 4, 32, 12...]
where the time goes in v6:
time: 73.6 us; the launch traced here: 72.3 us
  starting transfers between devices  29.1 us (40%)
  blocking collectives  19.5 us (26%)
  Pallas kernels  12.2 us (17%)
  waiting for transfers between devices  10.3 us (14%)
  local copies, waits for them, and re-layouts  1.01 us (1%)
    all_to_all x1, blocking collectives, exchange(): parts = lax.all_to_all(part, ('zl', 'x'), 0, 0, tiled=True)  19.5 us
    pallas_call x1, Pallas kernels, pair_sums(): pl.pallas_call(pair_kernel, out_shape=jax.ShapeDtypeStruct((16, 4, 32, 12...  11.3 us
    ppermute x3, waiting for transfers between devices, exchange(): lax.ppermute(target_block, 'zl', flip(4, k))  8.52 us
    ppermute x1, starting transfers between devices, exchange(): other = lax.ppermute(mine, 'zh', turn(2, 1))  7.73 us
    ppermute x3, starting transfers between devices, exchange(): first = {i: lax.ppermute(block, plane, weave(i, 0)) for i in SHIFTS}  5.68 us
    ppermute x4, starting transfers between devices, exchange(): other_core = [lax.ppermute(own_core[l], 'c', turn(2, 1)) for l in range(4)]  4.47 us
    ppermute x3, starting transfers between devices, exchange(): lax.ppermute(target_block, 'zl', flip(4, k))  4.12 us
    ppermute x3, starting transfers between devices, exchange(): rows = {j: lax.ppermute(pick(j), 'x', turn(4, j)) for j in SHIFTS}  3.68 us
  transfers between devices with their start and end apart: 17, of which 5 were waited for; matrix products, arithmetic and copies ran while one was open for 0% of the time, Pallas kernels for 0%

profile of v6, /device:TPU:1, one launch (start us, length us, event | category | flops | bytes accessed | tf_op | source)
XLA Modules:
  0.0 72.3 jit_solution(12241244604497010879)
XLA Ops:
  0.0 0.8 %copy.16 = bf16[1,4,32,128]{3,2,1,0:T(8,128)(2,1)S(1)} copy(bf16[1,4,32,128]{3,1,2,0:T(4,128)(2,1)} %bitcast.29) | data formatting | bytes 65536
  0.8 7.7 %collective-permute-start.6 = (bf16[4,32,128]{2,1,0:T(8,128)(2,1)S(1)}, bf16[4,32,128]{2,1,0:T(8,128)(2,1)S(1)}, u32[]{:S(2)}, u32[]{:S(2)}) collective-permute-start(bf16[4,32,128]{2,1,0:T(8,128)(2,1)S(1)} %bitcast.25), channel_id=1, source_target_pairs={{0,128},{128,0},{1,129},{129,1},{2,130},{130,2},{3,131},{131,3},{4... | collective-permute-start | bytes 98312 | tf_op jit(solution)/shard_map/ppermute | solution.py:210
  8.5 0.0 copy-done.9
  8.5 0.2 reshape.6
  8.7 1.1 %collective-permute-done.6 = bf16[4,32,128]{2,1,0:T(8,128)(2,1)S(1)} collective-permute-done((bf16[4,32,128]{2,1,0:T(8,128)(2,1)S(1)}, bf16[4,32,128]{2,1,0:T(8,128)(2,1)S(1)}, u32[]{:S(2)}, u32[]{:S(2)}) %collective-permute-start.6) | collective-permute-done | bytes 32800 | tf_op jit(solution)/shard_map/ppermute | solution.py:210
  9.9 3.0 %collective-permute-start.8 = (bf16[2,4,32,128]{3,2,1,0:T(8,128)(2,1)S(1)}, bf16[2,4,32,128]{3,2,1,0:T(8,128)(2,1)S(1)}, u32[]{:S(2)}, u32[]{:S(2)}) collective-permute-start(bf16[2,4,32,128]{3,2,1,0:T(8,128)(2,1)S(1)} %get-tuple-element.10), channel_id=1, source_target_pairs={{0,2},{16,80},{1,3},{17,81},{2,0},{18,82},{3,1},{19,83},{32,34},{4... | collective-permute-start | bytes 196616 | tf_op jit(solution)/shard_map/ppermute | solution.py:218
  12.9 0.4 collective-permute-start.7
  13.2 2.3 %collective-permute-start.9 = (bf16[2,4,32,128]{3,2,1,0:T(8,128)(2,1)S(1)}, bf16[2,4,32,128]{3,2,1,0:T(8,128)(2,1)S(1)}, u32[]{:S(2)}, u32[]{:S(2)}) collective-permute-start(bf16[2,4,32,128]{3,2,1,0:T(8,128)(2,1)S(1)} %get-tuple-element.10), channel_id=1, source_target_pairs={{0,3},{16,112},{1,0},{17,113},{2,1},{18,114},{3,2},{19,115},{32,35... | collective-permute-start | bytes 196616 | tf_op jit(solution)/shard_map/ppermute | solution.py:218
  15.5 2.6 %collective-permute-start.2 = (bf16[4,32,128]{2,1,0:T(8,128)(2,1)S(1)}, bf16[4,32,128]{2,1,0:T(8,128)(2,1)S(1)}, u32[]{:S(2)}, u32[]{:S(2)}) collective-permute-start(bf16[4,32,128]{2,1,0:T(8,128)(2,1)S(1)} %get-tuple-element.6), channel_id=1, source_target_pairs={{0,3},{1,0},{2,1},{3,2},{4,7},{5,4},{6,5},{7,6},{8,11},{9,8},{10,9... | collective-permute-start | bytes 98312 | tf_op jit(solution)/shard_map/ppermute | solution.py:213
  18.1 0.5 collective-permute-start.1
  18.6 0.0 collective-permute-done.8
  18.6 0.6 collective-permute-start
  19.2 0.0 collective-permute-done.7
  19.2 0.0 collective-permute-done.9
  19.2 0.0 copy-start.2
  19.3 0.0 copy-start
  19.3 2.1 %collective-permute-start.12 = (bf16[4,2,4,32,128]{4,3,2,1,0:T(8,128)(2,1)S(1)}, bf16[4,2,4,32,128]{4,3,2,1,0:T(8,128)(2,1)S(1)}, u32[]{:S(2)}, u32[]{:S(2)}) collective-permute-start(bf16[4,2,4,32,128]{4,3,2,1,0:T(8,128)(2,1)S(1)} %pad_maximum_fusion.refs_4_), channel_id=1, source_target_pairs={{0,96},{16,19},{1,97},{17,16},{2,98},{18,17},{3,99},{19,18},{32,0}... | collective-permute-start | bytes 786440 | tf_op jit(solution)/shard_map/ppermute | solution.py:220
  21.5 1.2 %collective-permute-start.11 = (bf16[4,2,4,32,128]{4,3,2,1,0:T(8,128)(2,1)S(1)}, bf16[4,2,4,32,128]{4,3,2,1,0:T(8,128)(2,1)S(1)}, u32[]{:S(2)}, u32[]{:S(2)}) collective-permute-start(bf16[4,2,4,32,128]{4,3,2,1,0:T(8,128)(2,1)S(1)} %pad_maximum_fusion.refs_4_), channel_id=1, source_target_pairs={{0,64},{16,18},{1,65},{17,19},{2,66},{18,16},{3,67},{19,17},{32,96... | collective-permute-start | bytes 786440 | tf_op jit(solution)/shard_map/ppermute | solution.py:220
  22.7 0.0 collective-permute-done.2
  22.7 0.0 collective-permute-start.10
  22.7 0.0 collective-permute-done.1
  22.7 0.6 collective-permute-done
  23.3 2.7 %collective-permute-start.5 = (bf16[4,4,32,128]{3,2,1,0:T(8,128)(2,1)S(1)}, bf16[4,4,32,128]{3,2,1,0:T(8,128)(2,1)S(1)}, u32[]{:S(2)}, u32[]{:S(2)}) collective-permute-start(bf16[4,4,32,128]{3,2,1,0:T(8,128)(2,1)S(1)} %pad_maximum_fusion.1.refs_0_), channel_id=1, source_target_pairs={{0,12},{4,8},{8,4},{12,0},{1,13},{5,9},{9,5},{13,1},{2,14},{6,10},... | collective-permute-start | bytes 393224 | tf_op jit(solution)/shard_map/ppermute | solution.py:215
  26.1 0.0 collective-permute-start.4
  26.1 3.3 %collective-permute-done.5.refs_3_ = bf16[4,4,32,128]{3,2,1,0:T(8,128)(2,1)S(1)} collective-permute-done((bf16[4,4,32,128]{3,2,1,0:T(8,128)(2,1)S(1)}, bf16[4,4,32,128]{3,2,1,0:T(8,128)(2,1)S(1)}, u32[]{:S(2)}, u32[]{:S(2)}) %collective-permute-start.5) | collective-permute-done | bytes 131104 | tf_op jit(solution)/shard_map/ppermute | solution.py:215
  29.3 3.3 %collective-permute-start.13 = (bf16[4,2,4,32,128]{4,3,2,1,0:T(8,128)(2,1)S(1)}, bf16[4,2,4,32,128]{4,3,2,1,0:T(8,128)(2,1)S(1)}, u32[]{:S(2)}, u32[]{:S(2)}) collective-permute-start(bf16[4,2,4,32,128]{4,3,2,1,0:T(8,128)(2,1)S(1)} %pad_maximum_fusion.refs_4_), channel_id=1, source_target_pairs={{0,16},{16,0},{1,17},{17,1},{2,18},{18,2},{3,19},{19,3},{4,20},{20... | collective-permute-start | bytes 786440 | tf_op jit(solution)/shard_map/ppermute | solution.py:222
  32.6 0.0 collective-permute-done.12.refs_7_
  32.6 0.0 collective-permute-start.16
  32.7 0.0 collective-permute-done.11.refs_6_
  32.7 0.5 collective-permute-start.15
  33.2 0.0 collective-permute-done.10.refs_5_
  33.2 0.7 collective-permute-start.14
  33.8 2.6 %collective-permute-done.4.refs_2_ = bf16[4,4,32,128]{3,2,1,0:T(8,128)(2,1)S(1)} collective-permute-done((bf16[4,4,32,128]{3,2,1,0:T(8,128)(2,1)S(1)}, bf16[4,4,32,128]{3,2,1,0:T(8,128)(2,1)S(1)}, u32[]{:S(2)}, u32[]{:S(2)}) %collective-permute-start.4) | collective-permute-done | bytes 131104 | tf_op jit(solution)/shard_map/ppermute | solution.py:215
  36.5 1.4 %collective-permute-start.3 = (bf16[4,4,32,128]{3,2,1,0:T(8,128)(2,1)S(1)}, bf16[4,4,32,128]{3,2,1,0:T(8,128)(2,1)S(1)}, u32[]{:S(2)}, u32[]{:S(2)}) collective-permute-start(bf16[4,4,32,128]{3,2,1,0:T(8,128)(2,1)S(1)} %pad_maximum_fusion.1.refs_0_), channel_id=1, source_target_pairs={{0,4},{4,0},{8,12},{12,8},{1,5},{5,1},{9,13},{13,9},{2,6},{6,2},{1... | collective-permute-start | bytes 393224 | tf_op jit(solution)/shard_map/ppermute | solution.py:215
  37.9 2.6 %collective-permute-done.3.refs_1_ = bf16[4,4,32,128]{3,2,1,0:T(8,128)(2,1)S(1)} collective-permute-done((bf16[4,4,32,128]{3,2,1,0:T(8,128)(2,1)S(1)}, bf16[4,4,32,128]{3,2,1,0:T(8,128)(2,1)S(1)}, u32[]{:S(2)}, u32[]{:S(2)}) %collective-permute-start.3) | collective-permute-done | bytes 131104 | tf_op jit(solution)/shard_map/ppermute | solution.py:215
  40.5 0.0 collective-permute-done.13.refs_8_
  40.5 0.0 collective-permute-done.16.refs_11_
  40.5 0.0 collective-permute-done.15.refs_10_
  40.5 0.0 collective-permute-done.14.refs_9_
  40.5 0.0 copy-done.5
  40.5 0.0 copy-done.6
  40.5 0.0 copy-done.3
  40.5 0.0 copy-done.4
  40.5 0.0 copy-done.1
  40.5 0.0 copy-done.2
  40.6 11.3 %shard_map.109 = bf16[16,4,32,128]{3,2,1,0:T(8,128)(2,1)S(1)} custom-call(bf16[4,4,32,128]{3,2,1,0:T(8,128)(2,1)S(1)} %pad_maximum_fusion.1.refs_0_, bf16[4,4,32,128]{3,2,1,0:T(8,128)(2,1)S(1)} %collective-permute-done.3.refs_1_, bf16[4,4,32,128]{3,2,1,0:T(8,128)(2,1)S(1)} %collective-permute-done.4.refs_2_, ...), custom_call_target="tpu_custom_call" | custom-call | tf_op jit(solution)/shard_map/pallas_call | solution.py:146
  51.9 19.5 %all_to_all.5.parts = bf16[16,4,32,128]{3,2,1,0:T(8,128)(2,1)S(1)} all-to-all(bf16[16,4,32,128]{3,2,1,0:T(8,128)(2,1)S(1)} %shard_map.109), channel_id=1, replica_groups=mesh['zh'=2,'y'=4,'c'=2,'zl'=4,'x'=4] {'zl','x'}, dimensions={0} | all-to-all | bytes 1048576 | tf_op jit(solution)/shard_map/all_to_all | solution.py:224
  71.3 0.9 %shard_map.110 = f32[4,4,4096]{2,1,0:T(4,128)} custom-call(bf16[16,4,32,128]{3,2,1,0:T(8,128)(2,1)S(1)} %all_to_all.5.parts), custom_call_target="tpu_custom_call" | custom-call | tf_op jit(solution)/shard_map/pallas_call | solution.py:176
  (15 shorter events, 0.1 us)
Async XLA Ops:
  0.0 8.5 %copy-start.9 = (bf16[4,4,4096]{2,1,0:T(4,128)(2,1)S(1)}, bf16[4,4,4096]{2,1,0:T(4,128)(2,1)}, u32[]{:S(2)}) copy-start(bf16[4,4,4096]{2,1,0:T(4,128)(2,1)} %param.11) | copy-start | bytes 393220
  0.8 9.0 %collective-permute-start.6 = (bf16[4,32,128]{2,1,0:T(8,128)(2,1)S(1)}, bf16[4,32,128]{2,1,0:T(8,128)(2,1)S(1)}, u32[]{:S(2)}, u32[]{:S(2)}) collective-permute-start(bf16[4,32,128]{2,1,0:T(8,128)(2,1)S(1)} %bitcast.25), channel_id=1, source_target_pairs={{0,128},{128,0},{1,129},{129,1},{2,130},{130,2},{3,131},{131,3},{4... | collective-permute-start | bytes 98312 | tf_op jit(solution)/shard_map/ppermute | solution.py:210
  9.8 30.7 %copy-start.5 = (bf16[256,256]{1,0:T(8,128)(2,1)S(1)}, bf16[256,256]{1,0:T(8,128)(2,1)}, u32[]{:S(2)}) copy-start(bf16[256,256]{1,0:T(8,128)(2,1)} %constant.59.clone.refs_15_) | copy-start | bytes 393220
  9.8 30.7 %copy-start.6 = (f32[64,128]{1,0:T(8,128)S(1)}, f32[64,128]{1,0:T(8,128)}, u32[]{:S(2)}) copy-start(f32[64,128]{1,0:T(8,128)} %constant.58.clone.refs_14_) | copy-start | bytes 98308
  9.9 8.8 %collective-permute-start.8 = (bf16[2,4,32,128]{3,2,1,0:T(8,128)(2,1)S(1)}, bf16[2,4,32,128]{3,2,1,0:T(8,128)(2,1)S(1)}, u32[]{:S(2)}, u32[]{:S(2)}) collective-permute-start(bf16[2,4,32,128]{3,2,1,0:T(8,128)(2,1)S(1)} %get-tuple-element.10), channel_id=1, source_target_pairs={{0,2},{16,80},{1,3},{17,81},{2,0},{18,82},{3,1},{19,83},{32,34},{4... | collective-permute-start | bytes 196616 | tf_op jit(solution)/shard_map/ppermute | solution.py:218
  12.9 6.4 %collective-permute-start.7 = (bf16[2,4,32,128]{3,2,1,0:T(8,128)(2,1)S(1)}, bf16[2,4,32,128]{3,2,1,0:T(8,128)(2,1)S(1)}, u32[]{:S(2)}, u32[]{:S(2)}) collective-permute-start(bf16[2,4,32,128]{3,2,1,0:T(8,128)(2,1)S(1)} %get-tuple-element.10), channel_id=1, source_target_pairs={{0,1},{16,48},{1,2},{17,49},{2,3},{18,50},{3,0},{19,51},{32,33},{4... | collective-permute-start | bytes 196616 | tf_op jit(solution)/shard_map/ppermute | solution.py:218
  13.2 6.0 %collective-permute-start.9 = (bf16[2,4,32,128]{3,2,1,0:T(8,128)(2,1)S(1)}, bf16[2,4,32,128]{3,2,1,0:T(8,128)(2,1)S(1)}, u32[]{:S(2)}, u32[]{:S(2)}) collective-permute-start(bf16[2,4,32,128]{3,2,1,0:T(8,128)(2,1)S(1)} %get-tuple-element.10), channel_id=1, source_target_pairs={{0,3},{16,112},{1,0},{17,113},{2,1},{18,114},{3,2},{19,115},{32,35... | collective-permute-start | bytes 196616 | tf_op jit(solution)/shard_map/ppermute | solution.py:218
  15.5 25.0 %copy-start.3 = (bf16[256,256]{1,0:T(8,128)(2,1)S(1)}, bf16[256,256]{1,0:T(8,128)(2,1)}, u32[]{:S(2)}) copy-start(bf16[256,256]{1,0:T(8,128)(2,1)} %constant.63.clone.refs_19_) | copy-start | bytes 393220
  15.5 25.0 %copy-start.4 = (bf16[256,256]{1,0:T(8,128)(2,1)S(1)}, bf16[256,256]{1,0:T(8,128)(2,1)}, u32[]{:S(2)}) copy-start(bf16[256,256]{1,0:T(8,128)(2,1)} %constant.61.clone.refs_17_) | copy-start | bytes 393220
  15.5 7.2 %collective-permute-start.2 = (bf16[4,32,128]{2,1,0:T(8,128)(2,1)S(1)}, bf16[4,32,128]{2,1,0:T(8,128)(2,1)S(1)}, u32[]{:S(2)}, u32[]{:S(2)}) collective-permute-start(bf16[4,32,128]{2,1,0:T(8,128)(2,1)S(1)} %get-tuple-element.6), channel_id=1, source_target_pairs={{0,3},{1,0},{2,1},{3,2},{4,7},{5,4},{6,5},{7,6},{8,11},{9,8},{10,9... | collective-permute-start | bytes 98312 | tf_op jit(solution)/shard_map/ppermute | solution.py:213
  18.1 4.6 %collective-permute-start.1 = (bf16[4,32,128]{2,1,0:T(8,128)(2,1)S(1)}, bf16[4,32,128]{2,1,0:T(8,128)(2,1)S(1)}, u32[]{:S(2)}, u32[]{:S(2)}) collective-permute-start(bf16[4,32,128]{2,1,0:T(8,128)(2,1)S(1)} %get-tuple-element.7), channel_id=1, source_target_pairs={{0,2},{1,3},{2,0},{3,1},{4,6},{5,7},{6,4},{7,5},{8,10},{9,11},{10,... | collective-permute-start | bytes 98312 | tf_op jit(solution)/shard_map/ppermute | solution.py:213
  18.6 4.7 %collective-permute-start = (bf16[4,32,128]{2,1,0:T(8,128)(2,1)S(1)}, bf16[4,32,128]{2,1,0:T(8,128)(2,1)S(1)}, u32[]{:S(2)}, u32[]{:S(2)}) collective-permute-start(bf16[4,32,128]{2,1,0:T(8,128)(2,1)S(1)} %get-tuple-element.8), channel_id=1, source_target_pairs={{0,1},{1,2},{2,3},{3,0},{4,5},{5,6},{6,7},{7,4},{8,9},{9,10},{10,1... | collective-permute-start | bytes 98312 | tf_op jit(solution)/shard_map/ppermute | solution.py:213
  19.2 21.3 %copy-start.1 = (bf16[256,512]{1,0:T(8,128)(2,1)S(1)}, bf16[256,512]{1,0:T(8,128)(2,1)}, u32[]{:S(2)}) copy-start(bf16[256,512]{1,0:T(8,128)(2,1)} %constant.62.clone.refs_18_) | copy-start | bytes 786436
  19.2 21.3 %copy-start.2 = (bf16[256,512]{1,0:T(8,128)(2,1)S(1)}, bf16[256,512]{1,0:T(8,128)(2,1)}, u32[]{:S(2)}) copy-start(bf16[256,512]{1,0:T(8,128)(2,1)} %constant.60.clone.refs_16_) | copy-start | bytes 786436
  19.3 21.2 %copy-start = (bf16[512,256]{1,0:T(8,128)(2,1)S(1)}, bf16[512,256]{1,0:T(8,128)(2,1)}, u32[]{:S(2)}) copy-start(bf16[512,256]{1,0:T(8,128)(2,1)} %constant.64.clone.refs_20_) | copy-start | bytes 786436
  19.3 13.3 %collective-permute-start.12 = (bf16[4,2,4,32,128]{4,3,2,1,0:T(8,128)(2,1)S(1)}, bf16[4,2,4,32,128]{4,3,2,1,0:T(8,128)(2,1)S(1)}, u32[]{:S(2)}, u32[]{:S(2)}) collective-permute-start(bf16[4,2,4,32,128]{4,3,2,1,0:T(8,128)(2,1)S(1)} %pad_maximum_fusion.refs_4_), channel_id=1, source_target_pairs={{0,96},{16,19},{1,97},{17,16},{2,98},{18,17},{3,99},{19,18},{32,0}... | collective-permute-start | bytes 786440 | tf_op jit(solution)/shard_map/ppermute | solution.py:220
  21.5 11.2 %collective-permute-start.11 = (bf16[4,2,4,32,128]{4,3,2,1,0:T(8,128)(2,1)S(1)}, bf16[4,2,4,32,128]{4,3,2,1,0:T(8,128)(2,1)S(1)}, u32[]{:S(2)}, u32[]{:S(2)}) collective-permute-start(bf16[4,2,4,32,128]{4,3,2,1,0:T(8,128)(2,1)S(1)} %pad_maximum_fusion.refs_4_), channel_id=1, source_target_pairs={{0,64},{16,18},{1,65},{17,19},{2,66},{18,16},{3,67},{19,17},{32,96... | collective-permute-start | bytes 786440 | tf_op jit(solution)/shard_map/ppermute | solution.py:220
  22.7 10.5 %collective-permute-start.10 = (bf16[4,2,4,32,128]{4,3,2,1,0:T(8,128)(2,1)S(1)}, bf16[4,2,4,32,128]{4,3,2,1,0:T(8,128)(2,1)S(1)}, u32[]{:S(2)}, u32[]{:S(2)}) collective-permute-start(bf16[4,2,4,32,128]{4,3,2,1,0:T(8,128)(2,1)S(1)} %pad_maximum_fusion.refs_4_), channel_id=1, source_target_pairs={{0,32},{16,17},{1,33},{17,18},{2,34},{18,19},{3,35},{19,16},{32,64... | collective-permute-start | bytes 786440 | tf_op jit(solution)/shard_map/ppermute | solution.py:220
  23.3 17.2 %copy-start.7 = (f32[8]{0:T(128)S(1)}, f32[8]{0:T(128)}, u32[]{:S(2)}) copy-start(f32[8]{0:T(128)} %refs_12_.1) | copy-start | bytes 100
  23.3 17.3 %copy-start.8 = (f32[8]{0:T(128)S(1)}, f32[8]{0:T(128)}, u32[]{:S(2)}) copy-start(f32[8]{0:T(128)} %refs_13_.1) | copy-start | bytes 100
  23.3 6.0 %collective-permute-start.5 = (bf16[4,4,32,128]{3,2,1,0:T(8,128)(2,1)S(1)}, bf16[4,4,32,128]{3,2,1,0:T(8,128)(2,1)S(1)}, u32[]{:S(2)}, u32[]{:S(2)}) collective-permute-start(bf16[4,4,32,128]{3,2,1,0:T(8,128)(2,1)S(1)} %pad_maximum_fusion.1.refs_0_), channel_id=1, source_target_pairs={{0,12},{4,8},{8,4},{12,0},{1,13},{5,9},{9,5},{13,1},{2,14},{6,10},... | collective-permute-start | bytes 393224 | tf_op jit(solution)/shard_map/ppermute | solution.py:215
  26.1 10.4 %collective-permute-start.4 = (bf16[4,4,32,128]{3,2,1,0:T(8,128)(2,1)S(1)}, bf16[4,4,32,128]{3,2,1,0:T(8,128)(2,1)S(1)}, u32[]{:S(2)}, u32[]{:S(2)}) collective-permute-start(bf16[4,4,32,128]{3,2,1,0:T(8,128)(2,1)S(1)} %pad_maximum_fusion.1.refs_0_), channel_id=1, source_target_pairs={{0,8},{4,12},{8,0},{12,4},{1,9},{5,13},{9,1},{13,5},{2,10},{6,14},... | collective-permute-start | bytes 393224 | tf_op jit(solution)/shard_map/ppermute | solution.py:215
  29.3 11.1 %collective-permute-start.13 = (bf16[4,2,4,32,128]{4,3,2,1,0:T(8,128)(2,1)S(1)}, bf16[4,2,4,32,128]{4,3,2,1,0:T(8,128)(2,1)S(1)}, u32[]{:S(2)}, u32[]{:S(2)}) collective-permute-start(bf16[4,2,4,32,128]{4,3,2,1,0:T(8,128)(2,1)S(1)} %pad_maximum_fusion.refs_4_), channel_id=1, source_target_pairs={{0,16},{16,0},{1,17},{17,1},{2,18},{18,2},{3,19},{19,3},{4,20},{20... | collective-permute-start | bytes 786440 | tf_op jit(solution)/shard_map/ppermute | solution.py:222
  32.6 7.8 %collective-permute-start.16 = (bf16[4,2,4,32,128]{4,3,2,1,0:T(8,128)(2,1)S(1)}, bf16[4,2,4,32,128]{4,3,2,1,0:T(8,128)(2,1)S(1)}, u32[]{:S(2)}, u32[]{:S(2)}) collective-permute-start(bf16[4,2,4,32,128]{4,3,2,1,0:T(8,128)(2,1)S(1)} %collective-permute-done.12.refs_7_), channel_id=1, source_target_pairs={{0,16},{16,0},{1,17},{17,1},{2,18},{18,2},{3,19},{19,3},{4,20},{20... | collective-permute-start | bytes 786440 | tf_op jit(solution)/shard_map/ppermute | solution.py:222
  32.7 7.8 %collective-permute-start.15 = (bf16[4,2,4,32,128]{4,3,2,1,0:T(8,128)(2,1)S(1)}, bf16[4,2,4,32,128]{4,3,2,1,0:T(8,128)(2,1)S(1)}, u32[]{:S(2)}, u32[]{:S(2)}) collective-permute-start(bf16[4,2,4,32,128]{4,3,2,1,0:T(8,128)(2,1)S(1)} %collective-permute-done.11.refs_6_), channel_id=1, source_target_pairs={{0,16},{16,0},{1,17},{17,1},{2,18},{18,2},{3,19},{19,3},{4,20},{20... | collective-permute-start | bytes 786440 | tf_op jit(solution)/shard_map/ppermute | solution.py:222
  33.2 7.3 %collective-permute-start.14 = (bf16[4,2,4,32,128]{4,3,2,1,0:T(8,128)(2,1)S(1)}, bf16[4,2,4,32,128]{4,3,2,1,0:T(8,128)(2,1)S(1)}, u32[]{:S(2)}, u32[]{:S(2)}) collective-permute-start(bf16[4,2,4,32,128]{4,3,2,1,0:T(8,128)(2,1)S(1)} %collective-permute-done.10.refs_5_), channel_id=1, source_target_pairs={{0,16},{16,0},{1,17},{17,1},{2,18},{18,2},{3,19},{19,3},{4,20},{20... | collective-permute-start | bytes 786440 | tf_op jit(solution)/shard_map/ppermute | solution.py:222
  36.5 4.0 %collective-permute-start.3 = (bf16[4,4,32,128]{3,2,1,0:T(8,128)(2,1)S(1)}, bf16[4,4,32,128]{3,2,1,0:T(8,128)(2,1)S(1)}, u32[]{:S(2)}, u32[]{:S(2)}) collective-permute-start(bf16[4,4,32,128]{3,2,1,0:T(8,128)(2,1)S(1)} %pad_maximum_fusion.1.refs_0_), channel_id=1, source_target_pairs={{0,4},{4,0},{8,12},{12,8},{1,5},{5,1},{9,13},{13,9},{2,6},{6,2},{1... | collective-permute-start | bytes 393224 | tf_op jit(solution)/shard_map/ppermute | solution.py:215

commit v7 on v6

--- a/solution.py
+++ b/solution.py
@@ -78,13 +78,13 @@
     def swap(a):
         return pltpu.roll(a, 64, 2)
 
-    def by_fours(step):
-        def four(group, carry):
-            for n in range(4):
-                step(4 * group + n)
+    def by_eights(step):
+        def eight(group, carry):
+            for n in range(8):
+                step(8 * group + n)
             return carry
 
-        lax.fori_loop(0, 4, four, 0)
+        lax.fori_loop(0, 2, eight, 0)
 
     def parts(a, axis):
         high = a.astype(BF16)
@@ -122,7 +122,7 @@
         along_z = dot(jnp.concatenate(dense, axis=1), z_in[...])
         field[b] = dot(y_in[...], parts(along_z, 0)).astype(BF16)
 
-    by_fours(enter)
+    by_eights(enter)
 
     for k in range(16):
         rows = slice(16 * k, 16 * k + 16)
@@ -138,7 +138,7 @@
         terms = terms + swap(terms)
         out[b] = jnp.where(lane, terms[:, :32], terms[:, 32:]).astype(out.dtype)
 
-    by_fours(leave)
+    by_eights(leave)
 
 
 def pair_sums(targets, sources, exponents, coefficients):

time: 73.6 us -> 72.8 us (0.989)
  Pallas kernels: 12.2 us -> 11.4 us
    pallas_call x1, Pallas kernels: 11.3 us -> 10.5 us  [pair_sums(): pl.pallas_call(pair_kernel, out_shape=jax.ShapeDtypeStruct((16, 4, 32, 12...]
where the time goes in v7:
time: 72.8 us; the launch traced here: 71.4 us
  starting transfers between devices  29.1 us (40%)
  blocking collectives  19.4 us (27%)
  Pallas kernels  11.4 us (16%)
  waiting for transfers between devices  10.3 us (14%)
  local copies, waits for them, and re-layouts  1.01 us (1%)
    all_to_all x1, blocking collectives, exchange(): parts = lax.all_to_all(part, ('zl', 'x'), 0, 0, tiled=True)  19.4 us
    pallas_call x1, Pallas kernels, pair_sums(): pl.pallas_call(pair_kernel, out_shape=jax.ShapeDtypeStruct((16, 4, 32, 12...  10.5 us
    ppermute x3, waiting for transfers between devices, exchange(): lax.ppermute(target_block, 'zl', flip(4, k))  8.52 us
    ppermute x1, starting transfers between devices, exchange(): other = lax.ppermute(mine, 'zh', turn(2, 1))  7.73 us
    ppermute x3, starting transfers between devices, exchange(): first = {i: lax.ppermute(block, plane, weave(i, 0)) for i in SHIFTS}  5.68 us
    ppermute x4, starting transfers between devices, exchange(): other_core = [lax.ppermute(own_core[l], 'c', turn(2, 1)) for l in range(4)]  4.47 us
    ppermute x3, starting transfers between devices, exchange(): lax.ppermute(target_block, 'zl', flip(4, k))  4.12 us
    ppermute x3, starting transfers between devices, exchange(): rows = {j: lax.ppermute(pick(j), 'x', turn(4, j)) for j in SHIFTS}  3.68 us
  transfers between devices with their start and end apart: 17, of which 5 were waited for; matrix products, arithmetic and copies ran while one was open for 0% of the time, Pallas kernels for 0%

profile of v7, /device:TPU:1, one launch (start us, length us, event | category | flops | bytes accessed | tf_op | source)
XLA Modules:
  0.0 71.4 jit_solution(15570248672931922823)
XLA Ops:
  0.0 0.8 %copy.16 = bf16[1,4,32,128]{3,2,1,0:T(8,128)(2,1)S(1)} copy(bf16[1,4,32,128]{3,1,2,0:T(4,128)(2,1)} %bitcast.29) | data formatting | bytes 65536
  0.8 7.7 %collective-permute-start.6 = (bf16[4,32,128]{2,1,0:T(8,128)(2,1)S(1)}, bf16[4,32,128]{2,1,0:T(8,128)(2,1)S(1)}, u32[]{:S(2)}, u32[]{:S(2)}) collective-permute-start(bf16[4,32,128]{2,1,0:T(8,128)(2,1)S(1)} %bitcast.25), channel_id=1, source_target_pairs={{0,128},{128,0},{1,129},{129,1},{2,130},{130,2},{3,131},{131,3},{4... | collective-permute-start | bytes 98312 | tf_op jit(solution)/shard_map/ppermute | solution.py:210
  8.5 0.0 copy-done.9
  8.5 0.2 reshape.6
  8.7 1.1 %collective-permute-done.6 = bf16[4,32,128]{2,1,0:T(8,128)(2,1)S(1)} collective-permute-done((bf16[4,32,128]{2,1,0:T(8,128)(2,1)S(1)}, bf16[4,32,128]{2,1,0:T(8,128)(2,1)S(1)}, u32[]{:S(2)}, u32[]{:S(2)}) %collective-permute-start.6) | collective-permute-done | bytes 32800 | tf_op jit(solution)/shard_map/ppermute | solution.py:210
  9.9 3.0 %collective-permute-start.8 = (bf16[2,4,32,128]{3,2,1,0:T(8,128)(2,1)S(1)}, bf16[2,4,32,128]{3,2,1,0:T(8,128)(2,1)S(1)}, u32[]{:S(2)}, u32[]{:S(2)}) collective-permute-start(bf16[2,4,32,128]{3,2,1,0:T(8,128)(2,1)S(1)} %get-tuple-element.10), channel_id=1, source_target_pairs={{0,2},{16,80},{1,3},{17,81},{2,0},{18,82},{3,1},{19,83},{32,34},{4... | collective-permute-start | bytes 196616 | tf_op jit(solution)/shard_map/ppermute | solution.py:218
  12.9 0.4 collective-permute-start.7
  13.2 2.3 %collective-permute-start.9 = (bf16[2,4,32,128]{3,2,1,0:T(8,128)(2,1)S(1)}, bf16[2,4,32,128]{3,2,1,0:T(8,128)(2,1)S(1)}, u32[]{:S(2)}, u32[]{:S(2)}) collective-permute-start(bf16[2,4,32,128]{3,2,1,0:T(8,128)(2,1)S(1)} %get-tuple-element.10), channel_id=1, source_target_pairs={{0,3},{16,112},{1,0},{17,113},{2,1},{18,114},{3,2},{19,115},{32,35... | collective-permute-start | bytes 196616 | tf_op jit(solution)/shard_map/ppermute | solution.py:218
  15.5 2.6 %collective-permute-start.2 = (bf16[4,32,128]{2,1,0:T(8,128)(2,1)S(1)}, bf16[4,32,128]{2,1,0:T(8,128)(2,1)S(1)}, u32[]{:S(2)}, u32[]{:S(2)}) collective-permute-start(bf16[4,32,128]{2,1,0:T(8,128)(2,1)S(1)} %get-tuple-element.6), channel_id=1, source_target_pairs={{0,3},{1,0},{2,1},{3,2},{4,7},{5,4},{6,5},{7,6},{8,11},{9,8},{10,9... | collective-permute-start | bytes 98312 | tf_op jit(solution)/shard_map/ppermute | solution.py:213
  18.1 0.5 collective-permute-start.1
  18.6 0.0 collective-permute-done.8
  18.6 0.6 collective-permute-start
  19.2 0.0 collective-permute-done.7
  19.2 0.0 collective-permute-done.9
  19.2 0.0 copy-start.2
  19.3 0.0 copy-start
  19.3 2.1 %collective-permute-start.12 = (bf16[4,2,4,32,128]{4,3,2,1,0:T(8,128)(2,1)S(1)}, bf16[4,2,4,32,128]{4,3,2,1,0:T(8,128)(2,1)S(1)}, u32[]{:S(2)}, u32[]{:S(2)}) collective-permute-start(bf16[4,2,4,32,128]{4,3,2,1,0:T(8,128)(2,1)S(1)} %pad_maximum_fusion.refs_4_), channel_id=1, source_target_pairs={{0,96},{16,19},{1,97},{17,16},{2,98},{18,17},{3,99},{19,18},{32,0}... | collective-permute-start | bytes 786440 | tf_op jit(solution)/shard_map/ppermute | solution.py:220
  21.5 1.2 %collective-permute-start.11 = (bf16[4,2,4,32,128]{4,3,2,1,0:T(8,128)(2,1)S(1)}, bf16[4,2,4,32,128]{4,3,2,1,0:T(8,128)(2,1)S(1)}, u32[]{:S(2)}, u32[]{:S(2)}) collective-permute-start(bf16[4,2,4,32,128]{4,3,2,1,0:T(8,128)(2,1)S(1)} %pad_maximum_fusion.refs_4_), channel_id=1, source_target_pairs={{0,64},{16,18},{1,65},{17,19},{2,66},{18,16},{3,67},{19,17},{32,96... | collective-permute-start | bytes 786440 | tf_op jit(solution)/shard_map/ppermute | solution.py:220
  22.7 0.0 collective-permute-done.2
  22.7 0.0 collective-permute-start.10
  22.7 0.0 collective-permute-done.1
  22.7 0.6 collective-permute-done
  23.3 2.7 %collective-permute-start.5 = (bf16[4,4,32,128]{3,2,1,0:T(8,128)(2,1)S(1)}, bf16[4,4,32,128]{3,2,1,0:T(8,128)(2,1)S(1)}, u32[]{:S(2)}, u32[]{:S(2)}) collective-permute-start(bf16[4,4,32,128]{3,2,1,0:T(8,128)(2,1)S(1)} %pad_maximum_fusion.1.refs_0_), channel_id=1, source_target_pairs={{0,12},{4,8},{8,4},{12,0},{1,13},{5,9},{9,5},{13,1},{2,14},{6,10},... | collective-permute-start | bytes 393224 | tf_op jit(solution)/shard_map/ppermute | solution.py:215
  26.1 0.0 collective-permute-start.4
  26.1 3.3 %collective-permute-done.5.refs_3_ = bf16[4,4,32,128]{3,2,1,0:T(8,128)(2,1)S(1)} collective-permute-done((bf16[4,4,32,128]{3,2,1,0:T(8,128)(2,1)S(1)}, bf16[4,4,32,128]{3,2,1,0:T(8,128)(2,1)S(1)}, u32[]{:S(2)}, u32[]{:S(2)}) %collective-permute-start.5) | collective-permute-done | bytes 131104 | tf_op jit(solution)/shard_map/ppermute | solution.py:215
  29.3 3.3 %collective-permute-start.13 = (bf16[4,2,4,32,128]{4,3,2,1,0:T(8,128)(2,1)S(1)}, bf16[4,2,4,32,128]{4,3,2,1,0:T(8,128)(2,1)S(1)}, u32[]{:S(2)}, u32[]{:S(2)}) collective-permute-start(bf16[4,2,4,32,128]{4,3,2,1,0:T(8,128)(2,1)S(1)} %pad_maximum_fusion.refs_4_), channel_id=1, source_target_pairs={{0,16},{16,0},{1,17},{17,1},{2,18},{18,2},{3,19},{19,3},{4,20},{20... | collective-permute-start | bytes 786440 | tf_op jit(solution)/shard_map/ppermute | solution.py:222
  32.6 0.0 collective-permute-done.12.refs_7_
  32.6 0.0 collective-permute-start.16
  32.7 0.0 collective-permute-done.11.refs_6_
  32.7 0.5 collective-permute-start.15
  33.2 0.0 collective-permute-done.10.refs_5_
  33.2 0.7 collective-permute-start.14
  33.8 2.6 %collective-permute-done.4.refs_2_ = bf16[4,4,32,128]{3,2,1,0:T(8,128)(2,1)S(1)} collective-permute-done((bf16[4,4,32,128]{3,2,1,0:T(8,128)(2,1)S(1)}, bf16[4,4,32,128]{3,2,1,0:T(8,128)(2,1)S(1)}, u32[]{:S(2)}, u32[]{:S(2)}) %collective-permute-start.4) | collective-permute-done | bytes 131104 | tf_op jit(solution)/shard_map/ppermute | solution.py:215
  36.5 1.4 %collective-permute-start.3 = (bf16[4,4,32,128]{3,2,1,0:T(8,128)(2,1)S(1)}, bf16[4,4,32,128]{3,2,1,0:T(8,128)(2,1)S(1)}, u32[]{:S(2)}, u32[]{:S(2)}) collective-permute-start(bf16[4,4,32,128]{3,2,1,0:T(8,128)(2,1)S(1)} %pad_maximum_fusion.1.refs_0_), channel_id=1, source_target_pairs={{0,4},{4,0},{8,12},{12,8},{1,5},{5,1},{9,13},{13,9},{2,6},{6,2},{1... | collective-permute-start | bytes 393224 | tf_op jit(solution)/shard_map/ppermute | solution.py:215
  37.9 2.6 %collective-permute-done.3.refs_1_ = bf16[4,4,32,128]{3,2,1,0:T(8,128)(2,1)S(1)} collective-permute-done((bf16[4,4,32,128]{3,2,1,0:T(8,128)(2,1)S(1)}, bf16[4,4,32,128]{3,2,1,0:T(8,128)(2,1)S(1)}, u32[]{:S(2)}, u32[]{:S(2)}) %collective-permute-start.3) | collective-permute-done | bytes 131104 | tf_op jit(solution)/shard_map/ppermute | solution.py:215
  40.5 0.0 collective-permute-done.13.refs_8_
  40.5 0.0 collective-permute-done.16.refs_11_
  40.5 0.0 collective-permute-done.15.refs_10_
  40.5 0.0 collective-permute-done.14.refs_9_
  40.5 0.0 copy-done.5
  40.5 0.0 copy-done.6
  40.5 0.0 copy-done.3
  40.5 0.0 copy-done.4
  40.5 0.0 copy-done.1
  40.5 0.0 copy-done.2
  40.6 10.5 %shard_map.109 = bf16[16,4,32,128]{3,2,1,0:T(8,128)(2,1)S(1)} custom-call(bf16[4,4,32,128]{3,2,1,0:T(8,128)(2,1)S(1)} %pad_maximum_fusion.1.refs_0_, bf16[4,4,32,128]{3,2,1,0:T(8,128)(2,1)S(1)} %collective-permute-done.3.refs_1_, bf16[4,4,32,128]{3,2,1,0:T(8,128)(2,1)S(1)} %collective-permute-done.4.refs_2_, ...), custom_call_target="tpu_custom_call" | custom-call | tf_op jit(solution)/shard_map/pallas_call | solution.py:146
  51.1 19.4 %all_to_all.5.parts = bf16[16,4,32,128]{3,2,1,0:T(8,128)(2,1)S(1)} all-to-all(bf16[16,4,32,128]{3,2,1,0:T(8,128)(2,1)S(1)} %shard_map.109), channel_id=1, replica_groups=mesh['zh'=2,'y'=4,'c'=2,'zl'=4,'x'=4] {'zl','x'}, dimensions={0} | all-to-all | bytes 1048576 | tf_op jit(solution)/shard_map/all_to_all | solution.py:224
  70.5 0.9 %shard_map.110 = f32[4,4,4096]{2,1,0:T(4,128)} custom-call(bf16[16,4,32,128]{3,2,1,0:T(8,128)(2,1)S(1)} %all_to_all.5.parts), custom_call_target="tpu_custom_call" | custom-call | tf_op jit(solution)/shard_map/pallas_call | solution.py:176
  (15 shorter events, 0.1 us)
Async XLA Ops:
  0.0 8.5 %copy-start.9 = (bf16[4,4,4096]{2,1,0:T(4,128)(2,1)S(1)}, bf16[4,4,4096]{2,1,0:T(4,128)(2,1)}, u32[]{:S(2)}) copy-start(bf16[4,4,4096]{2,1,0:T(4,128)(2,1)} %param.11) | copy-start | bytes 393220
  0.8 9.0 %collective-permute-start.6 = (bf16[4,32,128]{2,1,0:T(8,128)(2,1)S(1)}, bf16[4,32,128]{2,1,0:T(8,128)(2,1)S(1)}, u32[]{:S(2)}, u32[]{:S(2)}) collective-permute-start(bf16[4,32,128]{2,1,0:T(8,128)(2,1)S(1)} %bitcast.25), channel_id=1, source_target_pairs={{0,128},{128,0},{1,129},{129,1},{2,130},{130,2},{3,131},{131,3},{4... | collective-permute-start | bytes 98312 | tf_op jit(solution)/shard_map/ppermute | solution.py:210
  9.8 30.7 %copy-start.5 = (bf16[256,256]{1,0:T(8,128)(2,1)S(1)}, bf16[256,256]{1,0:T(8,128)(2,1)}, u32[]{:S(2)}) copy-start(bf16[256,256]{1,0:T(8,128)(2,1)} %constant.59.clone.refs_15_) | copy-start | bytes 393220
  9.8 30.7 %copy-start.6 = (f32[64,128]{1,0:T(8,128)S(1)}, f32[64,128]{1,0:T(8,128)}, u32[]{:S(2)}) copy-start(f32[64,128]{1,0:T(8,128)} %constant.58.clone.refs_14_) | copy-start | bytes 98308
  9.9 8.8 %collective-permute-start.8 = (bf16[2,4,32,128]{3,2,1,0:T(8,128)(2,1)S(1)}, bf16[2,4,32,128]{3,2,1,0:T(8,128)(2,1)S(1)}, u32[]{:S(2)}, u32[]{:S(2)}) collective-permute-start(bf16[2,4,32,128]{3,2,1,0:T(8,128)(2,1)S(1)} %get-tuple-element.10), channel_id=1, source_target_pairs={{0,2},{16,80},{1,3},{17,81},{2,0},{18,82},{3,1},{19,83},{32,34},{4... | collective-permute-start | bytes 196616 | tf_op jit(solution)/shard_map/ppermute | solution.py:218
  12.9 6.4 %collective-permute-start.7 = (bf16[2,4,32,128]{3,2,1,0:T(8,128)(2,1)S(1)}, bf16[2,4,32,128]{3,2,1,0:T(8,128)(2,1)S(1)}, u32[]{:S(2)}, u32[]{:S(2)}) collective-permute-start(bf16[2,4,32,128]{3,2,1,0:T(8,128)(2,1)S(1)} %get-tuple-element.10), channel_id=1, source_target_pairs={{0,1},{16,48},{1,2},{17,49},{2,3},{18,50},{3,0},{19,51},{32,33},{4... | collective-permute-start | bytes 196616 | tf_op jit(solution)/shard_map/ppermute | solution.py:218
  13.2 6.0 %collective-permute-start.9 = (bf16[2,4,32,128]{3,2,1,0:T(8,128)(2,1)S(1)}, bf16[2,4,32,128]{3,2,1,0:T(8,128)(2,1)S(1)}, u32[]{:S(2)}, u32[]{:S(2)}) collective-permute-start(bf16[2,4,32,128]{3,2,1,0:T(8,128)(2,1)S(1)} %get-tuple-element.10), channel_id=1, source_target_pairs={{0,3},{16,112},{1,0},{17,113},{2,1},{18,114},{3,2},{19,115},{32,35... | collective-permute-start | bytes 196616 | tf_op jit(solution)/shard_map/ppermute | solution.py:218
  15.5 25.0 %copy-start.3 = (bf16[256,256]{1,0:T(8,128)(2,1)S(1)}, bf16[256,256]{1,0:T(8,128)(2,1)}, u32[]{:S(2)}) copy-start(bf16[256,256]{1,0:T(8,128)(2,1)} %constant.63.clone.refs_19_) | copy-start | bytes 393220
  15.5 25.0 %copy-start.4 = (bf16[256,256]{1,0:T(8,128)(2,1)S(1)}, bf16[256,256]{1,0:T(8,128)(2,1)}, u32[]{:S(2)}) copy-start(bf16[256,256]{1,0:T(8,128)(2,1)} %constant.61.clone.refs_17_) | copy-start | bytes 393220
  15.5 7.2 %collective-permute-start.2 = (bf16[4,32,128]{2,1,0:T(8,128)(2,1)S(1)}, bf16[4,32,128]{2,1,0:T(8,128)(2,1)S(1)}, u32[]{:S(2)}, u32[]{:S(2)}) collective-permute-start(bf16[4,32,128]{2,1,0:T(8,128)(2,1)S(1)} %get-tuple-element.6), channel_id=1, source_target_pairs={{0,3},{1,0},{2,1},{3,2},{4,7},{5,4},{6,5},{7,6},{8,11},{9,8},{10,9... | collective-permute-start | bytes 98312 | tf_op jit(solution)/shard_map/ppermute | solution.py:213
  18.1 4.6 %collective-permute-start.1 = (bf16[4,32,128]{2,1,0:T(8,128)(2,1)S(1)}, bf16[4,32,128]{2,1,0:T(8,128)(2,1)S(1)}, u32[]{:S(2)}, u32[]{:S(2)}) collective-permute-start(bf16[4,32,128]{2,1,0:T(8,128)(2,1)S(1)} %get-tuple-element.7), channel_id=1, source_target_pairs={{0,2},{1,3},{2,0},{3,1},{4,6},{5,7},{6,4},{7,5},{8,10},{9,11},{10,... | collective-permute-start | bytes 98312 | tf_op jit(solution)/shard_map/ppermute | solution.py:213
  18.6 4.7 %collective-permute-start = (bf16[4,32,128]{2,1,0:T(8,128)(2,1)S(1)}, bf16[4,32,128]{2,1,0:T(8,128)(2,1)S(1)}, u32[]{:S(2)}, u32[]{:S(2)}) collective-permute-start(bf16[4,32,128]{2,1,0:T(8,128)(2,1)S(1)} %get-tuple-element.8), channel_id=1, source_target_pairs={{0,1},{1,2},{2,3},{3,0},{4,5},{5,6},{6,7},{7,4},{8,9},{9,10},{10,1... | collective-permute-start | bytes 98312 | tf_op jit(solution)/shard_map/ppermute | solution.py:213
  19.2 21.3 %copy-start.1 = (bf16[256,512]{1,0:T(8,128)(2,1)S(1)}, bf16[256,512]{1,0:T(8,128)(2,1)}, u32[]{:S(2)}) copy-start(bf16[256,512]{1,0:T(8,128)(2,1)} %constant.62.clone.refs_18_) | copy-start | bytes 786436
  19.2 21.3 %copy-start.2 = (bf16[256,512]{1,0:T(8,128)(2,1)S(1)}, bf16[256,512]{1,0:T(8,128)(2,1)}, u32[]{:S(2)}) copy-start(bf16[256,512]{1,0:T(8,128)(2,1)} %constant.60.clone.refs_16_) | copy-start | bytes 786436
  19.3 21.2 %copy-start = (bf16[512,256]{1,0:T(8,128)(2,1)S(1)}, bf16[512,256]{1,0:T(8,128)(2,1)}, u32[]{:S(2)}) copy-start(bf16[512,256]{1,0:T(8,128)(2,1)} %constant.64.clone.refs_20_) | copy-start | bytes 786436
  19.3 13.3 %collective-permute-start.12 = (bf16[4,2,4,32,128]{4,3,2,1,0:T(8,128)(2,1)S(1)}, bf16[4,2,4,32,128]{4,3,2,1,0:T(8,128)(2,1)S(1)}, u32[]{:S(2)}, u32[]{:S(2)}) collective-permute-start(bf16[4,2,4,32,128]{4,3,2,1,0:T(8,128)(2,1)S(1)} %pad_maximum_fusion.refs_4_), channel_id=1, source_target_pairs={{0,96},{16,19},{1,97},{17,16},{2,98},{18,17},{3,99},{19,18},{32,0}... | collective-permute-start | bytes 786440 | tf_op jit(solution)/shard_map/ppermute | solution.py:220
  21.5 11.2 %collective-permute-start.11 = (bf16[4,2,4,32,128]{4,3,2,1,0:T(8,128)(2,1)S(1)}, bf16[4,2,4,32,128]{4,3,2,1,0:T(8,128)(2,1)S(1)}, u32[]{:S(2)}, u32[]{:S(2)}) collective-permute-start(bf16[4,2,4,32,128]{4,3,2,1,0:T(8,128)(2,1)S(1)} %pad_maximum_fusion.refs_4_), channel_id=1, source_target_pairs={{0,64},{16,18},{1,65},{17,19},{2,66},{18,16},{3,67},{19,17},{32,96... | collective-permute-start | bytes 786440 | tf_op jit(solution)/shard_map/ppermute | solution.py:220
  22.7 10.5 %collective-permute-start.10 = (bf16[4,2,4,32,128]{4,3,2,1,0:T(8,128)(2,1)S(1)}, bf16[4,2,4,32,128]{4,3,2,1,0:T(8,128)(2,1)S(1)}, u32[]{:S(2)}, u32[]{:S(2)}) collective-permute-start(bf16[4,2,4,32,128]{4,3,2,1,0:T(8,128)(2,1)S(1)} %pad_maximum_fusion.refs_4_), channel_id=1, source_target_pairs={{0,32},{16,17},{1,33},{17,18},{2,34},{18,19},{3,35},{19,16},{32,64... | collective-permute-start | bytes 786440 | tf_op jit(solution)/shard_map/ppermute | solution.py:220
  23.3 17.2 %copy-start.7 = (f32[8]{0:T(128)S(1)}, f32[8]{0:T(128)}, u32[]{:S(2)}) copy-start(f32[8]{0:T(128)} %refs_12_.1) | copy-start | bytes 100
  23.3 17.3 %copy-start.8 = (f32[8]{0:T(128)S(1)}, f32[8]{0:T(128)}, u32[]{:S(2)}) copy-start(f32[8]{0:T(128)} %refs_13_.1) | copy-start | bytes 100
  23.3 6.0 %collective-permute-start.5 = (bf16[4,4,32,128]{3,2,1,0:T(8,128)(2,1)S(1)}, bf16[4,4,32,128]{3,2,1,0:T(8,128)(2,1)S(1)}, u32[]{:S(2)}, u32[]{:S(2)}) collective-permute-start(bf16[4,4,32,128]{3,2,1,0:T(8,128)(2,1)S(1)} %pad_maximum_fusion.1.refs_0_), channel_id=1, source_target_pairs={{0,12},{4,8},{8,4},{12,0},{1,13},{5,9},{9,5},{13,1},{2,14},{6,10},... | collective-permute-start | bytes 393224 | tf_op jit(solution)/shard_map/ppermute | solution.py:215
  26.1 10.4 %collective-permute-start.4 = (bf16[4,4,32,128]{3,2,1,0:T(8,128)(2,1)S(1)}, bf16[4,4,32,128]{3,2,1,0:T(8,128)(2,1)S(1)}, u32[]{:S(2)}, u32[]{:S(2)}) collective-permute-start(bf16[4,4,32,128]{3,2,1,0:T(8,128)(2,1)S(1)} %pad_maximum_fusion.1.refs_0_), channel_id=1, source_target_pairs={{0,8},{4,12},{8,0},{12,4},{1,9},{5,13},{9,1},{13,5},{2,10},{6,14},... | collective-permute-start | bytes 393224 | tf_op jit(solution)/shard_map/ppermute | solution.py:215
  29.3 11.1 %collective-permute-start.13 = (bf16[4,2,4,32,128]{4,3,2,1,0:T(8,128)(2,1)S(1)}, bf16[4,2,4,32,128]{4,3,2,1,0:T(8,128)(2,1)S(1)}, u32[]{:S(2)}, u32[]{:S(2)}) collective-permute-start(bf16[4,2,4,32,128]{4,3,2,1,0:T(8,128)(2,1)S(1)} %pad_maximum_fusion.refs_4_), channel_id=1, source_target_pairs={{0,16},{16,0},{1,17},{17,1},{2,18},{18,2},{3,19},{19,3},{4,20},{20... | collective-permute-start | bytes 786440 | tf_op jit(solution)/shard_map/ppermute | solution.py:222
  32.6 7.8 %collective-permute-start.16 = (bf16[4,2,4,32,128]{4,3,2,1,0:T(8,128)(2,1)S(1)}, bf16[4,2,4,32,128]{4,3,2,1,0:T(8,128)(2,1)S(1)}, u32[]{:S(2)}, u32[]{:S(2)}) collective-permute-start(bf16[4,2,4,32,128]{4,3,2,1,0:T(8,128)(2,1)S(1)} %collective-permute-done.12.refs_7_), channel_id=1, source_target_pairs={{0,16},{16,0},{1,17},{17,1},{2,18},{18,2},{3,19},{19,3},{4,20},{20... | collective-permute-start | bytes 786440 | tf_op jit(solution)/shard_map/ppermute | solution.py:222
  32.7 7.8 %collective-permute-start.15 = (bf16[4,2,4,32,128]{4,3,2,1,0:T(8,128)(2,1)S(1)}, bf16[4,2,4,32,128]{4,3,2,1,0:T(8,128)(2,1)S(1)}, u32[]{:S(2)}, u32[]{:S(2)}) collective-permute-start(bf16[4,2,4,32,128]{4,3,2,1,0:T(8,128)(2,1)S(1)} %collective-permute-done.11.refs_6_), channel_id=1, source_target_pairs={{0,16},{16,0},{1,17},{17,1},{2,18},{18,2},{3,19},{19,3},{4,20},{20... | collective-permute-start | bytes 786440 | tf_op jit(solution)/shard_map/ppermute | solution.py:222
  33.2 7.3 %collective-permute-start.14 = (bf16[4,2,4,32,128]{4,3,2,1,0:T(8,128)(2,1)S(1)}, bf16[4,2,4,32,128]{4,3,2,1,0:T(8,128)(2,1)S(1)}, u32[]{:S(2)}, u32[]{:S(2)}) collective-permute-start(bf16[4,2,4,32,128]{4,3,2,1,0:T(8,128)(2,1)S(1)} %collective-permute-done.10.refs_5_), channel_id=1, source_target_pairs={{0,16},{16,0},{1,17},{17,1},{2,18},{18,2},{3,19},{19,3},{4,20},{20... | collective-permute-start | bytes 786440 | tf_op jit(solution)/shard_map/ppermute | solution.py:222
  36.5 4.0 %collective-permute-start.3 = (bf16[4,4,32,128]{3,2,1,0:T(8,128)(2,1)S(1)}, bf16[4,4,32,128]{3,2,1,0:T(8,128)(2,1)S(1)}, u32[]{:S(2)}, u32[]{:S(2)}) collective-permute-start(bf16[4,4,32,128]{3,2,1,0:T(8,128)(2,1)S(1)} %pad_maximum_fusion.1.refs_0_), channel_id=1, source_target_pairs={{0,4},{4,0},{8,12},{12,8},{1,5},{5,1},{9,13},{13,9},{2,6},{6,2},{1... | collective-permute-start | bytes 393224 | tf_op jit(solution)/shard_map/ppermute | solution.py:215
